TPU v7x, 32 devices: a whole 2x2x4 slice. The times are simulated.
32 devices in a mesh: freq: 4 (over z), plane: 8 (over y, x, core).
Axes of the slice: x: 2, y: 2, z: 4, core: 2. Of those that a mesh axis runs over, the one named last changes fastest.
Arguments:
- wavefield: float32 [4, 2, 2048, 2048], P('freq', None, 'plane'), may hold values from -6 to 6
- inv_table: float32 [4, 8, 2, 128, 128], P('freq'), may hold values from -1 to 1, as said below
- couple_table: float32 [4, 2, 128, 128], P('freq'), may hold values from -1 to 1
- rhs_table: float32 [4, 8, 2], P('freq'), may hold values from -0.25 to 0.25
- recv_index: int32 [2, 16], replicated, may hold values from 0 to 7
- shot_index: int32 [2, 16], replicated, may hold values from 0 to 7
Outputs:
- migrated: float32 [4, 2, 2048, 2048], P('freq', None, 'plane')
- image: float32 [2, 2048], P(None, 'plane')
Inputs may be any that keep to these rules, and one draw needn't show every extreme that they name: `inv_table`: real and imaginary parts of the group inverses.
All inputs are finite; a program needn't handle non-finite values.
Results may differ from a plain program's by a relative error of at most 0.0003.
Values sent between devices are 32-bit elements; how exact they have to be, the bound alone decides.
No kernel may reach another device: no remote copies, remote signals or barrier semaphores. Data moves between devices by JAX's collectives and lax.ppermute only.
A program may use at most 64 MiB of HBM per device.

v0:
```python
import functools

import jax
import jax.numpy as jnp
from jax import lax
from jax.experimental import pallas as pl
from jax.experimental.pallas import tpu as pltpu
from jax.sharding import PartitionSpec as P

NX = 2048
GROUP = 128
DEPTHS = 2


highest = lax.Precision.HIGHEST


def complex_product(form, mat_re, mat_im, vec_re, vec_im):
    real_part = jnp.einsum(form, mat_re, vec_re, precision=highest) - jnp.einsum(
        form, mat_im, vec_im, precision=highest
    )
    imag_part = jnp.einsum(form, mat_re, vec_im, precision=highest) + jnp.einsum(
        form, mat_im, vec_re, precision=highest
    )
    return (real_part, imag_part)


def select_rows(index, table):
    levels = jnp.arange(table.shape[1], dtype=jnp.int32)
    one_hot = (index[:, None] == levels[None, :]).astype(jnp.float32)
    return jnp.einsum("kv,fv...->fk...", one_hot, table, precision=highest)


def coupling_powers(couple_table, group_count):
    power_re = couple_table[:, 0]
    power_im = couple_table[:, 1]
    powers = []
    reach = 1
    while reach < group_count:
        powers.append((power_re, power_im))
        power_re, power_im = complex_product("fab,fbc->fac", power_re, power_im, power_re, power_im)
        reach = reach * 2
    return powers


def shifted_up(values, reach, group_axis):
    count = values.shape[group_axis]
    kept = lax.slice_in_dim(values, reach, count, axis=group_axis)
    zero_shape = list(values.shape)
    zero_shape[group_axis] = reach
    return jnp.concatenate([kept, jnp.zeros(zero_shape, values.dtype)], axis=group_axis)


def line_pass(wave_field, index, inv_table, rhs_table, powers, along_last):
    line_axis = 3 if along_last else 2
    freqs = wave_field.shape[0]
    length = wave_field.shape[line_axis]
    group_count = length // GROUP
    inv_sel = select_rows(index, inv_table)
    rhs_sel = select_rows(index, rhs_table)
    pad_widths = [(0, 0), (0, 0), (0, 0), (0, 0)]
    pad_widths[line_axis] = (1, 1)
    padded = jnp.pad(wave_field, pad_widths)
    beside = lax.slice_in_dim(padded, 0, length, axis=line_axis) + lax.slice_in_dim(
        padded, 2, length + 2, axis=line_axis
    )
    second = beside - 2.0 * wave_field
    if along_last:
        shape = (freqs, wave_field.shape[2], group_count, GROUP)
        coef_re = rhs_sel[:, None, :, 0, None]
        coef_im = rhs_sel[:, None, :, 1, None]
        local_form = "fkab,flkb->flka"
        power_form = "fab,flkb->flka"
        group_axis = 2
    else:
        shape = (freqs, group_count, GROUP, wave_field.shape[3])
        coef_re = rhs_sel[:, :, 0, None, None]
        coef_im = rhs_sel[:, :, 1, None, None]
        local_form = "fkab,fkbm->fkam"
        power_form = "fab,fkbm->fkam"
        group_axis = 1
    base_re = wave_field[:, 0].reshape(shape)
    base_im = wave_field[:, 1].reshape(shape)
    second_re = second[:, 0].reshape(shape)
    second_im = second[:, 1].reshape(shape)
    source_re = base_re + coef_re * second_re - coef_im * second_im
    source_im = base_im + coef_re * second_im + coef_im * second_re
    solved_re, solved_im = complex_product(
        local_form, inv_sel[:, :, 0], inv_sel[:, :, 1], source_re, source_im
    )
    reach = 1
    for power_re, power_im in powers:
        add_re, add_im = complex_product(
            power_form,
            power_re,
            power_im,
            shifted_up(solved_re, reach, group_axis),
            shifted_up(solved_im, reach, group_axis),
        )
        solved_re = solved_re + add_re
        solved_im = solved_im + add_im
        reach = reach * 2
    out_shape = (freqs,) + wave_field.shape[2:]
    return jnp.stack([solved_re.reshape(out_shape), solved_im.reshape(out_shape)], axis=1)


def to_columns(wave_field):
    return lax.all_to_all(wave_field, "plane", split_axis=3, concat_axis=2, tiled=True)


def to_rows(wave_field):
    return lax.all_to_all(wave_field, "plane", split_axis=2, concat_axis=3, tiled=True)


def diagonal_rows(wave_field, first_row):
    count = wave_field.shape[2]
    block = lax.dynamic_slice_in_dim(wave_field[:, 0], first_row, count, axis=2)
    return jnp.sum(jnp.diagonal(block, axis1=1, axis2=2), axis=0)


def diagonal_columns(wave_field, first_row):
    count = wave_field.shape[3]
    block = lax.dynamic_slice_in_dim(wave_field[:, 0], first_row, count, axis=1)
    return jnp.sum(jnp.diagonal(block, axis1=1, axis2=2), axis=0)


def image_part(partial_value):
    return lax.psum(partial_value, "freq")


def shards(wavefield, inv_table, couple_table, rhs_table, recv_index, shot_index):
    powers = coupling_powers(couple_table, NX // GROUP)
    row_count = wavefield.shape[2]
    first_row = lax.axis_index("plane") * row_count
    wave_field = wavefield
    parts = []
    for step_index in range(DEPTHS):
        if step_index % 2 == 0:
            wave_field = line_pass(
                wave_field, recv_index[step_index], inv_table, rhs_table, powers, True
            )
            wave_field = to_columns(wave_field)
            wave_field = line_pass(
                wave_field, shot_index[step_index], inv_table, rhs_table, powers, False
            )
            parts.append(image_part(diagonal_columns(wave_field, first_row)))
        else:
            wave_field = line_pass(
                wave_field, shot_index[step_index], inv_table, rhs_table, powers, False
            )
            wave_field = to_rows(wave_field)
            wave_field = line_pass(
                wave_field, recv_index[step_index], inv_table, rhs_table, powers, True
            )
            parts.append(image_part(diagonal_rows(wave_field, first_row)))
    stacked = jnp.stack(parts)
    return (wave_field, stacked)


f32 = jnp.float32
bf16 = jnp.bfloat16


def halves(value):
    high = value.astype(bf16)
    low = (value - high.astype(f32)).astype(bf16)
    return high, low


def mul(left, right):
    return jnp.dot(left, right, preferred_element_type=f32)


def product(left, right):
    (left_high, left_low), (right_high, right_low) = left, right
    return mul(left_high, right_high) + mul(left_low, right_high) + mul(left_high, right_low)


def params(mebibytes):
    return pltpu.CompilerParams(vmem_limit_bytes=mebibytes * 1024 * 1024)


def whole(shape, dtype=f32):
    return jax.ShapeDtypeStruct(shape, dtype)


def smem():
    return pl.BlockSpec(memory_space=pltpu.SMEM)


def vmem():
    return pl.BlockSpec(memory_space=pltpu.VMEM)


def anywhere():
    return pl.BlockSpec(memory_space=pl.ANY)


def cost(macs, size):
    return pl.CostEstimate(flops=2 * macs, bytes_accessed=size, transcendentals=0)


def folded(level, inv_ref, rhs_ref):
    mat_re, mat_im = inv_ref[level, 0], inv_ref[level, 1]
    coef_re, coef_im = rhs_ref[0, level, 0], rhs_ref[0, level, 1]
    group = mat_re.shape[-1]
    lane = lax.broadcasted_iota(jnp.int32, mat_re.shape, 1)

    def differences(mat):
        low_side = jnp.where(lane == 0, 0.0, pltpu.roll(mat, 1, 1))
        high_side = jnp.where(lane == group - 1, 0.0, pltpu.roll(mat, group - 1, 1))
        return low_side + high_side - 2.0 * mat

    diff_re, diff_im = differences(mat_re), differences(mat_im)
    inner_re = mat_re + coef_re * diff_re - coef_im * diff_im
    inner_im = mat_im + coef_re * diff_im + coef_im * diff_re
    scaled_re = coef_re * mat_re - coef_im * mat_im
    scaled_im = coef_re * mat_im + coef_im * mat_re
    return inner_re, inner_im, scaled_re, scaled_im


def store_left(high_ref, low_ref, index, mat_re, mat_im):
    group = mat_re.shape[-1]
    blocks = ((mat_re, -mat_im), (mat_im, mat_re))
    for i in range(2):
        for j in range(2):
            where = (index, slice(i * group, (i + 1) * group), slice(j * group, (j + 1) * group))
            high_ref[where], low_ref[where] = halves(blocks[i][j])


def left_table_kernel(rhs_ref, inv_ref, couple_ref, high_ref, low_ref, edge_ref):
    levels, _, group, _ = inv_ref.shape
    for level in range(levels):
        inner_re, inner_im, scaled_re, scaled_im = folded(level, inv_ref, rhs_ref)
        store_left(high_ref, low_ref, level, inner_re, inner_im)
        for part, scaled in enumerate((scaled_re, scaled_im)):
            rows = slice(part * group, (part + 1) * group)
            edge_ref[level, 0, rows, :] = jnp.broadcast_to(scaled[:, 0:1], (group, group))
            edge_ref[level, 1, rows, :] = jnp.broadcast_to(scaled[:, group - 1 : group], (group, group))
    store_left(high_ref, low_ref, levels, couple_ref[0], couple_ref[1])


def right_table_kernel(rhs_ref, inv_ref, couple_ref, high_ref, low_ref, edge_ref):
    levels, _, group, _ = inv_ref.shape
    for level in range(levels + 1):
        if level < levels:
            inner_re, inner_im, scaled_re, scaled_im = folded(level, inv_ref, rhs_ref)
            scaled_re, scaled_im = scaled_re.T, scaled_im.T
            for side, row in enumerate((0, group - 1)):
                edge_re, edge_im = scaled_re[row : row + 1], scaled_im[row : row + 1]
                edge_ref[level, 2 * side : 2 * side + 1, :] = jnp.concatenate([edge_re, edge_im], axis=1)
                edge_ref[level, 2 * side + 1 : 2 * side + 2, :] = jnp.concatenate([-edge_im, edge_re], axis=1)
        else:
            inner_re, inner_im = couple_ref[0], couple_ref[1]
        turned_re, turned_im = inner_re.T, inner_im.T
        store_left(high_ref, low_ref, level, turned_re, -turned_im)


def make_tables(kernel, rhs, inv_table, couple_table, edge_shape):
    levels, _, group, _ = inv_table.shape
    shape = whole((levels + 1, 2 * group, 2 * group), bf16)
    return pl.pallas_call(
        kernel,
        out_shape=[shape, shape, whole(edge_shape)],
        in_specs=[smem(), vmem(), vmem()],
        out_specs=[vmem()] * 3,
        compiler_params=params(16),
        cost_estimate=cost(10**10, 4 * 1024 * 1024),
    )(rhs, inv_table, couple_table)


def edge_row_kernel(place_ref, field_ref, row_ref, held, sem):
    rows = field_ref.shape[2]
    odd = place_ref[0] % 2
    start = pl.multiple_of(odd * (rows - 8), 8)
    copy = pltpu.make_async_copy(field_ref.at[0, :, pl.ds(start, 8), :], held, sem)
    copy.start()
    copy.wait()
    for part in range(2):
        row_ref[0, part] = jnp.where(odd == 1, held[part, 7:8, :], held[part, 0:1, :])


def edge_row(place, field):
    length = field.shape[3]
    return pl.pallas_call(
        edge_row_kernel,
        out_shape=whole((1, 2, 1, length)),
        in_specs=[smem(), anywhere()],
        out_specs=vmem(),
        scratch_shapes=[pltpu.VMEM((2, 8, length), f32), pltpu.SemaphoreType.DMA],
        compiler_params=params(60),
        cost_estimate=cost(10**10, 1024 * 1024),
    )(place, field)


def line_groups(read, level_of, tables, low, high, following, below, above, write):
    high_ref, low_ref, edge_ref = tables
    last = high_ref.shape[0] - 1
    couple = (high_ref[last], low_ref[last])
    for k in reversed(range(low, high)):
        level = level_of(k)
        value_re, value_im = read(k)
        group = value_re.shape[1]
        solved = product(halves(jnp.concatenate([value_re, value_im], axis=1)), (high_ref[level], low_ref[level]))
        if following is not None:
            solved = solved + product(following, couple)
        before = [item[:, group - 1 : group] for item in read(k - 1)] if k > low else below
        for side, column in ((0, before), (1, above)):
            if column is not None:
                for part in range(2):
                    row = edge_ref[level, 2 * side + part : 2 * side + part + 1, :]
                    solved = solved + column[part] * row
        write(k, solved)
        following = halves(solved)
        above = [value_re[:, 0:1], value_im[:, 0:1]]


def rows_with_halo(field_ref, halo_ref, part, columns, halo_columns):
    row = jnp.broadcast_to(halo_ref[0, part, :, halo_columns], (8, columns.stop - columns.start))
    return jnp.concatenate([field_ref[0, part, :, columns], row], axis=0)


def first_pass_kernel(place_ref, index_ref, field_ref, beside_ref, halo_ref, high_ref, low_ref, edge_ref, *refs,
                      half, group, block):
    if half:
        carry_ref, keep_ref, send_ref, own = None, refs[1], refs[2], refs[3]
        state_ref = refs[0]
    else:
        carry_ref, _, keep_ref, send_ref, own = refs
        state_ref = None
    width = field_ref.shape[-1]
    count = width // group
    low = half * count
    core = place_ref[0] % 2

    def read(k):
        columns = slice((k - low) * group, (k - low + 1) * group)
        wide = slice(k * group, (k + 1) * group)
        return [rows_with_halo(field_ref, halo_ref, part, columns, wide) for part in range(2)]

    inside = slice(0, group)
    wide = slice((low - 1) * group, low * group) if half else slice(count * group, (count + 1) * group)
    beyond = [rows_with_halo(beside_ref, halo_ref, part, inside, wide) for part in range(2)]
    if half:
        below, above, following = [item[:, group - 1 : group] for item in beyond], None, None
    else:
        below, above, following = None, [item[:, 0:1] for item in beyond], halves(carry_ref[...])

    def write(k, solved):
        start = (k - low) * group
        b, inner = start // block, start % block
        own[b % 2, b // 2, 0, :, inner : inner + group] = solved[:, :group]
        own[b % 2, b // 2, 1, :, inner : inner + group] = solved[:, group:]
        if half and k == low:
            state_ref[...] = solved

    line_groups(
        read, lambda k: index_ref[0, k], (high_ref, low_ref, edge_ref), low, low + count, following, below, above, write
    )
    keep_ref[...] = own[core]
    send_ref[...] = own[1 - core]


def first_pass(place, recv_index, field, halo, tables, half, carry, after, block, group):
    rows, length = field.shape[2:]
    width = length // 2
    lines = rows + 8
    count = width // group
    shape = (width // (2 * block), 2, lines, block)
    beside = count - 1 if half else count
    args = [place, recv_index, field, field, halo, *tables]
    specs = [
        smem(), smem(),
        pl.BlockSpec((1, 2, rows, width), lambda i: (0, 0, 0, half)),
        pl.BlockSpec((1, 2, rows, group), lambda i: (0, 0, 0, beside)),
    ] + [vmem()] * 4
    outs = [whole(shape)] * 2
    if half:
        outs = [whole((lines, 2 * group))] + outs
    else:
        args += [carry, after]
        specs += [vmem(), anywhere()]
    return pl.pallas_call(
        functools.partial(first_pass_kernel, half=half, group=group, block=block),
        grid=(1,),
        out_shape=outs,
        in_specs=specs,
        out_specs=[vmem()] * len(outs),
        scratch_shapes=[pltpu.VMEM((2,) + shape, f32)],
        compiler_params=params(36),
        cost_estimate=cost(lines * width * group * 24, 8 * lines * width * 2),
    )(*args)


def add_edge(solved, edge_ref, level, side, row_re, row_im):
    group = edge_ref.shape[-1]
    wide = row_re.shape[-1]
    column = [edge_ref[level, side, part * group : (part + 1) * group, :] for part in range(2)]
    if wide > group:
        column = [jnp.concatenate([item] * (wide // group), axis=1) for item in column]
    term_re = column[0] * row_re - column[1] * row_im
    term_im = column[0] * row_im + column[1] * row_re
    both = jnp.concatenate([term_re, term_im], axis=0)
    return both if solved is None else solved + both


def second_groups(chip, groups, index_ref, tables):
    high_ref, low_ref, edge_ref = tables
    last = high_ref.shape[0] - 1
    couple = (high_ref[last], low_ref[last])
    base = chip * groups
    total = index_ref.shape[1]

    def open_state(row_re, row_im):
        after = base + groups
        level = index_ref[1, jnp.minimum(after, total - 1)]
        inside = jnp.where(after < total, 1.0, 0.0)
        return add_edge(None, edge_ref, level, 0, row_re * inside, row_im * inside)

    def step(k, value, following, before, after):
        level = index_ref[1, base + k]
        solved = product((high_ref[level], low_ref[level]), value)
        solved = solved + product(couple, following)
        if before is not None:
            solved = add_edge(solved, edge_ref, level, 0, *before)
        if after is not None:
            solved = add_edge(solved, edge_ref, level, 1, *after)
        return solved

    return open_state, step


def first_row(value, group):
    return value[0:1], value[group : group + 1]


def last_row(value, group):
    return value[group - 1 : group], value[2 * group - 1 : 2 * group]


def open_sweep_kernel(place_ref, index_ref, high_ref, low_ref, edge_ref, keep_ref, come_ref, _, near_ref, far_ref, local_ref,
                      base_ref, pair, *, groups, group):
    device = place_ref[0]
    chip, core = device // 2, device % 2
    tables = (high_ref, low_ref, edge_ref)
    last = high_ref.shape[0] - 1
    couple = (high_ref[last], low_ref[last])
    half = groups // 2
    lines = half * group
    width = keep_ref.shape[-1]

    def rows(upper, start, count):
        mine = upper == core
        return [
            jnp.where(mine, keep_ref[0, part, start : start + count, :], come_ref[0, part, start : start + count, :])
            for part in range(2)
        ]

    def store_pair(where, value):
        for sub in range(2):
            pair[sub, where, :] = value[:, sub * (width // 2) : (sub + 1) * (width // 2)]

    def given(k):
        return rows(k // half, (k % half) * group, group)

    open_state, step = second_groups(chip, groups, index_ref, tables)
    above = [item[0:1] for item in rows(1, lines, 8)]
    solved = following = state = None
    value = given(groups - 1)
    earlier = None
    for k in reversed(range(groups)):
        level = index_ref[0, chip * groups + k]
        below_value = given(k - 1) if k else None
        before = [item[group - 1 : group] for item in below_value] if k else [item[0:1] for item in rows(0, lines, 8)]
        now = product((high_ref[level], low_ref[level]), halves(jnp.concatenate(value, axis=0)))
        if following is not None:
            now = now + product(couple, following)
        now = add_edge(now, edge_ref, level, 0, *before)
        now = add_edge(now, edge_ref, level, 1, *above)
        above = [item[0:1] for item in value]
        value = below_value
        base_ref[k // half, k % half] = now[:group, (k % half) * group : (k % half + 1) * group]
        if k == groups - 1:
            row_re, row_im = last_row(now, group)
            for part, row in enumerate((row_re, row_im)):
                store_pair(slice(4 * group + 8 * part, 4 * group + 8 * part + 8), jnp.broadcast_to(row, (8, width)))
            state = halves(open_state(row_re, row_im))
        else:
            done = step(k + 1, following, state, last_row(now, group), first_row(earlier, group) if earlier is not None else None)
            local_ref[k + 1] = done
            state = halves(done)
        earlier = solved
        solved = now
        following = halves(now)
    done = step(0, following, state, None, first_row(earlier, group))
    local_ref[0] = done
    store_pair(slice(0, 2 * group), solved)
    store_pair(slice(2 * group, 4 * group), done)
    near_ref[...] = pair[chip % 2]
    far_ref[...] = pair[1 - chip % 2]


def power_kernel(index_ref, high_ref, low_ref, edge_ref, _, power_high, power_low, chip_high, chip_low, *, groups, group):
    last = high_ref.shape[0] - 1
    couple = (high_ref[last], low_ref[last])
    rows = lax.broadcasted_iota(jnp.int32, (2 * group, group), 0)
    columns = lax.broadcasted_iota(jnp.int32, (2 * group, group), 1)
    values = [None] * groups + [(rows == columns).astype(f32)]
    split = [None] * groups
    for k in reversed(range(groups)):
        values[k] = product(couple, halves(values[k + 1]))
        split[k] = halves(values[k])
        store_left(power_high, power_low, k, values[k][:group], values[k][group:])
    for q in range(chip_high.shape[0]):

        def store(k, done, q=q):
            if k == 0:
                store_left(chip_high, chip_low, q, done[:group], done[group:])

        linear_part(q + 1, groups, group, index_ref, (high_ref, low_ref, edge_ref), values, split, store)


def own_map_kernel(place_ref, index_ref, high_ref, low_ref, edge_ref, power_high, power_low, _, map_high, map_low,
                   *, groups, group):
    rows = lax.broadcasted_iota(jnp.int32, (2 * group, group), 0)
    columns = lax.broadcasted_iota(jnp.int32, (2 * group, group), 1)
    split = [(power_high[k, :, 0:group], power_low[k, :, 0:group]) for k in range(groups)]
    values = [high.astype(f32) + low.astype(f32) for high, low in split]
    values.append((rows == columns).astype(f32))

    def store(k, done):
        store_left(map_high, map_low, k, done[:group], done[group:])

    linear_part(place_ref[0] // 2, groups, group, index_ref, (high_ref, low_ref, edge_ref), values, split, store)


def linear_part(chip, groups, group, index_ref, tables, values, split, store):
    open_state, step = second_groups(chip, groups, index_ref, tables)
    state = halves(open_state(*last_row(values[groups - 1], group)))
    for k in reversed(range(groups)):
        before = last_row(values[k - 1], group) if k else None
        done = step(k, split[k], state, before, first_row(values[k + 1], group))
        state = halves(done)
        store(k, done)


def scan_kernel(place_ref, high_ref, low_ref, power_high, power_low, chip_high, chip_low, *refs, chips, group):
    pieces, outs, (held, rows) = refs[:chips], refs[-chips - 2 : -2], refs[-2:]
    chip = place_ref[0] // 2
    last = high_ref.shape[0] - 1
    size = 4 * group
    for offset in range(chips):
        held[chip ^ offset] = pieces[offset][...]
    keep = (power_high[0], power_low[0])
    rows[0] = jnp.zeros_like(rows[0])
    for q in range(chips - 1, 0, -1):
        first = halves(held[q, 0 : 2 * group, :])
        for part in range(2):
            tail = slice((part + 1) * group - 16, (part + 1) * group)
            row = product((high_ref[last, tail, :], low_ref[last, tail, :]), first)[15:16]
            base = size + 8 * part
            rows[q, 8 * part : 8 * part + 8, :] = held[q - 1, base : base + 8, :] + row
        if q > 1:
            second = halves(held[q, 2 * group : size, :])
            held[q - 1, 0 : 2 * group, :] = held[q - 1, 0 : 2 * group, :] + product(keep, first)
            held[q - 1, 2 * group : size, :] = (
                held[q - 1, 2 * group : size, :]
                + product((chip_high[q - 2], chip_low[q - 2]), first)
                + product(keep, second)
            )
    held[0] = jnp.zeros_like(held[0])
    for offset in range(chips):
        target = chip ^ offset
        outs[offset][0:size, :] = held[(target + 1) % chips, 0:size, :]
        outs[offset][size : size + 16, :] = rows[target]


def close_sweep_kernel(place_ref, index_ref, edge_ref, power_high, power_low, map_high, map_low, local_ref, base_ref,
                       near_ref, far_ref, _, own_ref, other_ref, image_ref, pair, result, *, groups, group, part_of, second_pair):
    device = place_ref[0]
    chip, core = device // 2, device % 2
    pair[chip % 2] = near_ref[...]
    pair[1 - chip % 2] = far_ref[...]

    def carried(start, count):
        return jnp.concatenate([pair[0, start : start + count, :], pair[1, start : start + count, :]], axis=1)

    first = halves(carried(0, 2 * group))
    second = halves(carried(2 * group, 2 * group))
    half = groups // 2
    for k in reversed(range(groups)):
        done = local_ref[k] + (
            product((map_high[k], map_low[k]), first) + product((power_high[k], power_low[k]), second)
        )
        if k == 0:
            level = index_ref[1, chip * groups]
            base = 4 * group
            done = add_edge(done, edge_ref, level, 0, carried(base, 8)[0:1], carried(base + 8, 8)[0:1])
        rows = slice((k % half) * group, (k % half + 1) * group)
        result[k // half, 0, rows, :] = done[:group]
        result[k // half, 1, rows, :] = done[group:]
    own_ref[...] = result[core]
    other_ref[...] = result[1 - core]
    image_ref[...] = jnp.zeros_like(image_ref)

    @pl.when((chip // 2 == part_of) & ((chip % 2) ^ (chip // 2) == second_pair))
    def _():
        for i in range(half):
            k = core * half + i
            columns = slice(i * group, (i + 1) * group)
            square = base_ref[core, i] + product(
                (power_high[k, 0:group, :], power_low[k, 0:group, :]), [item[:, columns] for item in first]
            )
            image_ref[:, columns] = diagonal_of(square)


def diagonal_of(square):
    rows = lax.broadcasted_iota(jnp.int32, square.shape, 0)
    columns = lax.broadcasted_iota(jnp.int32, square.shape, 1)
    return jnp.sum(jnp.where(rows == columns, square, 0.0), axis=0, keepdims=True)


def last_pass_kernel(place_ref, index_ref, high_ref, low_ref, edge_ref, *refs, half, step, group):
    owns, comes = refs[0:2], refs[2:4]
    if half:
        out_ref, state_ref, column_ref, image_ref, field, result, sems = refs[4:]
    else:
        carry_ref, beside_ref, _, *images = refs[4:-5]
        out_ref, image_ref, field, result, sems = refs[-5:]
    device = place_ref[0]
    chip, core = device // 2, device % 2
    block = owns[0].shape[-1]
    width = field.shape[-1]
    count = width // group
    low = half * count
    for second_pair in range(2):
        for ref, side in ((owns[second_pair], core), (comes[second_pair], 1 - core)):
            start = pl.multiple_of(((chip // 2 ^ second_pair) * 2 + side) * block, block)
            for part in range(2):
                field[part, :, pl.ds(start, block)] = ref[part]
    first = count + 1 if half else 0
    copies = []

    def read(k):
        return [field[part, :, (k - low) * group : (k - low + 1) * group] for part in range(2)]

    def write(k, solved):
        if half and k == low:
            state_ref[...] = solved
            return
        where = k - first
        result[where, 0] = solved[:, :group]
        result[where, 1] = solved[:, group:]
        copy = pltpu.make_async_copy(
            result.at[where], out_ref.at[0, :, :, k * group : (k + 1) * group], sems.at[where]
        )
        copy.start()
        copies.append(copy)

    tables = (high_ref, low_ref, edge_ref)
    following, above = None, None
    if half:
        for part, value in enumerate(read(low)):
            column_ref[part] = jnp.broadcast_to(value[:, 0:1], column_ref.shape[1:])
    else:
        level = index_ref[step, count]
        solved = carry_ref[...]
        for part, value in enumerate(read(count - 1)):
            solved = solved + value[:, group - 1 : group] * edge_ref[level, part : part + 1, :]
        write(count, solved)
        following = halves(solved)
        above = [beside_ref[part, :, 0:1] for part in range(2)]
    line_groups(read, lambda k: index_ref[step, k], tables, low, low + count, following, None, above, write)
    if half:
        image_ref[...] = jnp.zeros_like(image_ref)
    else:
        image_ref[1:2] = images[0][...]
        image_ref[0:1] = sum((item[...] for item in images[2:]), images[1][...])
    row = image_ref.shape[0] - 1
    for i in range(block // group):
        mine = device * (block // group) + i
        here = mine > count if half else mine <= count

        @pl.when(here)
        def _():
            square = result[jnp.where(here, mine - first, 0), 0, i * group : (i + 1) * group, :]
            image_ref[row : row + 1, i * group : (i + 1) * group] = diagonal_of(square)

    for copy in copies:
        copy.wait()


def last_pass(place, recv_index, tables, owns, comes, half, passed, shape, step, group):
    rows, length = shape[2:]
    width = length // 2
    count = width // group
    block = owns[0].shape[-1]
    args = [place, recv_index, *tables, *owns, *comes]
    any_space = pl.BlockSpec(memory_space=pl.ANY)
    specs = [smem()] * 2 + [vmem()] * 7
    outs = [whole(shape)]
    out_specs = [any_space]
    aliases = {}
    results = count - 1 if half else count + 1
    if half:
        outs += [whole((rows, 2 * group)), whole((2, rows, group))]
        out_specs += [vmem()] * 2
    else:
        migrated, state, column, *images = passed
        args += [state, column, migrated, *images]
        specs += [vmem(), vmem(), any_space] + [vmem()] * len(images)
        aliases = {len(args) - 1 - len(images): 0}
    return pl.pallas_call(
        functools.partial(last_pass_kernel, half=half, step=step, group=group),
        out_shape=outs + [whole((1 if half else 2, block))],
        in_specs=specs,
        out_specs=out_specs + [vmem()],
        scratch_shapes=[
            pltpu.VMEM((2, rows, width), f32),
            pltpu.VMEM((results, 2, rows, group), f32),
            pltpu.SemaphoreType.DMA((results,)),
        ],
        input_output_aliases=aliases,
        compiler_params=params(24),
        cost_estimate=cost(rows * width * group * 24, 8 * rows * width * 2),
    )(*args)


def sum_over(value, axis, count):
    reach = 1
    while reach < count:
        value = value + lax.ppermute(value, axis, [(i, i ^ reach) for i in range(count)])
        reach *= 2
    return value


def fast_shards(wavefield, inv_table, couple_table, rhs_table, recv_index, shot_index, *, devices, freqs):
    levels, _, group, _ = inv_table.shape[1:]
    rows, _ = wavefield.shape[2:]
    block = rows
    chips = devices // 2
    groups = 2 * rows // group
    device = lax.axis_index("plane")
    place = device.reshape(1).astype(jnp.int32)
    double = 2 * group
    partner = [(d, d ^ 1) for d in range(devices)]

    edge = edge_row(place, wavefield)
    swap = [(d, d + 1) for d in range(1, devices - 1, 2)] + [(d + 1, d) for d in range(1, devices - 1, 2)]
    halo = lax.ppermute(edge, "plane", swap)
    right = make_tables(right_table_kernel, rhs_table, inv_table[0], couple_table[0], (levels, 4, double))

    left = make_tables(left_table_kernel, rhs_table, inv_table[0], couple_table[0], (levels, 2, double, group))

    wide = block // 2
    piece = whole((4 * group + 16, wide))
    local = whole((groups, double, block))
    base = whole((2, groups // 2, group, group))
    matrices = whole((groups, double, double), bf16)
    middle = whole((chips - 2, double, double), bf16)
    powers = []

    def make_powers(ready):
        powers.extend(
            pl.pallas_call(
                functools.partial(power_kernel, groups=groups, group=group),
                out_shape=[matrices] * 2 + [middle] * 2,
                in_specs=[smem()] + [vmem()] * 3 + [anywhere()],
                out_specs=[vmem()] * 4,
                compiler_params=params(20),
                cost_estimate=cost(groups * group * group * group * 64, 4 * 1024 * 1024),
            )(shot_index, *left, ready)
        )
        return powers[0]

    keep, come = {}, {}
    locals_, bases, theirs = {}, {}, {}
    carry = after = None
    for half in (1, 0):
        result = first_pass(place, recv_index, wavefield, halo, right, half, carry, after, block, group)
        carry, keep[half], send = result if half else (None, *result)
        after = carry if half else make_powers(keep[half])
        come[half] = lax.ppermute(send, "plane", partner)
        for second_pair in (1, 0):
            spec = pltpu.PrefetchScalarGridSpec(
                num_scalar_prefetch=2,
                grid=(1,),
                in_specs=[vmem()] * 3
                + [pl.BlockSpec((1,) + keep[half].shape[1:], lambda i, at, _, o=second_pair: ((at[0] // 4) ^ o, 0, 0, 0))] * 2
                + [anywhere()],
                out_specs=[vmem()] * 4,
                scratch_shapes=[pltpu.VMEM((2,) + piece.shape, f32)],
            )
            name = "%d_%d" % (half, second_pair)
            near, far, locals_[name], bases[name] = pl.pallas_call(
                functools.partial(open_sweep_kernel, groups=groups, group=group),
                grid_spec=spec,
                out_shape=[piece, piece, local, base],
                compiler_params=params(24),
                cost_estimate=cost(groups * group * block * group * 48, 8 * groups * group * block * 3),
            )(place, shot_index, *left, keep[half], come[half], after)
            after = near
            for offset, item in ((2 * second_pair + 1, far), (2 * second_pair, near)):
                moves = [(d, d ^ (2 * offset)) for d in range(devices)]
                theirs[half, offset] = lax.ppermute(item, "plane", moves) if offset else item

    power_high, power_low, chip_high, chip_low = powers
    came = {}
    for half in (1, 0):
        carries = pl.pallas_call(
            functools.partial(scan_kernel, chips=chips, group=group),
            out_shape=[piece] * chips,
            in_specs=[smem()] + [vmem()] * (6 + chips) + [anywhere()],
            out_specs=[vmem()] * chips,
            scratch_shapes=[pltpu.VMEM((chips,) + piece.shape, f32), pltpu.VMEM((chips, 16, wide), f32)],
            compiler_params=params(20),
            cost_estimate=cost(3 * group * group * wide * 24, 4 * 1024 * 1024),
        )(place, left[0], left[1], power_high, power_low, chip_high, chip_low, *[theirs[half, o] for o in range(chips)], after)
        after = carries[0]
        if half:
            map_high, map_low = pl.pallas_call(
                functools.partial(own_map_kernel, groups=groups, group=group),
                out_shape=[matrices] * 2,
                in_specs=[smem()] * 2 + [vmem()] * 5 + [anywhere()],
                out_specs=[vmem()] * 2,
                compiler_params=params(20),
                cost_estimate=cost(groups * group * group * group * 32, 4 * 1024 * 1024),
            )(place, shot_index, *left, power_high, power_low, after)
            after = map_high
        for offset in (3, 1, 2, 0):
            moves = [(d, d ^ (2 * offset)) for d in range(devices)]
            came[half, offset] = lax.ppermute(carries[offset], "plane", moves) if offset else carries[0]

    images, image_last = [], None
    passed = None
    part = whole((2, rows, block))
    for half in (1, 0):
        owns, comes = [], []
        for second_pair in (0, 1):
            name = "%d_%d" % (half, second_pair)
            own, other, image = pl.pallas_call(
                functools.partial(
                    close_sweep_kernel, groups=groups, group=group, part_of=half, second_pair=second_pair
                ),
                out_shape=[part, part, whole((1, block))],
                in_specs=[smem()] * 2 + [vmem()] * 9 + [anywhere()],
                out_specs=[vmem()] * 3,
                scratch_shapes=[pltpu.VMEM((2,) + piece.shape, f32), pltpu.VMEM((2, 2, rows, block), f32)],
                compiler_params=params(20),
                cost_estimate=cost(groups * group * block * group * 24, 8 * groups * group * block * 2),
            )(
                place, shot_index, left[2], power_high, power_low, map_high, map_low, locals_[name], bases[name],
                came[half, 2 * second_pair], came[half, 2 * second_pair + 1], after,
            )
            after = image
            owns.append(own)
            comes.append(lax.ppermute(other, "plane", partner))
            images.append(image)
        if not half:
            passed = [*passed, image_last, *images]
        *passed, image_last = last_pass(place, recv_index, right, owns, comes, half, passed, wavefield.shape, 1, group)
        after = image_last
    image_last = sum_over(image_last, "freq", freqs)
    return passed[0], image_last


def solution(mesh):
    placed = (
        P("freq", None, "plane", None),
        P("freq", None, None, None, None),
        P("freq", None, None, None),
        P("freq", None, None),
        P(),
        P(),
    )
    devices = mesh.shape["plane"]
    freqs = mesh.shape["freq"]

    def body(*arrays):
        if devices == 8 and arrays[0].shape[2] == 2 * GROUP and arrays[0].shape[0] == 1 and freqs & (freqs - 1) == 0:
            return fast_shards(*arrays, devices=devices, freqs=freqs)
        return shards(*arrays)

    return jax.shard_map(
        body,
        mesh=mesh,
        in_specs=placed,
        out_specs=(P("freq", None, "plane", None), P(None, "plane")),
        check_vma=False,
    )
```

profile of v0, /device:TPU:0, one launch (start us, length us, event | category | flops | bytes accessed | tf_op | source)
XLA Modules:
  0.0 100.3 jit_solution(4844503829088737953)
XLA Ops:
  0.7 1.6 %shard_map.79 = f32[1,2,1,2048]{3,2,1,0:T(1,128)} custom-call(s32[1]{0:T(128)} %bitcast.place_ref, f32[1,2,256,2048]{3,2,1,0:T(8,128)} %beside_ref.3), custom_call_target="tpu_custom_call" | custom-call | flops 20000000000 | bytes 1048576 | tf_op jit(solution)/shard_map/pallas_call | solution.py:285
  3.1 1.9 %shard_map.77 = (bf16[9,256,256]{2,1,0:T(8,128)(2,1)S(1)}, bf16[9,256,256]{2,1,0:T(8,128)(2,1)S(1)}, f32[8,4,256]{2,1,0:T(4,128)S(1)}) custom-call(f32[1,8,2]{2,1,0:T(8,128)S(1)} %copy.9.rhs_ref, f32[8,2,128,128]{3,2,1,0:T(8,128)S(1)} %bitcast.3, f32[2,128,128]{2,1,0:T(8,128)S(1)} %bitcast.5), custom_call_target="tpu_custom_call" | custom-call | flops 20000000000 | bytes 4194304 | tf_op jit(solution)/shard_map/pallas_call | solution.py:262
  5.3 3.6 %shard_map.80 = (f32[264,256]{1,0:T(8,128)S(1)}, f32[2,2,264,256]{3,2,1,0:T(8,128)S(1)}, f32[2,2,264,256]{3,2,1,0:T(8,128)S(1)}) custom-call(s32[1]{0:T(128)} %bitcast.place_ref, s32[2,16]{1,0:T(2,128)S(1)} %copy-done.2, f32[1,2,256,2048]{3,2,1,0:T(8,128)S(1)} %copy-done, f32[1,2,256,2048]{3,2,1,0:T(8,128)S(1)} %copy-done, ...), custom_call_target="tpu_custom_call" | custom-call | flops 1660944384 | bytes 4325376 | tf_op jit(solution)/shard_map/pallas_call | solution.py:383
  8.9 4.4 %collective-permute-start.1 = (f32[2,2,264,256]{3,2,1,0:T(8,128)S(1)}, f32[2,2,264,256]{3,2,1,0:T(8,128)S(1)}, u32[]{:S(2)}, u32[]{:S(2)}) collective-permute-start(f32[2,2,264,256]{3,2,1,0:T(8,128)S(1)} %get-tuple-element.69), channel_id=1, source_target_pairs={{0,1},{1,0},{2,3},{3,2},{4,5},{5,4},{6,7},{7,6},{8,9},{9,8},{10,11... | collective-permute-start | bytes 3244040 | tf_op jit(solution)/shard_map/ppermute | solution.py:783
  13.3 1.9 %shard_map.78 = (bf16[9,256,256]{2,1,0:T(8,128)(2,1)S(1)}, bf16[9,256,256]{2,1,0:T(8,128)(2,1)S(1)}, f32[8,2,256,128]{3,2,1,0:T(8,128)S(1)}) custom-call(f32[1,8,2]{2,1,0:T(8,128)S(1)} %copy.9.rhs_ref, f32[8,2,128,128]{3,2,1,0:T(8,128)S(1)} %bitcast.4, f32[2,128,128]{2,1,0:T(8,128)S(1)} %bitcast.6), custom_call_target="tpu_custom_call" | custom-call | flops 20000000000 | bytes 4194304 | tf_op jit(solution)/shard_map/pallas_call | solution.py:262
  15.6 3.1 %shard_map.81 = (f32[528,128]{1,0:T(8,128)S(1)}, f32[528,128]{1,0:T(8,128)S(1)}, f32[4,256,256]{2,1,0:T(8,128)S(1)}, f32[2,2,128,128]{3,2,1,0:T(8,128)S(1)}) custom-call(s32[1]{0:T(128)} %bitcast.place_ref, s32[2,16]{1,0:T(2,128)S(1)} %copy-done.1, bf16[9,256,256]{2,1,0:T(8,128)(2,1)S(1)} %get-tuple-element.65.high_ref, ...), custom_call_target="tpu_custom_call" | custom-call | flops 1610612736 | bytes 3145728 | tf_op jit(solution)/shard_map/pallas_call | solution.py:795
  18.7 3.1 %shard_map.82 = (f32[528,128]{1,0:T(8,128)S(1)}, f32[528,128]{1,0:T(8,128)S(1)}, f32[4,256,256]{2,1,0:T(8,128)S(1)}, f32[2,2,128,128]{3,2,1,0:T(8,128)S(1)}) custom-call(s32[1]{0:T(128)} %bitcast.place_ref, s32[2,16]{1,0:T(2,128)S(1)} %copy-done.1, bf16[9,256,256]{2,1,0:T(8,128)(2,1)S(1)} %get-tuple-element.65.high_ref, ...), custom_call_target="tpu_custom_call" | custom-call | flops 1610612736 | bytes 3145728 | tf_op jit(solution)/shard_map/pallas_call | solution.py:795
  21.8 4.0 %shard_map.83 = (f32[2,2,264,256]{3,2,1,0:T(8,128)S(1)}, f32[2,2,264,256]{3,2,1,0:T(8,128)S(1)}) custom-call(s32[1]{0:T(128)} %bitcast.place_ref, s32[2,16]{1,0:T(2,128)S(1)} %copy-done.2, f32[1,2,256,2048]{3,2,1,0:T(8,128)S(1)} %copy-done, f32[1,2,256,2048]{3,2,1,0:T(8,128)S(1)} %copy-done, f32[1,2,1,2048]{3,2,1,0:T(1,128)S(1)} %collective-permute-done.halo_ref, ...), custom_call_target="tpu_custom_call" | custom-call | flops 1660944384 | bytes 4325376 | tf_op jit(solution)/shard_map/pallas_call | solution.py:383
  26.1 2.0 %collective-permute-start.3 = (f32[528,128]{1,0:T(8,128)S(1)}, f32[528,128]{1,0:T(8,128)S(1)}, u32[]{:S(2)}, u32[]{:S(2)}) collective-permute-start(f32[528,128]{1,0:T(8,128)S(1)} %get-tuple-element.70._), channel_id=1, source_target_pairs={{0,4},{1,5},{2,6},{3,7},{4,0},{5,1},{6,2},{7,3},{8,12},{9,13},{10,... | collective-permute-start | bytes 811016 | tf_op jit(solution)/shard_map/ppermute | solution.py:805
  29.7 3.8 %shard_map.84 = (bf16[4,256,256]{2,1,0:T(8,128)(2,1)S(1)}, bf16[4,256,256]{2,1,0:T(8,128)(2,1)S(1)}, bf16[2,256,256]{2,1,0:T(8,128)(2,1)S(1)}, bf16[2,256,256]{2,1,0:T(8,128)(2,1)S(1)}) custom-call(s32[2,16]{1,0:T(2,128)S(1)} %copy-done.1, bf16[9,256,256]{2,1,0:T(8,128)(2,1)S(1)} %get-tuple-element.65.high_ref, ...), custom_call_target="tpu_custom_call" | custom-call | flops 1073741824 | bytes 4194304 | tf_op jit(solution)/shard_map/pallas_call | solution.py:765
  33.5 3.1 %shard_map.85 = (f32[528,128]{1,0:T(8,128)S(1)}, f32[528,128]{1,0:T(8,128)S(1)}, f32[4,256,256]{2,1,0:T(8,128)S(1)}, f32[2,2,128,128]{3,2,1,0:T(8,128)S(1)}) custom-call(s32[1]{0:T(128)} %bitcast.place_ref, s32[2,16]{1,0:T(2,128)S(1)} %copy-done.1, bf16[9,256,256]{2,1,0:T(8,128)(2,1)S(1)} %get-tuple-element.65.high_ref, ...), custom_call_target="tpu_custom_call" | custom-call | flops 1610612736 | bytes 3145728 | tf_op jit(solution)/shard_map/pallas_call | solution.py:795
  36.6 2.2 %collective-permute-start.8 = (f32[528,128]{1,0:T(8,128)S(1)}, f32[528,128]{1,0:T(8,128)S(1)}, u32[]{:S(2)}, u32[]{:S(2)}) collective-permute-start(f32[528,128]{1,0:T(8,128)S(1)} %get-tuple-element.88), channel_id=1, source_target_pairs={{0,6},{1,7},{2,4},{3,5},{4,2},{5,3},{6,0},{7,1},{8,14},{9,15},{10,... | collective-permute-start | bytes 811016 | tf_op jit(solution)/shard_map/ppermute | solution.py:805
  39.9 3.1 %shard_map.86 = (f32[528,128]{1,0:T(8,128)S(1)}, f32[528,128]{1,0:T(8,128)S(1)}, f32[4,256,256]{2,1,0:T(8,128)S(1)}, f32[2,2,128,128]{3,2,1,0:T(8,128)S(1)}) custom-call(s32[1]{0:T(128)} %bitcast.place_ref, s32[2,16]{1,0:T(2,128)S(1)} %copy-done.1, bf16[9,256,256]{2,1,0:T(8,128)(2,1)S(1)} %get-tuple-element.65.high_ref, ...), custom_call_target="tpu_custom_call" | custom-call | flops 1610612736 | bytes 3145728 | tf_op jit(solution)/shard_map/pallas_call | solution.py:795
  44.4 1.9 %collective-permute-start.10 = (f32[528,128]{1,0:T(8,128)S(1)}, f32[528,128]{1,0:T(8,128)S(1)}, u32[]{:S(2)}, u32[]{:S(2)}) collective-permute-start(f32[528,128]{1,0:T(8,128)S(1)} %get-tuple-element.93), channel_id=1, source_target_pairs={{0,2},{1,3},{2,0},{3,1},{4,6},{5,7},{6,4},{7,5},{8,10},{9,11},{10,... | collective-permute-start | bytes 811016 | tf_op jit(solution)/shard_map/ppermute | solution.py:832
  47.2 2.9 %collective-permute-done.8.refs_3_ = f32[528,128]{1,0:T(8,128)S(1)} collective-permute-done((f32[528,128]{1,0:T(8,128)S(1)}, f32[528,128]{1,0:T(8,128)S(1)}, u32[]{:S(2)}, u32[]{:S(2)}) %collective-permute-start.8) | collective-permute-done | bytes 270368 | tf_op jit(solution)/shard_map/ppermute | solution.py:805
  51.3 1.8 %shard_map.88 = (bf16[4,256,256]{2,1,0:T(8,128)(2,1)S(1)}, bf16[4,256,256]{2,1,0:T(8,128)(2,1)S(1)}) custom-call(s32[1]{0:T(128)} %bitcast.place_ref, s32[2,16]{1,0:T(2,128)S(1)} %copy-done.1, bf16[9,256,256]{2,1,0:T(8,128)(2,1)S(1)} %get-tuple-element.65.high_ref, bf16[9,256,256]{2,1,0:T(8,128)(2,1)S(1)} %get-tuple-element.66.low_ref, ...), custom_call_target="tpu_custom_call" | custom-call | flops 536870912 | bytes 4194304 | tf_op jit(solution)/shard_map/pallas_call | solution.py:821
  55.6 4.7 %collective-permute-done.10.far_ref = f32[528,128]{1,0:T(8,128)S(1)} collective-permute-done((f32[528,128]{1,0:T(8,128)S(1)}, f32[528,128]{1,0:T(8,128)S(1)}, u32[]{:S(2)}, u32[]{:S(2)}) %collective-permute-start.10) | collective-permute-done | bytes 270368 | tf_op jit(solution)/shard_map/ppermute | solution.py:832
  60.3 2.0 %shard_map.90 = (f32[2,256,256]{2,1,0:T(8,128)S(1)}, f32[2,256,256]{2,1,0:T(8,128)S(1)}, f32[1,256]{1,0:T(1,128)S(1)}) custom-call(s32[1]{0:T(128)} %bitcast.place_ref, s32[2,16]{1,0:T(2,128)S(1)} %copy-done.1, f32[8,2,256,128]{3,2,1,0:T(8,128)S(1)} %get-tuple-element.64.edge_ref, bf16[4,256,256]{2,1,0:T(8,128)(2,1)S(1)} %get-tuple-element.73._.power_high, ...), custom_call_target="tpu_custom_call" | custom-call | flops 805306368 | bytes 2097152 | tf_op jit(solution)/shard_map/pallas_call | solution.py:841
  62.3 4.3 %collective-permute-done.12.far_ref = f32[528,128]{1,0:T(8,128)S(1)} collective-permute-done((f32[528,128]{1,0:T(8,128)S(1)}, f32[528,128]{1,0:T(8,128)S(1)}, u32[]{:S(2)}, u32[]{:S(2)}) %collective-permute-start.12) | collective-permute-done | bytes 270368 | tf_op jit(solution)/shard_map/ppermute | solution.py:832
  66.6 1.8 %shard_map.91 = (f32[2,256,256]{2,1,0:T(8,128)S(1)}, f32[2,256,256]{2,1,0:T(8,128)S(1)}, f32[1,256]{1,0:T(1,128)S(1)}) custom-call(s32[1]{0:T(128)} %bitcast.place_ref, s32[2,16]{1,0:T(2,128)S(1)} %copy-done.1, f32[8,2,256,128]{3,2,1,0:T(8,128)S(1)} %get-tuple-element.64.edge_ref, bf16[4,256,256]{2,1,0:T(8,128)(2,1)S(1)} %get-tuple-element.73._.power_high, ...), custom_call_target="tpu_custom_call" | custom-call | flops 805306368 | bytes 2097152 | tf_op jit(solution)/shard_map/pallas_call | solution.py:841
  70.1 1.9 %collective-permute-start.16 = (f32[528,128]{1,0:T(8,128)S(1)}, f32[528,128]{1,0:T(8,128)S(1)}, u32[]{:S(2)}, u32[]{:S(2)}) collective-permute-start(f32[528,128]{1,0:T(8,128)S(1)} %get-tuple-element.108), channel_id=1, source_target_pairs={{0,6},{1,7},{2,4},{3,5},{4,2},{5,3},{6,0},{7,1},{8,14},{9,15},{10,... | collective-permute-start | bytes 811016 | tf_op jit(solution)/shard_map/ppermute | solution.py:832
  72.0 3.7 %shard_map.92 = (f32[1,2,256,2048]{3,2,1,0:T(8,128)}, f32[256,256]{1,0:T(8,128)S(1)}, f32[2,256,128]{2,1,0:T(8,128)S(1)}, f32[1,256]{1,0:T(1,128)S(1)}) custom-call(s32[1]{0:T(128)} %bitcast.place_ref, s32[2,16]{1,0:T(2,128)S(1)} %copy-done.2, bf16[9,256,256]{2,1,0:T(8,128)(2,1)S(1)} %get-tuple-element.61.high_ref, ...), custom_call_target="tpu_custom_call" | custom-call | flops 1610612736 | bytes 4194304 | tf_op jit(solution)/shard_map/pallas_call | solution.py:713
  75.7 2.2 %collective-permute-done.9.far_ref = f32[528,128]{1,0:T(8,128)S(1)} collective-permute-done((f32[528,128]{1,0:T(8,128)S(1)}, f32[528,128]{1,0:T(8,128)S(1)}, u32[]{:S(2)}, u32[]{:S(2)}) %collective-permute-start.9) | collective-permute-done | bytes 270368 | tf_op jit(solution)/shard_map/ppermute | solution.py:832
  77.9 2.0 %shard_map.93 = (f32[2,256,256]{2,1,0:T(8,128)S(1)}, f32[2,256,256]{2,1,0:T(8,128)S(1)}, f32[1,256]{1,0:T(1,128)S(1)}) custom-call(s32[1]{0:T(128)} %bitcast.place_ref, s32[2,16]{1,0:T(2,128)S(1)} %copy-done.1, f32[8,2,256,128]{3,2,1,0:T(8,128)S(1)} %get-tuple-element.64.edge_ref, bf16[4,256,256]{2,1,0:T(8,128)(2,1)S(1)} %get-tuple-element.73._.power_high, ...), custom_call_target="tpu_custom_call" | custom-call | flops 805306368 | bytes 2097152 | tf_op jit(solution)/shard_map/pallas_call | solution.py:841
  80.0 3.6 %collective-permute-done.15.near_ref = f32[528,128]{1,0:T(8,128)S(1)} collective-permute-done((f32[528,128]{1,0:T(8,128)S(1)}, f32[528,128]{1,0:T(8,128)S(1)}, u32[]{:S(2)}, u32[]{:S(2)}) %collective-permute-start.15) | collective-permute-done | bytes 270368 | tf_op jit(solution)/shard_map/ppermute | solution.py:832
  83.6 1.8 %shard_map.94 = (f32[2,256,256]{2,1,0:T(8,128)S(1)}, f32[2,256,256]{2,1,0:T(8,128)S(1)}, f32[1,256]{1,0:T(1,128)S(1)}) custom-call(s32[1]{0:T(128)} %bitcast.place_ref, s32[2,16]{1,0:T(2,128)S(1)} %copy-done.1, f32[8,2,256,128]{3,2,1,0:T(8,128)S(1)} %get-tuple-element.64.edge_ref, bf16[4,256,256]{2,1,0:T(8,128)(2,1)S(1)} %get-tuple-element.73._.power_high, ...), custom_call_target="tpu_custom_call" | custom-call | flops 805306368 | bytes 2097152 | tf_op jit(solution)/shard_map/pallas_call | solution.py:841
  85.5 1.9 %collective-permute-done.18.refs_3_ = f32[2,256,256]{2,1,0:T(8,128)S(1)} collective-permute-done((f32[2,256,256]{2,1,0:T(8,128)S(1)}, f32[2,256,256]{2,1,0:T(8,128)S(1)}, u32[]{:S(2)}, u32[]{:S(2)}) %collective-permute-start.18) | collective-permute-done | bytes 524320 | tf_op jit(solution)/shard_map/ppermute | solution.py:857
  87.4 4.2 %shard_map.95 = (f32[1,2,256,2048]{3,2,1,0:T(8,128)}, f32[2,256]{1,0:T(2,128)S(1)}) custom-call(s32[1]{0:T(128)} %bitcast.place_ref, s32[2,16]{1,0:T(2,128)S(1)} %copy-done.2, bf16[9,256,256]{2,1,0:T(8,128)(2,1)S(1)} %get-tuple-element.61.high_ref, bf16[9,256,256]{2,1,0:T(8,128)(2,1)S(1)} %get-tuple-element.62.low_ref, ...), custom_call_target="tpu_custom_call", output_to_operand_aliasing={{0}: (11, {})} | custom-call | flops 1610612736 | bytes 4194304 | tf_op jit(solution)/shard_map/pallas_call | solution.py:713
  91.6 1.6 %collective-permute-start.19 = (f32[2,256]{1,0:T(2,128)S(1)}, f32[2,256]{1,0:T(2,128)S(1)}, u32[]{:S(2)}, u32[]{:S(2)}) collective-permute-start(f32[2,256]{1,0:T(2,128)S(1)} %get-tuple-element.119), channel_id=1, source_target_pairs={{0,8},{8,0},{16,24},{24,16},{1,9},{9,1},{17,25},{25,17},{2,10},{10... | collective-permute-start | bytes 6152 | tf_op jit(solution)/shard_map/ppermute | solution.py:732
  93.2 2.0 %collective-permute-done.19 = f32[2,256]{1,0:T(2,128)S(1)} collective-permute-done((f32[2,256]{1,0:T(2,128)S(1)}, f32[2,256]{1,0:T(2,128)S(1)}, u32[]{:S(2)}, u32[]{:S(2)}) %collective-permute-start.19) | collective-permute-done | bytes 2080 | tf_op jit(solution)/shard_map/ppermute | solution.py:732
  95.2 2.6 %collective-permute-start.20 = (f32[2,256]{1,0:T(2,128)S(1)}, f32[2,256]{1,0:T(2,128)S(1)}, u32[]{:S(2)}, u32[]{:S(2)}) collective-permute-start(f32[2,256]{1,0:T(2,128)S(1)} %add.6), channel_id=1, source_target_pairs={{0,16},{8,24},{16,0},{24,8},{1,17},{9,25},{17,1},{25,9},{2,18},{10... | collective-permute-start | bytes 6152 | tf_op jit(solution)/shard_map/ppermute | solution.py:732
  97.8 1.9 %collective-permute-done.20 = f32[2,256]{1,0:T(2,128)S(1)} collective-permute-done((f32[2,256]{1,0:T(2,128)S(1)}, f32[2,256]{1,0:T(2,128)S(1)}, u32[]{:S(2)}, u32[]{:S(2)}) %collective-permute-start.20) | collective-permute-done | bytes 2080 | tf_op jit(solution)/shard_map/ppermute | solution.py:732
  (44 shorter events, 13.0 us)
Async XLA Ops:
  0.6 2.3 %copy-start.5 = (f32[1,8,2]{1,2,0:T(2,128)S(1)}, f32[1,8,2]{1,2,0:T(2,128)}, u32[]{:S(2)}) copy-start(f32[1,8,2]{1,2,0:T(2,128)} %param.9) | copy-start | bytes 196
  0.6 2.4 %copy-start.3 = (f32[1,8,2,128,128]{4,3,2,1,0:T(8,128)S(1)}, f32[1,8,2,128,128]{4,3,2,1,0:T(8,128)}, u32[]{:S(2)}) copy-start(f32[1,8,2,128,128]{4,3,2,1,0:T(8,128)} %param.7) | copy-start | bytes 3145732
  0.7 2.4 %copy-start.4 = (f32[1,2,128,128]{3,2,1,0:T(8,128)S(1)}, f32[1,2,128,128]{3,2,1,0:T(8,128)}, u32[]{:S(2)}) copy-start(f32[1,2,128,128]{3,2,1,0:T(8,128)} %param.8) | copy-start | bytes 393220
  2.3 2.7 %collective-permute-start = (f32[1,2,1,2048]{3,2,1,0:T(1,128)}, f32[1,2,1,2048]{3,2,1,0:T(1,128)S(1)}, u32[]{:S(2)}, u32[]{:S(2)}) collective-permute-start(f32[1,2,1,2048]{3,2,1,0:T(1,128)} %shard_map.79), channel_id=1, source_target_pairs={{1,2},{3,4},{5,6},{2,1},{4,3},{6,5},{9,10},{11,12},{13,14},{10,9},... | collective-permute-start | bytes 49160 | tf_op jit(solution)/shard_map/ppermute | solution.py:750
  3.1 2.2 %copy-start = (f32[1,2,256,2048]{3,2,1,0:T(8,128)S(1)}, f32[1,2,256,2048]{3,2,1,0:T(8,128)}, u32[]{:S(2)}) copy-start(f32[1,2,256,2048]{3,2,1,0:T(8,128)} %beside_ref.3) | copy-start | bytes 12582916
  3.1 2.2 %copy-start.2 = (s32[2,16]{1,0:T(2,128)S(1)}, s32[2,16]{1,0:T(2,128)}, u32[]{:S(2)}) copy-start(s32[2,16]{1,0:T(2,128)} %index_ref.27) | copy-start | bytes 388
  8.9 6.7 %copy-start.1 = (s32[2,16]{1,0:T(2,128)S(1)}, s32[2,16]{1,0:T(2,128)}, u32[]{:S(2)}) copy-start(s32[2,16]{1,0:T(2,128)} %index_ref.26) | copy-start | bytes 388
  8.9 6.7 %collective-permute-start.1 = (f32[2,2,264,256]{3,2,1,0:T(8,128)S(1)}, f32[2,2,264,256]{3,2,1,0:T(8,128)S(1)}, u32[]{:S(2)}, u32[]{:S(2)}) collective-permute-start(f32[2,2,264,256]{3,2,1,0:T(8,128)S(1)} %get-tuple-element.69), channel_id=1, source_target_pairs={{0,1},{1,0},{2,3},{3,2},{4,5},{5,4},{6,7},{7,6},{8,9},{9,8},{10,11... | collective-permute-start | bytes 3244040 | tf_op jit(solution)/shard_map/ppermute | solution.py:783
  25.7 7.8 %collective-permute-start.5 = (f32[2,2,264,256]{3,2,1,0:T(8,128)S(1)}, f32[2,2,264,256]{3,2,1,0:T(8,128)S(1)}, u32[]{:S(2)}, u32[]{:S(2)}) collective-permute-start(f32[2,2,264,256]{3,2,1,0:T(8,128)S(1)} %get-tuple-element.79), channel_id=1, source_target_pairs={{0,1},{1,0},{2,3},{3,2},{4,5},{5,4},{6,7},{7,6},{8,9},{9,8},{10,11... | collective-permute-start | bytes 3244040 | tf_op jit(solution)/shard_map/ppermute | solution.py:783
  26.1 17.2 %collective-permute-start.3 = (f32[528,128]{1,0:T(8,128)S(1)}, f32[528,128]{1,0:T(8,128)S(1)}, u32[]{:S(2)}, u32[]{:S(2)}) collective-permute-start(f32[528,128]{1,0:T(8,128)S(1)} %get-tuple-element.70._), channel_id=1, source_target_pairs={{0,4},{1,5},{2,6},{3,7},{4,0},{5,1},{6,2},{7,3},{8,12},{9,13},{10,... | collective-permute-start | bytes 811016 | tf_op jit(solution)/shard_map/ppermute | solution.py:805
  28.2 14.8 %collective-permute-start.4 = (f32[528,128]{1,0:T(8,128)S(1)}, f32[528,128]{1,0:T(8,128)S(1)}, u32[]{:S(2)}, u32[]{:S(2)}) collective-permute-start(f32[528,128]{1,0:T(8,128)S(1)} %get-tuple-element.78), channel_id=1, source_target_pairs={{0,6},{1,7},{2,4},{3,5},{4,2},{5,3},{6,0},{7,1},{8,14},{9,15},{10,... | collective-permute-start | bytes 811016 | tf_op jit(solution)/shard_map/ppermute | solution.py:805
  29.4 13.9 %collective-permute-start.2 = (f32[528,128]{1,0:T(8,128)S(1)}, f32[528,128]{1,0:T(8,128)S(1)}, u32[]{:S(2)}, u32[]{:S(2)}) collective-permute-start(f32[528,128]{1,0:T(8,128)S(1)} %get-tuple-element.77), channel_id=1, source_target_pairs={{0,2},{1,3},{2,0},{3,1},{4,6},{5,7},{6,4},{7,5},{8,10},{9,11},{10,... | collective-permute-start | bytes 811016 | tf_op jit(solution)/shard_map/ppermute | solution.py:805
  36.6 13.5 %collective-permute-start.8 = (f32[528,128]{1,0:T(8,128)S(1)}, f32[528,128]{1,0:T(8,128)S(1)}, u32[]{:S(2)}, u32[]{:S(2)}) collective-permute-start(f32[528,128]{1,0:T(8,128)S(1)} %get-tuple-element.88), channel_id=1, source_target_pairs={{0,6},{1,7},{2,4},{3,5},{4,2},{5,3},{6,0},{7,1},{8,14},{9,15},{10,... | collective-permute-start | bytes 811016 | tf_op jit(solution)/shard_map/ppermute | solution.py:805
  38.8 15.6 %collective-permute-start.7 = (f32[528,128]{1,0:T(8,128)S(1)}, f32[528,128]{1,0:T(8,128)S(1)}, u32[]{:S(2)}, u32[]{:S(2)}) collective-permute-start(f32[528,128]{1,0:T(8,128)S(1)} %get-tuple-element.80._), channel_id=1, source_target_pairs={{0,4},{1,5},{2,6},{3,7},{4,0},{5,1},{6,2},{7,3},{8,12},{9,13},{10,... | collective-permute-start | bytes 811016 | tf_op jit(solution)/shard_map/ppermute | solution.py:805
  43.0 11.4 %collective-permute-start.6 = (f32[528,128]{1,0:T(8,128)S(1)}, f32[528,128]{1,0:T(8,128)S(1)}, u32[]{:S(2)}, u32[]{:S(2)}) collective-permute-start(f32[528,128]{1,0:T(8,128)S(1)} %get-tuple-element.87), channel_id=1, source_target_pairs={{0,2},{1,3},{2,0},{3,1},{4,6},{5,7},{6,4},{7,5},{8,10},{9,11},{10,... | collective-permute-start | bytes 811016 | tf_op jit(solution)/shard_map/ppermute | solution.py:805
  44.4 15.8 %collective-permute-start.10 = (f32[528,128]{1,0:T(8,128)S(1)}, f32[528,128]{1,0:T(8,128)S(1)}, u32[]{:S(2)}, u32[]{:S(2)}) collective-permute-start(f32[528,128]{1,0:T(8,128)S(1)} %get-tuple-element.93), channel_id=1, source_target_pairs={{0,2},{1,3},{2,0},{3,1},{4,6},{5,7},{6,4},{7,5},{8,10},{9,11},{10,... | collective-permute-start | bytes 811016 | tf_op jit(solution)/shard_map/ppermute | solution.py:832
  46.3 16.1 %collective-permute-start.11 = (f32[528,128]{1,0:T(8,128)S(1)}, f32[528,128]{1,0:T(8,128)S(1)}, u32[]{:S(2)}, u32[]{:S(2)}) collective-permute-start(f32[528,128]{1,0:T(8,128)S(1)} %get-tuple-element.97), channel_id=1, source_target_pairs={{0,4},{1,5},{2,6},{3,7},{4,0},{5,1},{6,2},{7,3},{8,12},{9,13},{10,... | collective-permute-start | bytes 811016 | tf_op jit(solution)/shard_map/ppermute | solution.py:832
  50.1 16.5 %collective-permute-start.12 = (f32[528,128]{1,0:T(8,128)S(1)}, f32[528,128]{1,0:T(8,128)S(1)}, u32[]{:S(2)}, u32[]{:S(2)}) collective-permute-start(f32[528,128]{1,0:T(8,128)S(1)} %get-tuple-element.98), channel_id=1, source_target_pairs={{0,6},{1,7},{2,4},{3,5},{4,2},{5,3},{6,0},{7,1},{8,14},{9,15},{10,... | collective-permute-start | bytes 811016 | tf_op jit(solution)/shard_map/ppermute | solution.py:832
  62.3 9.8 %collective-permute-start.13 = (f32[2,256,256]{2,1,0:T(8,128)S(1)}, f32[2,256,256]{2,1,0:T(8,128)S(1)}, u32[]{:S(2)}, u32[]{:S(2)}) collective-permute-start(f32[2,256,256]{2,1,0:T(8,128)S(1)} %get-tuple-element.101), channel_id=1, source_target_pairs={{0,1},{1,0},{2,3},{3,2},{4,5},{5,4},{6,7},{7,6},{8,9},{9,8},{10,11... | collective-permute-start | bytes 1572872 | tf_op jit(solution)/shard_map/ppermute | solution.py:857
  68.4 3.6 %collective-permute-start.14 = (f32[2,256,256]{2,1,0:T(8,128)S(1)}, f32[2,256,256]{2,1,0:T(8,128)S(1)}, u32[]{:S(2)}, u32[]{:S(2)}) collective-permute-start(f32[2,256,256]{2,1,0:T(8,128)S(1)} %get-tuple-element.102), channel_id=1, source_target_pairs={{0,1},{1,0},{2,3},{3,2},{4,5},{5,4},{6,7},{7,6},{8,9},{9,8},{10,11... | collective-permute-start | bytes 1572872 | tf_op jit(solution)/shard_map/ppermute | solution.py:857
  68.5 9.4 %collective-permute-start.9 = (f32[528,128]{1,0:T(8,128)S(1)}, f32[528,128]{1,0:T(8,128)S(1)}, u32[]{:S(2)}, u32[]{:S(2)}) collective-permute-start(f32[528,128]{1,0:T(8,128)S(1)} %get-tuple-element.90), channel_id=1, source_target_pairs={{0,2},{1,3},{2,0},{3,1},{4,6},{5,7},{6,4},{7,5},{8,10},{9,11},{10,... | collective-permute-start | bytes 811016 | tf_op jit(solution)/shard_map/ppermute | solution.py:832
  69.3 14.3 %collective-permute-start.15 = (f32[528,128]{1,0:T(8,128)S(1)}, f32[528,128]{1,0:T(8,128)S(1)}, u32[]{:S(2)}, u32[]{:S(2)}) collective-permute-start(f32[528,128]{1,0:T(8,128)S(1)} %get-tuple-element.107), channel_id=1, source_target_pairs={{0,4},{1,5},{2,6},{3,7},{4,0},{5,1},{6,2},{7,3},{8,12},{9,13},{10,... | collective-permute-start | bytes 811016 | tf_op jit(solution)/shard_map/ppermute | solution.py:832
  70.1 13.5 %collective-permute-start.16 = (f32[528,128]{1,0:T(8,128)S(1)}, f32[528,128]{1,0:T(8,128)S(1)}, u32[]{:S(2)}, u32[]{:S(2)}) collective-permute-start(f32[528,128]{1,0:T(8,128)S(1)} %get-tuple-element.108), channel_id=1, source_target_pairs={{0,6},{1,7},{2,4},{3,5},{4,2},{5,3},{6,0},{7,1},{8,14},{9,15},{10,... | collective-permute-start | bytes 811016 | tf_op jit(solution)/shard_map/ppermute | solution.py:832
  79.9 5.6 %collective-permute-start.17 = (f32[2,256,256]{2,1,0:T(8,128)S(1)}, f32[2,256,256]{2,1,0:T(8,128)S(1)}, u32[]{:S(2)}, u32[]{:S(2)}) collective-permute-start(f32[2,256,256]{2,1,0:T(8,128)S(1)} %get-tuple-element.111), channel_id=1, source_target_pairs={{0,1},{1,0},{2,3},{3,2},{4,5},{5,4},{6,7},{7,6},{8,9},{9,8},{10,11... | collective-permute-start | bytes 1572872 | tf_op jit(solution)/shard_map/ppermute | solution.py:857
  85.4 2.0 %collective-permute-start.18 = (f32[2,256,256]{2,1,0:T(8,128)S(1)}, f32[2,256,256]{2,1,0:T(8,128)S(1)}, u32[]{:S(2)}, u32[]{:S(2)}) collective-permute-start(f32[2,256,256]{2,1,0:T(8,128)S(1)} %get-tuple-element.112), channel_id=1, source_target_pairs={{0,1},{1,0},{2,3},{3,2},{4,5},{5,4},{6,7},{7,6},{8,9},{9,8},{10,11... | collective-permute-start | bytes 1572872 | tf_op jit(solution)/shard_map/ppermute | solution.py:857
  91.6 3.7 %collective-permute-start.19 = (f32[2,256]{1,0:T(2,128)S(1)}, f32[2,256]{1,0:T(2,128)S(1)}, u32[]{:S(2)}, u32[]{:S(2)}) collective-permute-start(f32[2,256]{1,0:T(2,128)S(1)} %get-tuple-element.119), channel_id=1, source_target_pairs={{0,8},{8,0},{16,24},{24,16},{1,9},{9,1},{17,25},{25,17},{2,10},{10... | collective-permute-start | bytes 6152 | tf_op jit(solution)/shard_map/ppermute | solution.py:732
  95.2 4.5 %collective-permute-start.20 = (f32[2,256]{1,0:T(2,128)S(1)}, f32[2,256]{1,0:T(2,128)S(1)}, u32[]{:S(2)}, u32[]{:S(2)}) collective-permute-start(f32[2,256]{1,0:T(2,128)S(1)} %add.6), channel_id=1, source_target_pairs={{0,16},{8,24},{16,0},{24,8},{1,17},{9,25},{17,1},{25,9},{2,18},{10... | collective-permute-start | bytes 6152 | tf_op jit(solution)/shard_map/ppermute | solution.py:732
where the time goes:
time: 100 us
  Pallas kernels  48.5 us (48%)
  waiting for transfers between devices  25.3 us (25%)
  starting transfers between devices  24.7 us (25%)
    ppermute x6, waiting for transfers between devices, fast_shards(): lax.ppermute(carries[offset], 'plane', moves)  14.7 us
    pallas_call x4, Pallas kernels, fast_shards(): pl.pallas_call(functools.partial(open_sweep_kernel, groups=groups, group=...  12.3 us
    pallas_call x2, Pallas kernels, last_pass(): pl.pallas_call(functools.partial(last_pass_kernel, half=half, step=step,...  7.9 us
    ppermute x6, starting transfers between devices, fast_shards(): lax.ppermute(carries[offset], 'plane', moves)  7.58 us
    pallas_call x2, Pallas kernels, first_pass(): pl.pallas_call(functools.partial(first_pass_kernel, half=half, group=grou...  7.56 us
    pallas_call x4, Pallas kernels, fast_shards(): pl.pallas_call(functools.partial(close_sweep_kernel, groups=groups, group...  7.55 us
    ppermute x6, starting transfers between devices, fast_shards(): lax.ppermute(item, 'plane', moves)  7.14 us
    ppermute x2, starting transfers between devices, fast_shards(): come[half] = lax.ppermute(send, 'plane', partner)  4.81 us
  transfers between devices with their start and end apart: 21, of which 10 were waited for; matrix products, arithmetic and copies ran while one was open for 0% of the time, Pallas kernels for 29%

commit v1 on v0

--- a/solution.py
+++ b/solution.py
@@ -482,8 +482,10 @@
         base_ref[k // half, k % half] = now[:group, (k % half) * group : (k % half + 1) * group]
         if k == groups - 1:
             row_re, row_im = last_row(now, group)
-            for part, row in enumerate((row_re, row_im)):
-                store_pair(slice(4 * group + 8 * part, 4 * group + 8 * part + 8), jnp.broadcast_to(row, (8, width)))
+            store_pair(
+                slice(4 * group, 4 * group + 8),
+                jnp.concatenate([row_re, row_im, jnp.zeros((6, width), f32)], axis=0),
+            )
             state = halves(open_state(row_re, row_im))
         else:
             done = step(k + 1, following, state, last_row(now, group), first_row(earlier, group) if earlier is not None else None)
@@ -558,8 +560,7 @@
         for part in range(2):
             tail = slice((part + 1) * group - 16, (part + 1) * group)
             row = product((high_ref[last, tail, :], low_ref[last, tail, :]), first)[15:16]
-            base = size + 8 * part
-            rows[q, 8 * part : 8 * part + 8, :] = held[q - 1, base : base + 8, :] + row
+            rows[q, part : part + 1, :] = held[q - 1, size + part : size + part + 1, :] + row
         if q > 1:
             second = halves(held[q, 2 * group : size, :])
             held[q - 1, 0 : 2 * group, :] = held[q - 1, 0 : 2 * group, :] + product(keep, first)
@@ -572,7 +573,7 @@
     for offset in range(chips):
         target = chip ^ offset
         outs[offset][0:size, :] = held[(target + 1) % chips, 0:size, :]
-        outs[offset][size : size + 16, :] = rows[target]
+        outs[offset][size : size + 8, :] = rows[target]
 
 
 def close_sweep_kernel(place_ref, index_ref, edge_ref, power_high, power_low, map_high, map_low, local_ref, base_ref,
@@ -595,7 +596,7 @@
         if k == 0:
             level = index_ref[1, chip * groups]
             base = 4 * group
-            done = add_edge(done, edge_ref, level, 0, carried(base, 8)[0:1], carried(base + 8, 8)[0:1])
+            done = add_edge(done, edge_ref, level, 0, carried(base, 8)[0:1], carried(base, 8)[1:2])
         rows = slice((k % half) * group, (k % half + 1) * group)
         result[k // half, 0, rows, :] = done[:group]
         result[k // half, 1, rows, :] = done[group:]
@@ -753,7 +754,7 @@
     left = make_tables(left_table_kernel, rhs_table, inv_table[0], couple_table[0], (levels, 2, double, group))
 
     wide = block // 2
-    piece = whole((4 * group + 16, wide))
+    piece = whole((4 * group + 8, wide))
     local = whole((groups, double, block))
     base = whole((2, groups // 2, group, group))
     matrices = whole((groups, double, double), bf16)
@@ -775,35 +776,43 @@
 
     keep, come = {}, {}
     locals_, bases, theirs = {}, {}, {}
-    carry = after = None
-    for half in (1, 0):
-        result = first_pass(place, recv_index, wavefield, halo, right, half, carry, after, block, group)
-        carry, keep[half], send = result if half else (None, *result)
-        after = carry if half else make_powers(keep[half])
+
+    def first(half, carry, ready):
+        result = first_pass(place, recv_index, wavefield, halo, right, half, carry, ready, block, group)
+        *carry, keep[half], send = result
         come[half] = lax.ppermute(send, "plane", partner)
-        for second_pair in (1, 0):
-            spec = pltpu.PrefetchScalarGridSpec(
-                num_scalar_prefetch=2,
-                grid=(1,),
-                in_specs=[vmem()] * 3
-                + [pl.BlockSpec((1,) + keep[half].shape[1:], lambda i, at, _, o=second_pair: ((at[0] // 4) ^ o, 0, 0, 0))] * 2
-                + [anywhere()],
-                out_specs=[vmem()] * 4,
-                scratch_shapes=[pltpu.VMEM((2,) + piece.shape, f32)],
-            )
-            name = "%d_%d" % (half, second_pair)
-            near, far, locals_[name], bases[name] = pl.pallas_call(
-                functools.partial(open_sweep_kernel, groups=groups, group=group),
-                grid_spec=spec,
-                out_shape=[piece, piece, local, base],
-                compiler_params=params(24),
-                cost_estimate=cost(groups * group * block * group * 48, 8 * groups * group * block * 3),
-            )(place, shot_index, *left, keep[half], come[half], after)
-            after = near
-            for offset, item in ((2 * second_pair + 1, far), (2 * second_pair, near)):
-                moves = [(d, d ^ (2 * offset)) for d in range(devices)]
-                theirs[half, offset] = lax.ppermute(item, "plane", moves) if offset else item
-
+        return carry
+
+    def open_sweep(half, second_pair, ready):
+        spec = pltpu.PrefetchScalarGridSpec(
+            num_scalar_prefetch=2,
+            grid=(1,),
+            in_specs=[vmem()] * 3
+            + [pl.BlockSpec((1,) + keep[half].shape[1:], lambda i, at, _: ((at[0] // 4) ^ second_pair, 0, 0, 0))] * 2
+            + [anywhere()],
+            out_specs=[vmem()] * 4,
+            scratch_shapes=[pltpu.VMEM((2,) + piece.shape, f32)],
+        )
+        name = "%d_%d" % (half, second_pair)
+        near, far, locals_[name], bases[name] = pl.pallas_call(
+            functools.partial(open_sweep_kernel, groups=groups, group=group),
+            grid_spec=spec,
+            out_shape=[piece, piece, local, base],
+            compiler_params=params(24),
+            cost_estimate=cost(groups * group * block * group * 48, 8 * groups * group * block * 3),
+        )(place, shot_index, *left, keep[half], come[half], ready)
+        for offset, item in ((2 * second_pair + 1, far), (2 * second_pair, near)):
+            moves = [(d, d ^ (2 * offset)) for d in range(devices)]
+            theirs[half, offset] = lax.ppermute(item, "plane", moves) if offset else item
+        return near
+
+    (carry,) = first(1, None, None)
+    after = open_sweep(1, 1, carry)
+    first(0, carry, after)
+    after = open_sweep(1, 0, keep[0])
+    after = open_sweep(0, 1, after)
+    after = open_sweep(0, 0, after)
+    after = make_powers(after)
     power_high, power_low, chip_high, chip_low = powers
     came = {}
     for half in (1, 0):
@@ -812,7 +821,7 @@
             out_shape=[piece] * chips,
             in_specs=[smem()] + [vmem()] * (6 + chips) + [anywhere()],
             out_specs=[vmem()] * chips,
-            scratch_shapes=[pltpu.VMEM((chips,) + piece.shape, f32), pltpu.VMEM((chips, 16, wide), f32)],
+            scratch_shapes=[pltpu.VMEM((chips,) + piece.shape, f32), pltpu.VMEM((chips, 8, wide), f32)],
             compiler_params=params(20),
             cost_estimate=cost(3 * group * group * wide * 24, 4 * 1024 * 1024),
         )(place, left[0], left[1], power_high, power_low, chip_high, chip_low, *[theirs[half, o] for o in range(chips)], after)

time: 100 us -> 96.4 us (0.964)
  waiting for transfers between devices: 25.3 us -> 21.9 us
    ppermute x6, waiting for transfers between devices: 14.7 us -> 13 us  [fast_shards(): lax.ppermute(carries[offset], 'plane', moves)]
    ppermute x8, waiting for transfers between devices: 4.72 us -> 3.09 us  [the longest x6 2.62 us: open_sweep(): lax.ppermute(item, 'plane', moves)]
  transfers between devices with their start and end apart: 21 -> 21, of which waited for: 10 -> 9; matrix products, arithmetic and copies ran while one was open for 0% -> 0% of each run, Pallas kernels for 29% -> 33%
where the time goes in v1:
time: 96.4 us; the launch traced here: 96.3 us
  Pallas kernels  48.3 us (50%)
  starting transfers between devices  24.3 us (25%)
  waiting for transfers between devices  21.9 us (23%)
    ppermute x6, waiting for transfers between devices, fast_shards(): lax.ppermute(carries[offset], 'plane', moves)  13 us
    pallas_call x4, Pallas kernels, open_sweep(): pl.pallas_call(functools.partial(open_sweep_kernel, groups=groups, group=...  12.4 us
    pallas_call x2, Pallas kernels, last_pass(): pl.pallas_call(functools.partial(last_pass_kernel, half=half, step=step,...  7.89 us
    pallas_call x4, Pallas kernels, fast_shards(): pl.pallas_call(functools.partial(close_sweep_kernel, groups=groups, group...  7.48 us
    pallas_call x2, Pallas kernels, first_pass(): pl.pallas_call(functools.partial(first_pass_kernel, half=half, group=grou...  7.39 us
    ppermute x6, starting transfers between devices, open_sweep(): lax.ppermute(item, 'plane', moves)  7.19 us
    ppermute x6, starting transfers between devices, fast_shards(): lax.ppermute(carries[offset], 'plane', moves)  7.11 us
    ppermute x2, starting transfers between devices, first(): come[half] = lax.ppermute(send, 'plane', partner)  4.83 us
  transfers between devices with their start and end apart: 21, of which 9 were waited for; matrix products, arithmetic and copies ran while one was open for 0% of the time, Pallas kernels for 33%

profile of v1, /device:TPU:0, one launch (start us, length us, event | category | flops | bytes accessed | tf_op | source)
XLA Modules:
  0.0 96.3 jit_solution(10870608263353267506)
XLA Ops:
  0.7 1.6 %shard_map.79 = f32[1,2,1,2048]{3,2,1,0:T(1,128)} custom-call(s32[1]{0:T(128)} %bitcast.place_ref, f32[1,2,256,2048]{3,2,1,0:T(8,128)} %beside_ref.3), custom_call_target="tpu_custom_call" | custom-call | flops 20000000000 | bytes 1048576 | tf_op jit(solution)/shard_map/pallas_call | solution.py:285
  3.1 1.9 %shard_map.77 = (bf16[9,256,256]{2,1,0:T(8,128)(2,1)S(1)}, bf16[9,256,256]{2,1,0:T(8,128)(2,1)S(1)}, f32[8,4,256]{2,1,0:T(4,128)S(1)}) custom-call(f32[1,8,2]{2,1,0:T(8,128)S(1)} %copy.9.rhs_ref, f32[8,2,128,128]{3,2,1,0:T(8,128)S(1)} %bitcast.3, f32[2,128,128]{2,1,0:T(8,128)S(1)} %bitcast.5), custom_call_target="tpu_custom_call" | custom-call | flops 20000000000 | bytes 4194304 | tf_op jit(solution)/shard_map/pallas_call | solution.py:262
  5.3 3.6 %shard_map.80 = (f32[264,256]{1,0:T(8,128)S(1)}, f32[2,2,264,256]{3,2,1,0:T(8,128)S(1)}, f32[2,2,264,256]{3,2,1,0:T(8,128)S(1)}) custom-call(s32[1]{0:T(128)} %bitcast.place_ref, s32[2,16]{1,0:T(2,128)S(1)} %copy-done.2, f32[1,2,256,2048]{3,2,1,0:T(8,128)S(1)} %copy-done, f32[1,2,256,2048]{3,2,1,0:T(8,128)S(1)} %copy-done, ...), custom_call_target="tpu_custom_call" | custom-call | flops 1660944384 | bytes 4325376 | tf_op jit(solution)/shard_map/pallas_call | solution.py:383
  8.9 4.4 %collective-permute-start.1 = (f32[2,2,264,256]{3,2,1,0:T(8,128)S(1)}, f32[2,2,264,256]{3,2,1,0:T(8,128)S(1)}, u32[]{:S(2)}, u32[]{:S(2)}) collective-permute-start(f32[2,2,264,256]{3,2,1,0:T(8,128)S(1)} %get-tuple-element.69), channel_id=1, source_target_pairs={{0,1},{1,0},{2,3},{3,2},{4,5},{5,4},{6,7},{7,6},{8,9},{9,8},{10,11... | collective-permute-start | bytes 3244040 | tf_op jit(solution)/shard_map/ppermute | solution.py:783
  13.3 1.9 %shard_map.78 = (bf16[9,256,256]{2,1,0:T(8,128)(2,1)S(1)}, bf16[9,256,256]{2,1,0:T(8,128)(2,1)S(1)}, f32[8,2,256,128]{3,2,1,0:T(8,128)S(1)}) custom-call(f32[1,8,2]{2,1,0:T(8,128)S(1)} %copy.9.rhs_ref, f32[8,2,128,128]{3,2,1,0:T(8,128)S(1)} %bitcast.4, f32[2,128,128]{2,1,0:T(8,128)S(1)} %bitcast.6), custom_call_target="tpu_custom_call" | custom-call | flops 20000000000 | bytes 4194304 | tf_op jit(solution)/shard_map/pallas_call | solution.py:262
  15.6 3.1 %shard_map.81 = (f32[520,128]{1,0:T(8,128)S(1)}, f32[520,128]{1,0:T(8,128)S(1)}, f32[4,256,256]{2,1,0:T(8,128)S(1)}, f32[2,2,128,128]{3,2,1,0:T(8,128)S(1)}) custom-call(s32[1]{0:T(128)} %bitcast.place_ref, s32[2,16]{1,0:T(2,128)S(1)} %copy-done.1, bf16[9,256,256]{2,1,0:T(8,128)(2,1)S(1)} %get-tuple-element.65.high_ref, ...), custom_call_target="tpu_custom_call" | custom-call | flops 1610612736 | bytes 3145728 | tf_op jit(solution)/shard_map/pallas_call | solution.py:797
  18.7 3.8 %shard_map.82 = (f32[2,2,264,256]{3,2,1,0:T(8,128)S(1)}, f32[2,2,264,256]{3,2,1,0:T(8,128)S(1)}) custom-call(s32[1]{0:T(128)} %bitcast.place_ref, s32[2,16]{1,0:T(2,128)S(1)} %copy-done.2, f32[1,2,256,2048]{3,2,1,0:T(8,128)S(1)} %copy-done, f32[1,2,256,2048]{3,2,1,0:T(8,128)S(1)} %copy-done, f32[1,2,1,2048]{3,2,1,0:T(1,128)S(1)} %collective-permute-done.halo_ref, ...), custom_call_target="tpu_custom_call" | custom-call | flops 1660944384 | bytes 4325376 | tf_op jit(solution)/shard_map/pallas_call | solution.py:383
  22.9 2.0 %collective-permute-start.4 = (f32[520,128]{1,0:T(8,128)S(1)}, f32[520,128]{1,0:T(8,128)S(1)}, u32[]{:S(2)}, u32[]{:S(2)}) collective-permute-start(f32[520,128]{1,0:T(8,128)S(1)} %get-tuple-element.70.refs_1_), channel_id=1, source_target_pairs={{0,4},{1,5},{2,6},{3,7},{4,0},{5,1},{6,2},{7,3},{8,12},{9,13},{10,... | collective-permute-start | bytes 798728 | tf_op jit(solution)/shard_map/ppermute | solution.py:806
  26.2 3.2 %shard_map.83 = (f32[520,128]{1,0:T(8,128)S(1)}, f32[520,128]{1,0:T(8,128)S(1)}, f32[4,256,256]{2,1,0:T(8,128)S(1)}, f32[2,2,128,128]{3,2,1,0:T(8,128)S(1)}) custom-call(s32[1]{0:T(128)} %bitcast.place_ref, s32[2,16]{1,0:T(2,128)S(1)} %copy-done.1, bf16[9,256,256]{2,1,0:T(8,128)(2,1)S(1)} %get-tuple-element.65.high_ref, ...), custom_call_target="tpu_custom_call" | custom-call | flops 1610612736 | bytes 3145728 | tf_op jit(solution)/shard_map/pallas_call | solution.py:797
  29.7 3.0 %shard_map.84 = (f32[520,128]{1,0:T(8,128)S(1)}, f32[520,128]{1,0:T(8,128)S(1)}, f32[4,256,256]{2,1,0:T(8,128)S(1)}, f32[2,2,128,128]{3,2,1,0:T(8,128)S(1)}) custom-call(s32[1]{0:T(128)} %bitcast.place_ref, s32[2,16]{1,0:T(2,128)S(1)} %copy-done.1, bf16[9,256,256]{2,1,0:T(8,128)(2,1)S(1)} %get-tuple-element.65.high_ref, ...), custom_call_target="tpu_custom_call" | custom-call | flops 1610612736 | bytes 3145728 | tf_op jit(solution)/shard_map/pallas_call | solution.py:797
  32.7 2.2 %collective-permute-start.8 = (f32[520,128]{1,0:T(8,128)S(1)}, f32[520,128]{1,0:T(8,128)S(1)}, u32[]{:S(2)}, u32[]{:S(2)}) collective-permute-start(f32[520,128]{1,0:T(8,128)S(1)} %get-tuple-element.88), channel_id=1, source_target_pairs={{0,6},{1,7},{2,4},{3,5},{4,2},{5,3},{6,0},{7,1},{8,14},{9,15},{10,... | collective-permute-start | bytes 798728 | tf_op jit(solution)/shard_map/ppermute | solution.py:806
  36.1 3.0 %shard_map.85 = (f32[520,128]{1,0:T(8,128)S(1)}, f32[520,128]{1,0:T(8,128)S(1)}, f32[4,256,256]{2,1,0:T(8,128)S(1)}, f32[2,2,128,128]{3,2,1,0:T(8,128)S(1)}) custom-call(s32[1]{0:T(128)} %bitcast.place_ref, s32[2,16]{1,0:T(2,128)S(1)} %copy-done.1, bf16[9,256,256]{2,1,0:T(8,128)(2,1)S(1)} %get-tuple-element.65.high_ref, ...), custom_call_target="tpu_custom_call" | custom-call | flops 1610612736 | bytes 3145728 | tf_op jit(solution)/shard_map/pallas_call | solution.py:797
  39.1 3.8 %shard_map.86 = (bf16[4,256,256]{2,1,0:T(8,128)(2,1)S(1)}, bf16[4,256,256]{2,1,0:T(8,128)(2,1)S(1)}, bf16[2,256,256]{2,1,0:T(8,128)(2,1)S(1)}, bf16[2,256,256]{2,1,0:T(8,128)(2,1)S(1)}) custom-call(s32[2,16]{1,0:T(2,128)S(1)} %copy-done.1, bf16[9,256,256]{2,1,0:T(8,128)(2,1)S(1)} %get-tuple-element.65.high_ref, ...), custom_call_target="tpu_custom_call" | custom-call | flops 1073741824 | bytes 4194304 | tf_op jit(solution)/shard_map/pallas_call | solution.py:766
  44.3 1.9 %collective-permute-start.10 = (f32[520,128]{1,0:T(8,128)S(1)}, f32[520,128]{1,0:T(8,128)S(1)}, u32[]{:S(2)}, u32[]{:S(2)}) collective-permute-start(f32[520,128]{1,0:T(8,128)S(1)} %get-tuple-element.93), channel_id=1, source_target_pairs={{0,2},{1,3},{2,0},{3,1},{4,6},{5,7},{6,4},{7,5},{8,10},{9,11},{10,... | collective-permute-start | bytes 798728 | tf_op jit(solution)/shard_map/ppermute | solution.py:841
  47.9 1.8 %shard_map.88 = (bf16[4,256,256]{2,1,0:T(8,128)(2,1)S(1)}, bf16[4,256,256]{2,1,0:T(8,128)(2,1)S(1)}) custom-call(s32[1]{0:T(128)} %bitcast.place_ref, s32[2,16]{1,0:T(2,128)S(1)} %copy-done.1, bf16[9,256,256]{2,1,0:T(8,128)(2,1)S(1)} %get-tuple-element.65.high_ref, bf16[9,256,256]{2,1,0:T(8,128)(2,1)S(1)} %get-tuple-element.66.low_ref, ...), custom_call_target="tpu_custom_call" | custom-call | flops 536870912 | bytes 4194304 | tf_op jit(solution)/shard_map/pallas_call | solution.py:830
  49.6 2.6 %collective-permute-done.6.refs_1_ = f32[520,128]{1,0:T(8,128)S(1)} collective-permute-done((f32[520,128]{1,0:T(8,128)S(1)}, f32[520,128]{1,0:T(8,128)S(1)}, u32[]{:S(2)}, u32[]{:S(2)}) %collective-permute-start.6) | collective-permute-done | bytes 266272 | tf_op jit(solution)/shard_map/ppermute | solution.py:806
  53.3 4.6 %collective-permute-done.10.far_ref = f32[520,128]{1,0:T(8,128)S(1)} collective-permute-done((f32[520,128]{1,0:T(8,128)S(1)}, f32[520,128]{1,0:T(8,128)S(1)}, u32[]{:S(2)}, u32[]{:S(2)}) %collective-permute-start.10) | collective-permute-done | bytes 266272 | tf_op jit(solution)/shard_map/ppermute | solution.py:841
  58.0 2.0 %shard_map.90 = (f32[2,256,256]{2,1,0:T(8,128)S(1)}, f32[2,256,256]{2,1,0:T(8,128)S(1)}, f32[1,256]{1,0:T(1,128)S(1)}) custom-call(s32[1]{0:T(128)} %bitcast.place_ref, s32[2,16]{1,0:T(2,128)S(1)} %copy-done.1, f32[8,2,256,128]{3,2,1,0:T(8,128)S(1)} %get-tuple-element.64.edge_ref, bf16[4,256,256]{2,1,0:T(8,128)(2,1)S(1)} %get-tuple-element.76.power_high.refs_4_, ...), custom_call_target="tpu_custom_call" | custom-call | flops 805306368 | bytes 2097152 | tf_op jit(solution)/shard_map/pallas_call | solution.py:850
  60.0 2.8 %collective-permute-done.12.far_ref = f32[520,128]{1,0:T(8,128)S(1)} collective-permute-done((f32[520,128]{1,0:T(8,128)S(1)}, f32[520,128]{1,0:T(8,128)S(1)}, u32[]{:S(2)}, u32[]{:S(2)}) %collective-permute-start.12) | collective-permute-done | bytes 266272 | tf_op jit(solution)/shard_map/ppermute | solution.py:841
  62.8 1.7 %shard_map.91 = (f32[2,256,256]{2,1,0:T(8,128)S(1)}, f32[2,256,256]{2,1,0:T(8,128)S(1)}, f32[1,256]{1,0:T(1,128)S(1)}) custom-call(s32[1]{0:T(128)} %bitcast.place_ref, s32[2,16]{1,0:T(2,128)S(1)} %copy-done.1, f32[8,2,256,128]{3,2,1,0:T(8,128)S(1)} %get-tuple-element.64.edge_ref, bf16[4,256,256]{2,1,0:T(8,128)(2,1)S(1)} %get-tuple-element.76.power_high.refs_4_, ...), custom_call_target="tpu_custom_call" | custom-call | flops 805306368 | bytes 2097152 | tf_op jit(solution)/shard_map/pallas_call | solution.py:850
  66.3 1.9 %collective-permute-start.16 = (f32[520,128]{1,0:T(8,128)S(1)}, f32[520,128]{1,0:T(8,128)S(1)}, u32[]{:S(2)}, u32[]{:S(2)}) collective-permute-start(f32[520,128]{1,0:T(8,128)S(1)} %get-tuple-element.108), channel_id=1, source_target_pairs={{0,6},{1,7},{2,4},{3,5},{4,2},{5,3},{6,0},{7,1},{8,14},{9,15},{10,... | collective-permute-start | bytes 798728 | tf_op jit(solution)/shard_map/ppermute | solution.py:841
  68.2 3.7 %shard_map.92 = (f32[1,2,256,2048]{3,2,1,0:T(8,128)}, f32[256,256]{1,0:T(8,128)S(1)}, f32[2,256,128]{2,1,0:T(8,128)S(1)}, f32[1,256]{1,0:T(1,128)S(1)}) custom-call(s32[1]{0:T(128)} %bitcast.place_ref, s32[2,16]{1,0:T(2,128)S(1)} %copy-done.2, bf16[9,256,256]{2,1,0:T(8,128)(2,1)S(1)} %get-tuple-element.61.high_ref, ...), custom_call_target="tpu_custom_call" | custom-call | flops 1610612736 | bytes 4194304 | tf_op jit(solution)/shard_map/pallas_call | solution.py:714
  71.9 2.1 %collective-permute-done.9.far_ref = f32[520,128]{1,0:T(8,128)S(1)} collective-permute-done((f32[520,128]{1,0:T(8,128)S(1)}, f32[520,128]{1,0:T(8,128)S(1)}, u32[]{:S(2)}, u32[]{:S(2)}) %collective-permute-start.9) | collective-permute-done | bytes 266272 | tf_op jit(solution)/shard_map/ppermute | solution.py:841
  74.0 2.0 %shard_map.93 = (f32[2,256,256]{2,1,0:T(8,128)S(1)}, f32[2,256,256]{2,1,0:T(8,128)S(1)}, f32[1,256]{1,0:T(1,128)S(1)}) custom-call(s32[1]{0:T(128)} %bitcast.place_ref, s32[2,16]{1,0:T(2,128)S(1)} %copy-done.1, f32[8,2,256,128]{3,2,1,0:T(8,128)S(1)} %get-tuple-element.64.edge_ref, bf16[4,256,256]{2,1,0:T(8,128)(2,1)S(1)} %get-tuple-element.76.power_high.refs_4_, ...), custom_call_target="tpu_custom_call" | custom-call | flops 805306368 | bytes 2097152 | tf_op jit(solution)/shard_map/pallas_call | solution.py:850
  76.1 3.5 %collective-permute-done.15.near_ref = f32[520,128]{1,0:T(8,128)S(1)} collective-permute-done((f32[520,128]{1,0:T(8,128)S(1)}, f32[520,128]{1,0:T(8,128)S(1)}, u32[]{:S(2)}, u32[]{:S(2)}) %collective-permute-start.15) | collective-permute-done | bytes 266272 | tf_op jit(solution)/shard_map/ppermute | solution.py:841
  79.6 1.8 %shard_map.94 = (f32[2,256,256]{2,1,0:T(8,128)S(1)}, f32[2,256,256]{2,1,0:T(8,128)S(1)}, f32[1,256]{1,0:T(1,128)S(1)}) custom-call(s32[1]{0:T(128)} %bitcast.place_ref, s32[2,16]{1,0:T(2,128)S(1)} %copy-done.1, f32[8,2,256,128]{3,2,1,0:T(8,128)S(1)} %get-tuple-element.64.edge_ref, bf16[4,256,256]{2,1,0:T(8,128)(2,1)S(1)} %get-tuple-element.76.power_high.refs_4_, ...), custom_call_target="tpu_custom_call" | custom-call | flops 805306368 | bytes 2097152 | tf_op jit(solution)/shard_map/pallas_call | solution.py:850
  81.5 1.9 %collective-permute-done.18.refs_3_ = f32[2,256,256]{2,1,0:T(8,128)S(1)} collective-permute-done((f32[2,256,256]{2,1,0:T(8,128)S(1)}, f32[2,256,256]{2,1,0:T(8,128)S(1)}, u32[]{:S(2)}, u32[]{:S(2)}) %collective-permute-start.18) | collective-permute-done | bytes 524320 | tf_op jit(solution)/shard_map/ppermute | solution.py:866
  83.3 4.2 %shard_map.95 = (f32[1,2,256,2048]{3,2,1,0:T(8,128)}, f32[2,256]{1,0:T(2,128)S(1)}) custom-call(s32[1]{0:T(128)} %bitcast.place_ref, s32[2,16]{1,0:T(2,128)S(1)} %copy-done.2, bf16[9,256,256]{2,1,0:T(8,128)(2,1)S(1)} %get-tuple-element.61.high_ref, bf16[9,256,256]{2,1,0:T(8,128)(2,1)S(1)} %get-tuple-element.62.low_ref, ...), custom_call_target="tpu_custom_call", output_to_operand_aliasing={{0}: (11, {})} | custom-call | flops 1610612736 | bytes 4194304 | tf_op jit(solution)/shard_map/pallas_call | solution.py:714
  87.5 1.6 %collective-permute-start.19 = (f32[2,256]{1,0:T(2,128)S(1)}, f32[2,256]{1,0:T(2,128)S(1)}, u32[]{:S(2)}, u32[]{:S(2)}) collective-permute-start(f32[2,256]{1,0:T(2,128)S(1)} %get-tuple-element.119), channel_id=1, source_target_pairs={{0,8},{8,0},{16,24},{24,16},{1,9},{9,1},{17,25},{25,17},{2,10},{10... | collective-permute-start | bytes 6152 | tf_op jit(solution)/shard_map/ppermute | solution.py:733
  89.2 2.0 %collective-permute-done.19 = f32[2,256]{1,0:T(2,128)S(1)} collective-permute-done((f32[2,256]{1,0:T(2,128)S(1)}, f32[2,256]{1,0:T(2,128)S(1)}, u32[]{:S(2)}, u32[]{:S(2)}) %collective-permute-start.19) | collective-permute-done | bytes 2080 | tf_op jit(solution)/shard_map/ppermute | solution.py:733
  91.2 2.6 %collective-permute-start.20 = (f32[2,256]{1,0:T(2,128)S(1)}, f32[2,256]{1,0:T(2,128)S(1)}, u32[]{:S(2)}, u32[]{:S(2)}) collective-permute-start(f32[2,256]{1,0:T(2,128)S(1)} %add.6), channel_id=1, source_target_pairs={{0,16},{8,24},{16,0},{24,8},{1,17},{9,25},{17,1},{25,9},{2,18},{10... | collective-permute-start | bytes 6152 | tf_op jit(solution)/shard_map/ppermute | solution.py:733
  93.8 1.9 %collective-permute-done.20 = f32[2,256]{1,0:T(2,128)S(1)} collective-permute-done((f32[2,256]{1,0:T(2,128)S(1)}, f32[2,256]{1,0:T(2,128)S(1)}, u32[]{:S(2)}, u32[]{:S(2)}) %collective-permute-start.20) | collective-permute-done | bytes 2080 | tf_op jit(solution)/shard_map/ppermute | solution.py:733
  (44 shorter events, 11.3 us)
Async XLA Ops:
  0.6 2.3 %copy-start.5 = (f32[1,8,2]{1,2,0:T(2,128)S(1)}, f32[1,8,2]{1,2,0:T(2,128)}, u32[]{:S(2)}) copy-start(f32[1,8,2]{1,2,0:T(2,128)} %param.9) | copy-start | bytes 196
  0.6 2.4 %copy-start.3 = (f32[1,8,2,128,128]{4,3,2,1,0:T(8,128)S(1)}, f32[1,8,2,128,128]{4,3,2,1,0:T(8,128)}, u32[]{:S(2)}) copy-start(f32[1,8,2,128,128]{4,3,2,1,0:T(8,128)} %param.7) | copy-start | bytes 3145732
  0.7 2.4 %copy-start.4 = (f32[1,2,128,128]{3,2,1,0:T(8,128)S(1)}, f32[1,2,128,128]{3,2,1,0:T(8,128)}, u32[]{:S(2)}) copy-start(f32[1,2,128,128]{3,2,1,0:T(8,128)} %param.8) | copy-start | bytes 393220
  2.3 2.7 %collective-permute-start = (f32[1,2,1,2048]{3,2,1,0:T(1,128)}, f32[1,2,1,2048]{3,2,1,0:T(1,128)S(1)}, u32[]{:S(2)}, u32[]{:S(2)}) collective-permute-start(f32[1,2,1,2048]{3,2,1,0:T(1,128)} %shard_map.79), channel_id=1, source_target_pairs={{1,2},{3,4},{5,6},{2,1},{4,3},{6,5},{9,10},{11,12},{13,14},{10,9},... | collective-permute-start | bytes 49160 | tf_op jit(solution)/shard_map/ppermute | solution.py:751
  3.1 2.2 %copy-start = (f32[1,2,256,2048]{3,2,1,0:T(8,128)S(1)}, f32[1,2,256,2048]{3,2,1,0:T(8,128)}, u32[]{:S(2)}) copy-start(f32[1,2,256,2048]{3,2,1,0:T(8,128)} %beside_ref.3) | copy-start | bytes 12582916
  3.1 2.2 %copy-start.2 = (s32[2,16]{1,0:T(2,128)S(1)}, s32[2,16]{1,0:T(2,128)}, u32[]{:S(2)}) copy-start(s32[2,16]{1,0:T(2,128)} %index_ref.27) | copy-start | bytes 388
  8.9 6.7 %copy-start.1 = (s32[2,16]{1,0:T(2,128)S(1)}, s32[2,16]{1,0:T(2,128)}, u32[]{:S(2)}) copy-start(s32[2,16]{1,0:T(2,128)} %index_ref.26) | copy-start | bytes 388
  8.9 6.7 %collective-permute-start.1 = (f32[2,2,264,256]{3,2,1,0:T(8,128)S(1)}, f32[2,2,264,256]{3,2,1,0:T(8,128)S(1)}, u32[]{:S(2)}, u32[]{:S(2)}) collective-permute-start(f32[2,2,264,256]{3,2,1,0:T(8,128)S(1)} %get-tuple-element.69), channel_id=1, source_target_pairs={{0,1},{1,0},{2,3},{3,2},{4,5},{5,4},{6,7},{7,6},{8,9},{9,8},{10,11... | collective-permute-start | bytes 3244040 | tf_op jit(solution)/shard_map/ppermute | solution.py:783
  22.4 7.2 %collective-permute-start.2 = (f32[2,2,264,256]{3,2,1,0:T(8,128)S(1)}, f32[2,2,264,256]{3,2,1,0:T(8,128)S(1)}, u32[]{:S(2)}, u32[]{:S(2)}) collective-permute-start(f32[2,2,264,256]{3,2,1,0:T(8,128)S(1)} %get-tuple-element.72), channel_id=1, source_target_pairs={{0,1},{1,0},{2,3},{3,2},{4,5},{5,4},{6,7},{7,6},{8,9},{9,8},{10,11... | collective-permute-start | bytes 3244040 | tf_op jit(solution)/shard_map/ppermute | solution.py:783
  22.9 20.3 %collective-permute-start.4 = (f32[520,128]{1,0:T(8,128)S(1)}, f32[520,128]{1,0:T(8,128)S(1)}, u32[]{:S(2)}, u32[]{:S(2)}) collective-permute-start(f32[520,128]{1,0:T(8,128)S(1)} %get-tuple-element.70.refs_1_), channel_id=1, source_target_pairs={{0,4},{1,5},{2,6},{3,7},{4,0},{5,1},{6,2},{7,3},{8,12},{9,13},{10,... | collective-permute-start | bytes 798728 | tf_op jit(solution)/shard_map/ppermute | solution.py:806
  24.9 18.0 %collective-permute-start.5 = (f32[520,128]{1,0:T(8,128)S(1)}, f32[520,128]{1,0:T(8,128)S(1)}, u32[]{:S(2)}, u32[]{:S(2)}) collective-permute-start(f32[520,128]{1,0:T(8,128)S(1)} %get-tuple-element.81), channel_id=1, source_target_pairs={{0,6},{1,7},{2,4},{3,5},{4,2},{5,3},{6,0},{7,1},{8,14},{9,15},{10,... | collective-permute-start | bytes 798728 | tf_op jit(solution)/shard_map/ppermute | solution.py:806
  29.4 13.8 %collective-permute-start.3 = (f32[520,128]{1,0:T(8,128)S(1)}, f32[520,128]{1,0:T(8,128)S(1)}, u32[]{:S(2)}, u32[]{:S(2)}) collective-permute-start(f32[520,128]{1,0:T(8,128)S(1)} %get-tuple-element.80), channel_id=1, source_target_pairs={{0,2},{1,3},{2,0},{3,1},{4,6},{5,7},{6,4},{7,5},{8,10},{9,11},{10,... | collective-permute-start | bytes 798728 | tf_op jit(solution)/shard_map/ppermute | solution.py:806
  32.7 14.4 %collective-permute-start.8 = (f32[520,128]{1,0:T(8,128)S(1)}, f32[520,128]{1,0:T(8,128)S(1)}, u32[]{:S(2)}, u32[]{:S(2)}) collective-permute-start(f32[520,128]{1,0:T(8,128)S(1)} %get-tuple-element.88), channel_id=1, source_target_pairs={{0,6},{1,7},{2,4},{3,5},{4,2},{5,3},{6,0},{7,1},{8,14},{9,15},{10,... | collective-permute-start | bytes 798728 | tf_op jit(solution)/shard_map/ppermute | solution.py:806
  35.0 17.3 %collective-permute-start.7 = (f32[520,128]{1,0:T(8,128)S(1)}, f32[520,128]{1,0:T(8,128)S(1)}, u32[]{:S(2)}, u32[]{:S(2)}) collective-permute-start(f32[520,128]{1,0:T(8,128)S(1)} %get-tuple-element.74._), channel_id=1, source_target_pairs={{0,4},{1,5},{2,6},{3,7},{4,0},{5,1},{6,2},{7,3},{8,12},{9,13},{10,... | collective-permute-start | bytes 798728 | tf_op jit(solution)/shard_map/ppermute | solution.py:806
  42.9 9.3 %collective-permute-start.6 = (f32[520,128]{1,0:T(8,128)S(1)}, f32[520,128]{1,0:T(8,128)S(1)}, u32[]{:S(2)}, u32[]{:S(2)}) collective-permute-start(f32[520,128]{1,0:T(8,128)S(1)} %get-tuple-element.87), channel_id=1, source_target_pairs={{0,2},{1,3},{2,0},{3,1},{4,6},{5,7},{6,4},{7,5},{8,10},{9,11},{10,... | collective-permute-start | bytes 798728 | tf_op jit(solution)/shard_map/ppermute | solution.py:806
  44.3 13.7 %collective-permute-start.10 = (f32[520,128]{1,0:T(8,128)S(1)}, f32[520,128]{1,0:T(8,128)S(1)}, u32[]{:S(2)}, u32[]{:S(2)}) collective-permute-start(f32[520,128]{1,0:T(8,128)S(1)} %get-tuple-element.93), channel_id=1, source_target_pairs={{0,2},{1,3},{2,0},{3,1},{4,6},{5,7},{6,4},{7,5},{8,10},{9,11},{10,... | collective-permute-start | bytes 798728 | tf_op jit(solution)/shard_map/ppermute | solution.py:841
  46.2 13.9 %collective-permute-start.11 = (f32[520,128]{1,0:T(8,128)S(1)}, f32[520,128]{1,0:T(8,128)S(1)}, u32[]{:S(2)}, u32[]{:S(2)}) collective-permute-start(f32[520,128]{1,0:T(8,128)S(1)} %get-tuple-element.97), channel_id=1, source_target_pairs={{0,4},{1,5},{2,6},{3,7},{4,0},{5,1},{6,2},{7,3},{8,12},{9,13},{10,... | collective-permute-start | bytes 798728 | tf_op jit(solution)/shard_map/ppermute | solution.py:841
  47.1 15.7 %collective-permute-start.12 = (f32[520,128]{1,0:T(8,128)S(1)}, f32[520,128]{1,0:T(8,128)S(1)}, u32[]{:S(2)}, u32[]{:S(2)}) collective-permute-start(f32[520,128]{1,0:T(8,128)S(1)} %get-tuple-element.98), channel_id=1, source_target_pairs={{0,6},{1,7},{2,4},{3,5},{4,2},{5,3},{6,0},{7,1},{8,14},{9,15},{10,... | collective-permute-start | bytes 798728 | tf_op jit(solution)/shard_map/ppermute | solution.py:841
  59.9 8.3 %collective-permute-start.13 = (f32[2,256,256]{2,1,0:T(8,128)S(1)}, f32[2,256,256]{2,1,0:T(8,128)S(1)}, u32[]{:S(2)}, u32[]{:S(2)}) collective-permute-start(f32[2,256,256]{2,1,0:T(8,128)S(1)} %get-tuple-element.101), channel_id=1, source_target_pairs={{0,1},{1,0},{2,3},{3,2},{4,5},{5,4},{6,7},{7,6},{8,9},{9,8},{10,11... | collective-permute-start | bytes 1572872 | tf_op jit(solution)/shard_map/ppermute | solution.py:866
  64.6 3.6 %collective-permute-start.14 = (f32[2,256,256]{2,1,0:T(8,128)S(1)}, f32[2,256,256]{2,1,0:T(8,128)S(1)}, u32[]{:S(2)}, u32[]{:S(2)}) collective-permute-start(f32[2,256,256]{2,1,0:T(8,128)S(1)} %get-tuple-element.102), channel_id=1, source_target_pairs={{0,1},{1,0},{2,3},{3,2},{4,5},{5,4},{6,7},{7,6},{8,9},{9,8},{10,11... | collective-permute-start | bytes 1572872 | tf_op jit(solution)/shard_map/ppermute | solution.py:866
  64.6 9.3 %collective-permute-start.9 = (f32[520,128]{1,0:T(8,128)S(1)}, f32[520,128]{1,0:T(8,128)S(1)}, u32[]{:S(2)}, u32[]{:S(2)}) collective-permute-start(f32[520,128]{1,0:T(8,128)S(1)} %get-tuple-element.90), channel_id=1, source_target_pairs={{0,2},{1,3},{2,0},{3,1},{4,6},{5,7},{6,4},{7,5},{8,10},{9,11},{10,... | collective-permute-start | bytes 798728 | tf_op jit(solution)/shard_map/ppermute | solution.py:841
  65.5 14.2 %collective-permute-start.15 = (f32[520,128]{1,0:T(8,128)S(1)}, f32[520,128]{1,0:T(8,128)S(1)}, u32[]{:S(2)}, u32[]{:S(2)}) collective-permute-start(f32[520,128]{1,0:T(8,128)S(1)} %get-tuple-element.107), channel_id=1, source_target_pairs={{0,4},{1,5},{2,6},{3,7},{4,0},{5,1},{6,2},{7,3},{8,12},{9,13},{10,... | collective-permute-start | bytes 798728 | tf_op jit(solution)/shard_map/ppermute | solution.py:841
  66.3 13.3 %collective-permute-start.16 = (f32[520,128]{1,0:T(8,128)S(1)}, f32[520,128]{1,0:T(8,128)S(1)}, u32[]{:S(2)}, u32[]{:S(2)}) collective-permute-start(f32[520,128]{1,0:T(8,128)S(1)} %get-tuple-element.108), channel_id=1, source_target_pairs={{0,6},{1,7},{2,4},{3,5},{4,2},{5,3},{6,0},{7,1},{8,14},{9,15},{10,... | collective-permute-start | bytes 798728 | tf_op jit(solution)/shard_map/ppermute | solution.py:841
  76.0 5.5 %collective-permute-start.17 = (f32[2,256,256]{2,1,0:T(8,128)S(1)}, f32[2,256,256]{2,1,0:T(8,128)S(1)}, u32[]{:S(2)}, u32[]{:S(2)}) collective-permute-start(f32[2,256,256]{2,1,0:T(8,128)S(1)} %get-tuple-element.111), channel_id=1, source_target_pairs={{0,1},{1,0},{2,3},{3,2},{4,5},{5,4},{6,7},{7,6},{8,9},{9,8},{10,11... | collective-permute-start | bytes 1572872 | tf_op jit(solution)/shard_map/ppermute | solution.py:866
  81.4 2.0 %collective-permute-start.18 = (f32[2,256,256]{2,1,0:T(8,128)S(1)}, f32[2,256,256]{2,1,0:T(8,128)S(1)}, u32[]{:S(2)}, u32[]{:S(2)}) collective-permute-start(f32[2,256,256]{2,1,0:T(8,128)S(1)} %get-tuple-element.112), channel_id=1, source_target_pairs={{0,1},{1,0},{2,3},{3,2},{4,5},{5,4},{6,7},{7,6},{8,9},{9,8},{10,11... | collective-permute-start | bytes 1572872 | tf_op jit(solution)/shard_map/ppermute | solution.py:866
  87.5 3.7 %collective-permute-start.19 = (f32[2,256]{1,0:T(2,128)S(1)}, f32[2,256]{1,0:T(2,128)S(1)}, u32[]{:S(2)}, u32[]{:S(2)}) collective-permute-start(f32[2,256]{1,0:T(2,128)S(1)} %get-tuple-element.119), channel_id=1, source_target_pairs={{0,8},{8,0},{16,24},{24,16},{1,9},{9,1},{17,25},{25,17},{2,10},{10... | collective-permute-start | bytes 6152 | tf_op jit(solution)/shard_map/ppermute | solution.py:733
  91.2 4.5 %collective-permute-start.20 = (f32[2,256]{1,0:T(2,128)S(1)}, f32[2,256]{1,0:T(2,128)S(1)}, u32[]{:S(2)}, u32[]{:S(2)}) collective-permute-start(f32[2,256]{1,0:T(2,128)S(1)} %add.6), channel_id=1, source_target_pairs={{0,16},{8,24},{16,0},{24,8},{1,17},{9,25},{17,1},{25,9},{2,18},{10... | collective-permute-start | bytes 6152 | tf_op jit(solution)/shard_map/ppermute | solution.py:733

commit v2 on v1

--- a/solution.py
+++ b/solution.py
@@ -502,47 +502,72 @@
     far_ref[...] = pair[1 - chip % 2]
 
 
-def power_kernel(index_ref, high_ref, low_ref, edge_ref, _, power_high, power_low, chip_high, chip_low, *, groups, group):
+def unit_rows(group):
+    rows = lax.broadcasted_iota(jnp.int32, (group, 2 * group), 0)
+    columns = lax.broadcasted_iota(jnp.int32, (group, 2 * group), 1)
+    return (rows == columns).astype(f32)
+
+
+def store_turned(high_ref, low_ref, index, turned):
+    group = turned.shape[0]
+    store_left(high_ref, low_ref, index, turned[:, :group].T, turned[:, group:].T)
+
+
+def power_kernel(index_ref, high_ref, low_ref, edge_ref, _, power_high, power_low, turned_ref, chip_high, chip_low,
+                 *, groups, group):
+    tables = (high_ref, low_ref, edge_ref)
     last = high_ref.shape[0] - 1
     couple = (high_ref[last], low_ref[last])
-    rows = lax.broadcasted_iota(jnp.int32, (2 * group, group), 0)
-    columns = lax.broadcasted_iota(jnp.int32, (2 * group, group), 1)
-    values = [None] * groups + [(rows == columns).astype(f32)]
-    split = [None] * groups
+    values = [None] * groups + [unit_rows(group)]
     for k in reversed(range(groups)):
-        values[k] = product(couple, halves(values[k + 1]))
-        split[k] = halves(values[k])
-        store_left(power_high, power_low, k, values[k][:group], values[k][group:])
+        values[k] = product(halves(values[k + 1]), couple)
+        store_turned(power_high, power_low, k, values[k])
+        turned_ref[k] = values[k]
+    split = [halves(value) for value in values]
     for q in range(chip_high.shape[0]):
 
         def store(k, done, q=q):
             if k == 0:
-                store_left(chip_high, chip_low, q, done[:group], done[group:])
-
-        linear_part(q + 1, groups, group, index_ref, (high_ref, low_ref, edge_ref), values, split, store)
-
-
-def own_map_kernel(place_ref, index_ref, high_ref, low_ref, edge_ref, power_high, power_low, _, map_high, map_low,
-                   *, groups, group):
-    rows = lax.broadcasted_iota(jnp.int32, (2 * group, group), 0)
-    columns = lax.broadcasted_iota(jnp.int32, (2 * group, group), 1)
-    split = [(power_high[k, :, 0:group], power_low[k, :, 0:group]) for k in range(groups)]
-    values = [high.astype(f32) + low.astype(f32) for high, low in split]
-    values.append((rows == columns).astype(f32))
+                store_turned(chip_high, chip_low, q, done)
+
+        linear_part(q + 1, groups, group, index_ref, tables, values, split, store)
+
+
+def own_map_kernel(place_ref, index_ref, high_ref, low_ref, edge_ref, turned_ref, _, map_high, map_low, *, groups, group):
+    values = [turned_ref[k] for k in range(groups)] + [unit_rows(group)]
+    split = [halves(value) for value in values]
 
     def store(k, done):
-        store_left(map_high, map_low, k, done[:group], done[group:])
+        store_turned(map_high, map_low, k, done)
 
     linear_part(place_ref[0] // 2, groups, group, index_ref, (high_ref, low_ref, edge_ref), values, split, store)
 
 
 def linear_part(chip, groups, group, index_ref, tables, values, split, store):
-    open_state, step = second_groups(chip, groups, index_ref, tables)
-    state = halves(open_state(*last_row(values[groups - 1], group)))
+    high_ref, low_ref, edge_ref = tables
+    last = high_ref.shape[0] - 1
+    couple = (high_ref[last], low_ref[last])
+    base, total = chip * groups, index_ref.shape[1]
+
+    def edge(level, side, column_re, column_im):
+        rows = [edge_ref[level, 2 * side + part : 2 * side + part + 1, :] for part in range(2)]
+        return column_re * rows[0] + column_im * rows[1]
+
+    def first_column(value):
+        return value[:, 0:1], value[:, group : group + 1]
+
+    def last_column(value):
+        return value[:, group - 1 : group], value[:, 2 * group - 1 : 2 * group]
+
+    after = base + groups
+    inside = jnp.where(after < total, 1.0, 0.0)
+    done = edge(index_ref[1, jnp.minimum(after, total - 1)], 0, *last_column(values[groups - 1])) * inside
     for k in reversed(range(groups)):
-        before = last_row(values[k - 1], group) if k else None
-        done = step(k, split[k], state, before, first_row(values[k + 1], group))
-        state = halves(done)
+        level = index_ref[1, base + k]
+        done = product(split[k], (high_ref[level], low_ref[level])) + product(halves(done), couple)
+        if k:
+            done = done + edge(level, 0, *last_column(values[k - 1]))
+        done = done + edge(level, 1, *first_column(values[k + 1]))
         store(k, done)
 
 
@@ -577,9 +602,11 @@
 
 
 def close_sweep_kernel(place_ref, index_ref, edge_ref, power_high, power_low, map_high, map_low, local_ref, base_ref,
-                       near_ref, far_ref, _, own_ref, other_ref, image_ref, pair, result, *, groups, group, part_of, second_pair):
+                       near_ref, far_ref, _, out_ref, *refs, groups, group, part_of, second_pair):
+    image_ref, pair = refs if len(refs) == 2 else (None, refs[0])
     device = place_ref[0]
     chip, core = device // 2, device % 2
+    side = core if image_ref is not None else 1 - core
     pair[chip % 2] = near_ref[...]
     pair[1 - chip % 2] = far_ref[...]
 
@@ -589,19 +616,20 @@
     first = halves(carried(0, 2 * group))
     second = halves(carried(2 * group, 2 * group))
     half = groups // 2
-    for k in reversed(range(groups)):
+    for i in reversed(range(half)):
+        k = side * half + i
         done = local_ref[k] + (
             product((map_high[k], map_low[k]), first) + product((power_high[k], power_low[k]), second)
         )
-        if k == 0:
+        if i == 0:
             level = index_ref[1, chip * groups]
-            base = 4 * group
-            done = add_edge(done, edge_ref, level, 0, carried(base, 8)[0:1], carried(base, 8)[1:2])
-        rows = slice((k % half) * group, (k % half + 1) * group)
-        result[k // half, 0, rows, :] = done[:group]
-        result[k // half, 1, rows, :] = done[group:]
-    own_ref[...] = result[core]
-    other_ref[...] = result[1 - core]
+            inside = jnp.where(side == 0, 1.0, 0.0)
+            rows = carried(4 * group, 8) * inside
+            done = add_edge(done, edge_ref, level, 0, rows[0:1], rows[1:2])
+        out_ref[0, i * group : (i + 1) * group, :] = done[:group]
+        out_ref[1, i * group : (i + 1) * group, :] = done[group:]
+    if image_ref is None:
+        return
     image_ref[...] = jnp.zeros_like(image_ref)
 
     @pl.when((chip // 2 == part_of) & ((chip % 2) ^ (chip // 2) == second_pair))
@@ -624,26 +652,32 @@
 def last_pass_kernel(place_ref, index_ref, high_ref, low_ref, edge_ref, *refs, half, step, group):
     owns, comes = refs[0:2], refs[2:4]
     if half:
-        out_ref, state_ref, column_ref, image_ref, field, result, sems = refs[4:]
+        out_ref, state_ref, column_ref, image_ref, result, sems = refs[4:]
     else:
-        carry_ref, beside_ref, _, *images = refs[4:-5]
-        out_ref, image_ref, field, result, sems = refs[-5:]
+        carry_ref, beside_ref, *images = refs[4:-2]
+        result, image_ref = refs[-2:]
     device = place_ref[0]
     chip, core = device // 2, device % 2
     block = owns[0].shape[-1]
-    width = field.shape[-1]
-    count = width // group
+    count = 4 * block // group
     low = half * count
-    for second_pair in range(2):
-        for ref, side in ((owns[second_pair], core), (comes[second_pair], 1 - core)):
-            start = pl.multiple_of(((chip // 2 ^ second_pair) * 2 + side) * block, block)
-            for part in range(2):
-                field[part, :, pl.ds(start, block)] = ref[part]
     first = count + 1 if half else 0
     copies = []
 
+    ready = {}
+
     def read(k):
-        return [field[part, :, (k - low) * group : (k - low + 1) * group] for part in range(2)]
+        if k not in ready:
+            q, inner = (k - low) * group // block, (k - low) * group % block
+            columns = slice(inner, inner + group)
+            ready[k] = [
+                jnp.where(chip // 2 == q // 2, *(
+                    jnp.where(core == q % 2, owns[item][part, :, columns], comes[item][part, :, columns])
+                    for item in range(2)
+                ))
+                for part in range(2)
+            ]
+        return ready[k]
 
     def write(k, solved):
         if half and k == low:
@@ -652,6 +686,8 @@
         where = k - first
         result[where, 0] = solved[:, :group]
         result[where, 1] = solved[:, group:]
+        if not half:
+            return
         copy = pltpu.make_async_copy(
             result.at[where], out_ref.at[0, :, :, k * group : (k + 1) * group], sems.at[where]
         )
@@ -697,34 +733,52 @@
     count = width // group
     block = owns[0].shape[-1]
     args = [place, recv_index, *tables, *owns, *comes]
-    any_space = pl.BlockSpec(memory_space=pl.ANY)
     specs = [smem()] * 2 + [vmem()] * 7
-    outs = [whole(shape)]
-    out_specs = [any_space]
-    aliases = {}
-    results = count - 1 if half else count + 1
+    results = whole((count - 1 if half else count + 1, 2, rows, group))
+    scratch = []
     if half:
-        outs += [whole((rows, 2 * group)), whole((2, rows, group))]
-        out_specs += [vmem()] * 2
+        outs = [whole(shape), whole((rows, 2 * group)), whole((2, rows, group))]
+        out_specs = [anywhere(), vmem(), vmem()]
+        scratch = [pltpu.VMEM(results.shape, f32), pltpu.SemaphoreType.DMA((count - 1,))]
     else:
-        migrated, state, column, *images = passed
-        args += [state, column, migrated, *images]
-        specs += [vmem(), vmem(), any_space] + [vmem()] * len(images)
-        aliases = {len(args) - 1 - len(images): 0}
+        args += passed
+        specs += [vmem()] * len(passed)
+        outs = [results]
+        out_specs = [vmem()]
     return pl.pallas_call(
         functools.partial(last_pass_kernel, half=half, step=step, group=group),
         out_shape=outs + [whole((1 if half else 2, block))],
         in_specs=specs,
         out_specs=out_specs + [vmem()],
-        scratch_shapes=[
-            pltpu.VMEM((2, rows, width), f32),
-            pltpu.VMEM((results, 2, rows, group), f32),
-            pltpu.SemaphoreType.DMA((results,)),
-        ],
-        input_output_aliases=aliases,
+        scratch_shapes=scratch,
         compiler_params=params(24),
         cost_estimate=cost(rows * width * group * 24, 8 * rows * width * 2),
     )(*args)
+
+
+def store_kernel(groups_ref, _, out_ref, sems):
+    group = groups_ref.shape[-1]
+    copies = [
+        pltpu.make_async_copy(groups_ref.at[k], out_ref.at[0, :, :, k * group : (k + 1) * group], sems.at[k])
+        for k in range(groups_ref.shape[0])
+    ]
+    for copy in copies:
+        copy.start()
+    for copy in copies:
+        copy.wait()
+
+
+def store_groups(pieces, migrated):
+    return pl.pallas_call(
+        store_kernel,
+        out_shape=whole(migrated.shape),
+        in_specs=[anywhere(), anywhere()],
+        out_specs=anywhere(),
+        scratch_shapes=[pltpu.SemaphoreType.DMA((pieces.shape[0],))],
+        input_output_aliases={1: 0},
+        cost_estimate=cost(0, 8 * 1024 * 1024),
+        compiler_params=params(4),
+    )(pieces, migrated)
 
 
 def sum_over(value, axis, count):
@@ -765,12 +819,12 @@
         powers.extend(
             pl.pallas_call(
                 functools.partial(power_kernel, groups=groups, group=group),
-                out_shape=[matrices] * 2 + [middle] * 2,
+                out_shape=[matrices] * 2 + [whole((groups, group, double))] + [middle] * 2,
                 in_specs=[smem()] + [vmem()] * 3 + [anywhere()],
-                out_specs=[vmem()] * 4,
+                out_specs=[vmem()] * 5,
                 compiler_params=params(20),
                 cost_estimate=cost(groups * group * group * group * 64, 4 * 1024 * 1024),
-            )(shot_index, *left, ready)
+            )(shot_index, *right, ready)
         )
         return powers[0]
 
@@ -813,7 +867,7 @@
     after = open_sweep(0, 1, after)
     after = open_sweep(0, 0, after)
     after = make_powers(after)
-    power_high, power_low, chip_high, chip_low = powers
+    power_high, power_low, power_turned, chip_high, chip_low = powers
     came = {}
     for half in (1, 0):
         carries = pl.pallas_call(
@@ -830,11 +884,11 @@
             map_high, map_low = pl.pallas_call(
                 functools.partial(own_map_kernel, groups=groups, group=group),
                 out_shape=[matrices] * 2,
-                in_specs=[smem()] * 2 + [vmem()] * 5 + [anywhere()],
+                in_specs=[smem()] * 2 + [vmem()] * 4 + [anywhere()],
                 out_specs=[vmem()] * 2,
                 compiler_params=params(20),
                 cost_estimate=cost(groups * group * group * group * 32, 4 * 1024 * 1024),
-            )(place, shot_index, *left, power_high, power_low, after)
+            )(place, shot_index, *right, power_turned, after)
             after = map_high
         for offset in (3, 1, 2, 0):
             moves = [(d, d ^ (2 * offset)) for d in range(devices)]
@@ -847,30 +901,34 @@
         owns, comes = [], []
         for second_pair in (0, 1):
             name = "%d_%d" % (half, second_pair)
-            own, other, image = pl.pallas_call(
-                functools.partial(
-                    close_sweep_kernel, groups=groups, group=group, part_of=half, second_pair=second_pair
-                ),
-                out_shape=[part, part, whole((1, block))],
-                in_specs=[smem()] * 2 + [vmem()] * 9 + [anywhere()],
-                out_specs=[vmem()] * 3,
-                scratch_shapes=[pltpu.VMEM((2,) + piece.shape, f32), pltpu.VMEM((2, 2, rows, block), f32)],
-                compiler_params=params(20),
-                cost_estimate=cost(groups * group * block * group * 24, 8 * groups * group * block * 2),
-            )(
-                place, shot_index, left[2], power_high, power_low, map_high, map_low, locals_[name], bases[name],
-                came[half, 2 * second_pair], came[half, 2 * second_pair + 1], after,
-            )
-            after = image
-            owns.append(own)
-            comes.append(lax.ppermute(other, "plane", partner))
-            images.append(image)
+            for kind in ("far", "near"):
+                outs = [part] + ([whole((1, block))] if kind == "near" else [])
+                result = pl.pallas_call(
+                    functools.partial(
+                        close_sweep_kernel, groups=groups, group=group, part_of=half, second_pair=second_pair
+                    ),
+                    out_shape=outs,
+                    in_specs=[smem()] * 2 + [vmem()] * 9 + [anywhere()],
+                    out_specs=[vmem()] * len(outs),
+                    scratch_shapes=[pltpu.VMEM((2,) + piece.shape, f32)],
+                    compiler_params=params(20),
+                    cost_estimate=cost(groups * group * block * group * 12, 4 * groups * group * block * 2),
+                )(
+                    place, shot_index, left[2], power_high, power_low, map_high, map_low, locals_[name], bases[name],
+                    came[half, 2 * second_pair], came[half, 2 * second_pair + 1], after,
+                )
+                after = result[-1]
+                if kind == "far":
+                    comes.append(lax.ppermute(result[0], "plane", partner))
+            owns.append(result[0])
+            images.append(result[1])
         if not half:
-            passed = [*passed, image_last, *images]
+            migrated, *passed = *passed, image_last, *images
         *passed, image_last = last_pass(place, recv_index, right, owns, comes, half, passed, wavefield.shape, 1, group)
         after = image_last
+    migrated = store_groups(passed[0], migrated)
     image_last = sum_over(image_last, "freq", freqs)
-    return passed[0], image_last
+    return migrated, image_last
 
 
 def solution(mesh):

time: 96.4 us -> 95.4 us (0.990)
  waiting for transfers between devices: 21.9 us -> 17.5 us
  Pallas kernels: 48.3 us -> 50.4 us
  starting transfers between devices: 24.3 us -> 25.6 us
    ppermute x6, waiting for transfers between devices: 13 us -> 10.2 us  [fast_shards(): lax.ppermute(carries[offset], 'plane', moves)]
    pallas_call x4 -> x8, Pallas kernels: 7.48 us -> 9.93 us  [fast_shards(): pl.pallas_call(functools.partial(close_sweep_kernel, groups=groups, group...]
    ppermute x2, waiting for transfers between devices: 3.91 us -> 2.41 us  [sum_over(): lax.ppermute(value, axis, [(i, i ^ reach) for i in range(count)])]
    pallas_call x0 -> x1, Pallas kernels: none -> 1.47 us  [store_groups(): pl.pallas_call(store_kernel, out_shape=whole(migrated.shape), in_specs=[a...]
    pallas_call x1, Pallas kernels: 3.81 us -> 2.7 us  [make_powers(): pl.pallas_call(functools.partial(power_kernel, groups=groups, group=group...]
  transfers between devices with their start and end apart: 21 -> 21, of which waited for: 9 -> 10; matrix products, arithmetic and copies ran while one was open for 0% -> 0% of each run, Pallas kernels for 33% -> 34%
where the time goes in v2:
time: 95.4 us; the launch traced here: 95.3 us
  Pallas kernels  50.4 us (53%)
  starting transfers between devices  25.6 us (27%)
  waiting for transfers between devices  17.5 us (18%)
    pallas_call x4, Pallas kernels, open_sweep(): pl.pallas_call(functools.partial(open_sweep_kernel, groups=groups, group=...  12.4 us
    ppermute x6, waiting for transfers between devices, fast_shards(): lax.ppermute(carries[offset], 'plane', moves)  10.2 us
    pallas_call x8, Pallas kernels, fast_shards(): pl.pallas_call(functools.partial(close_sweep_kernel, groups=groups, group...  9.93 us
    ppermute x6, starting transfers between devices, fast_shards(): lax.ppermute(carries[offset], 'plane', moves)  7.53 us
    pallas_call x2, Pallas kernels, first_pass(): pl.pallas_call(functools.partial(first_pass_kernel, half=half, group=grou...  7.39 us
    pallas_call x2, Pallas kernels, last_pass(): pl.pallas_call(functools.partial(last_pass_kernel, half=half, step=step,...  7.32 us
    ppermute x6, starting transfers between devices, open_sweep(): lax.ppermute(item, 'plane', moves)  7.2 us
    ppermute x2, starting transfers between devices, first(): come[half] = lax.ppermute(send, 'plane', partner)  4.82 us
  transfers between devices with their start and end apart: 21, of which 10 were waited for; matrix products, arithmetic and copies ran while one was open for 0% of the time, Pallas kernels for 34%

profile of v2, /device:TPU:0, one launch (start us, length us, event | category | flops | bytes accessed | tf_op | source)
XLA Modules:
  0.0 95.3 jit_solution(956444061541803916)
XLA Ops:
  0.7 1.6 %shard_map.79 = f32[1,2,1,2048]{3,2,1,0:T(1,128)} custom-call(s32[1]{0:T(128)} %bitcast.place_ref, f32[1,2,256,2048]{3,2,1,0:T(8,128)} %beside_ref.3), custom_call_target="tpu_custom_call" | custom-call | flops 20000000000 | bytes 1048576 | tf_op jit(solution)/shard_map/pallas_call | solution.py:285
  3.1 1.9 %shard_map.77 = (bf16[9,256,256]{2,1,0:T(8,128)(2,1)S(1)}, bf16[9,256,256]{2,1,0:T(8,128)(2,1)S(1)}, f32[8,4,256]{2,1,0:T(4,128)S(1)}) custom-call(f32[1,8,2]{2,1,0:T(8,128)S(1)} %copy.9.rhs_ref, f32[8,2,128,128]{3,2,1,0:T(8,128)S(1)} %bitcast.3, f32[2,128,128]{2,1,0:T(8,128)S(1)} %bitcast.5), custom_call_target="tpu_custom_call" | custom-call | flops 20000000000 | bytes 4194304 | tf_op jit(solution)/shard_map/pallas_call | solution.py:262
  5.3 3.6 %shard_map.80 = (f32[264,256]{1,0:T(8,128)S(1)}, f32[2,2,264,256]{3,2,1,0:T(8,128)S(1)}, f32[2,2,264,256]{3,2,1,0:T(8,128)S(1)}) custom-call(s32[1]{0:T(128)} %bitcast.place_ref, s32[2,16]{1,0:T(2,128)S(1)} %copy-done.2, f32[1,2,256,2048]{3,2,1,0:T(8,128)S(1)} %copy-done, f32[1,2,256,2048]{3,2,1,0:T(8,128)S(1)} %copy-done, ...), custom_call_target="tpu_custom_call" | custom-call | flops 1660944384 | bytes 4325376 | tf_op jit(solution)/shard_map/pallas_call | solution.py:383
  8.9 4.4 %collective-permute-start.1 = (f32[2,2,264,256]{3,2,1,0:T(8,128)S(1)}, f32[2,2,264,256]{3,2,1,0:T(8,128)S(1)}, u32[]{:S(2)}, u32[]{:S(2)}) collective-permute-start(f32[2,2,264,256]{3,2,1,0:T(8,128)S(1)} %get-tuple-element.66), channel_id=1, source_target_pairs={{0,1},{1,0},{2,3},{3,2},{4,5},{5,4},{6,7},{7,6},{8,9},{9,8},{10,11... | collective-permute-start | bytes 3244040 | tf_op jit(solution)/shard_map/ppermute | solution.py:837
  13.3 1.9 %shard_map.78 = (bf16[9,256,256]{2,1,0:T(8,128)(2,1)S(1)}, bf16[9,256,256]{2,1,0:T(8,128)(2,1)S(1)}, f32[8,2,256,128]{3,2,1,0:T(8,128)S(1)}) custom-call(f32[1,8,2]{2,1,0:T(8,128)S(1)} %copy.9.rhs_ref, f32[8,2,128,128]{3,2,1,0:T(8,128)S(1)} %bitcast.4, f32[2,128,128]{2,1,0:T(8,128)S(1)} %bitcast.6), custom_call_target="tpu_custom_call" | custom-call | flops 20000000000 | bytes 4194304 | tf_op jit(solution)/shard_map/pallas_call | solution.py:262
  15.6 3.1 %shard_map.81 = (f32[520,128]{1,0:T(8,128)S(1)}, f32[520,128]{1,0:T(8,128)S(1)}, f32[4,256,256]{2,1,0:T(8,128)S(1)}, f32[2,2,128,128]{3,2,1,0:T(8,128)S(1)}) custom-call(s32[1]{0:T(128)} %bitcast.place_ref, s32[2,16]{1,0:T(2,128)S(1)} %copy-done.1, bf16[9,256,256]{2,1,0:T(8,128)(2,1)S(1)} %get-tuple-element.62.high_ref, ...), custom_call_target="tpu_custom_call" | custom-call | flops 1610612736 | bytes 3145728 | tf_op jit(solution)/shard_map/pallas_call | solution.py:851
  18.7 3.8 %shard_map.82 = (f32[2,2,264,256]{3,2,1,0:T(8,128)S(1)}, f32[2,2,264,256]{3,2,1,0:T(8,128)S(1)}) custom-call(s32[1]{0:T(128)} %bitcast.place_ref, s32[2,16]{1,0:T(2,128)S(1)} %copy-done.2, f32[1,2,256,2048]{3,2,1,0:T(8,128)S(1)} %copy-done, f32[1,2,256,2048]{3,2,1,0:T(8,128)S(1)} %copy-done, f32[1,2,1,2048]{3,2,1,0:T(1,128)S(1)} %collective-permute-done.halo_ref, ...), custom_call_target="tpu_custom_call" | custom-call | flops 1660944384 | bytes 4325376 | tf_op jit(solution)/shard_map/pallas_call | solution.py:383
  22.9 2.0 %collective-permute-start.4 = (f32[520,128]{1,0:T(8,128)S(1)}, f32[520,128]{1,0:T(8,128)S(1)}, u32[]{:S(2)}, u32[]{:S(2)}) collective-permute-start(f32[520,128]{1,0:T(8,128)S(1)} %get-tuple-element.67.refs_1_), channel_id=1, source_target_pairs={{0,4},{1,5},{2,6},{3,7},{4,0},{5,1},{6,2},{7,3},{8,12},{9,13},{10,... | collective-permute-start | bytes 798728 | tf_op jit(solution)/shard_map/ppermute | solution.py:860
  24.9 1.3 %collective-permute-start.5 = (f32[520,128]{1,0:T(8,128)S(1)}, f32[520,128]{1,0:T(8,128)S(1)}, u32[]{:S(2)}, u32[]{:S(2)}) collective-permute-start(f32[520,128]{1,0:T(8,128)S(1)} %get-tuple-element.79), channel_id=1, source_target_pairs={{0,6},{1,7},{2,4},{3,5},{4,2},{5,3},{6,0},{7,1},{8,14},{9,15},{10,... | collective-permute-start | bytes 798728 | tf_op jit(solution)/shard_map/ppermute | solution.py:860
  26.2 3.2 %shard_map.83 = (f32[520,128]{1,0:T(8,128)S(1)}, f32[520,128]{1,0:T(8,128)S(1)}, f32[4,256,256]{2,1,0:T(8,128)S(1)}, f32[2,2,128,128]{3,2,1,0:T(8,128)S(1)}) custom-call(s32[1]{0:T(128)} %bitcast.place_ref, s32[2,16]{1,0:T(2,128)S(1)} %copy-done.1, bf16[9,256,256]{2,1,0:T(8,128)(2,1)S(1)} %get-tuple-element.62.high_ref, ...), custom_call_target="tpu_custom_call" | custom-call | flops 1610612736 | bytes 3145728 | tf_op jit(solution)/shard_map/pallas_call | solution.py:851
  29.7 3.0 %shard_map.84 = (f32[520,128]{1,0:T(8,128)S(1)}, f32[520,128]{1,0:T(8,128)S(1)}, f32[4,256,256]{2,1,0:T(8,128)S(1)}, f32[2,2,128,128]{3,2,1,0:T(8,128)S(1)}) custom-call(s32[1]{0:T(128)} %bitcast.place_ref, s32[2,16]{1,0:T(2,128)S(1)} %copy-done.1, bf16[9,256,256]{2,1,0:T(8,128)(2,1)S(1)} %get-tuple-element.62.high_ref, ...), custom_call_target="tpu_custom_call" | custom-call | flops 1610612736 | bytes 3145728 | tf_op jit(solution)/shard_map/pallas_call | solution.py:851
  32.7 3.0 %shard_map.85 = (f32[520,128]{1,0:T(8,128)S(1)}, f32[520,128]{1,0:T(8,128)S(1)}, f32[4,256,256]{2,1,0:T(8,128)S(1)}, f32[2,2,128,128]{3,2,1,0:T(8,128)S(1)}) custom-call(s32[1]{0:T(128)} %bitcast.place_ref, s32[2,16]{1,0:T(2,128)S(1)} %copy-done.1, bf16[9,256,256]{2,1,0:T(8,128)(2,1)S(1)} %get-tuple-element.62.high_ref, ...), custom_call_target="tpu_custom_call" | custom-call | flops 1610612736 | bytes 3145728 | tf_op jit(solution)/shard_map/pallas_call | solution.py:851
  35.8 1.9 %collective-permute-start.6 = (f32[520,128]{1,0:T(8,128)S(1)}, f32[520,128]{1,0:T(8,128)S(1)}, u32[]{:S(2)}, u32[]{:S(2)}) collective-permute-start(f32[520,128]{1,0:T(8,128)S(1)} %get-tuple-element.85), channel_id=1, source_target_pairs={{0,2},{1,3},{2,0},{3,1},{4,6},{5,7},{6,4},{7,5},{8,10},{9,11},{10,... | collective-permute-start | bytes 798728 | tf_op jit(solution)/shard_map/ppermute | solution.py:860
  38.6 2.7 %shard_map.86 = (bf16[4,256,256]{2,1,0:T(8,128)(2,1)S(1)}, bf16[4,256,256]{2,1,0:T(8,128)(2,1)S(1)}, f32[4,128,256]{2,1,0:T(8,128)S(1)}, bf16[2,256,256]{2,1,0:T(8,128)(2,1)S(1)}, bf16[2,256,256]{2,1,0:T(8,128)(2,1)S(1)}) custom-call(s32[2,16]{1,0:T(2,128)S(1)} %copy-done.1, bf16[9,256,256]{2,1,0:T(8,128)(2,1)S(1)} %get-tuple-element.58.high_ref, ...), custom_call_target="tpu_custom_call" | custom-call | flops 1073741824 | bytes 4194304 | tf_op jit(solution)/shard_map/pallas_call | solution.py:820
  43.2 1.9 %collective-permute-start.10 = (f32[520,128]{1,0:T(8,128)S(1)}, f32[520,128]{1,0:T(8,128)S(1)}, u32[]{:S(2)}, u32[]{:S(2)}) collective-permute-start(f32[520,128]{1,0:T(8,128)S(1)} %get-tuple-element.91), channel_id=1, source_target_pairs={{0,2},{1,3},{2,0},{3,1},{4,6},{5,7},{6,4},{7,5},{8,10},{9,11},{10,... | collective-permute-start | bytes 798728 | tf_op jit(solution)/shard_map/ppermute | solution.py:895
  46.0 1.3 %collective-permute-start.12 = (f32[520,128]{1,0:T(8,128)S(1)}, f32[520,128]{1,0:T(8,128)S(1)}, u32[]{:S(2)}, u32[]{:S(2)}) collective-permute-start(f32[520,128]{1,0:T(8,128)S(1)} %get-tuple-element.96), channel_id=1, source_target_pairs={{0,6},{1,7},{2,4},{3,5},{4,2},{5,3},{6,0},{7,1},{8,14},{9,15},{10,... | collective-permute-start | bytes 798728 | tf_op jit(solution)/shard_map/ppermute | solution.py:895
  47.3 1.6 %shard_map.88 = (bf16[4,256,256]{2,1,0:T(8,128)(2,1)S(1)}, bf16[4,256,256]{2,1,0:T(8,128)(2,1)S(1)}) custom-call(s32[1]{0:T(128)} %bitcast.place_ref, s32[2,16]{1,0:T(2,128)S(1)} %copy-done.1, bf16[9,256,256]{2,1,0:T(8,128)(2,1)S(1)} %get-tuple-element.58.high_ref, bf16[9,256,256]{2,1,0:T(8,128)(2,1)S(1)} %get-tuple-element.59.low_ref, ...), custom_call_target="tpu_custom_call" | custom-call | flops 536870912 | bytes 4194304 | tf_op jit(solution)/shard_map/pallas_call | solution.py:884
  48.9 3.4 %collective-permute-done.8.refs_3_ = f32[520,128]{1,0:T(8,128)S(1)} collective-permute-done((f32[520,128]{1,0:T(8,128)S(1)}, f32[520,128]{1,0:T(8,128)S(1)}, u32[]{:S(2)}, u32[]{:S(2)}) %collective-permute-start.8) | collective-permute-done | bytes 266272 | tf_op jit(solution)/shard_map/ppermute | solution.py:860
  53.4 3.5 %collective-permute-done.10.far_ref = f32[520,128]{1,0:T(8,128)S(1)} collective-permute-done((f32[520,128]{1,0:T(8,128)S(1)}, f32[520,128]{1,0:T(8,128)S(1)}, u32[]{:S(2)}, u32[]{:S(2)}) %collective-permute-start.10) | collective-permute-done | bytes 266272 | tf_op jit(solution)/shard_map/ppermute | solution.py:895
  56.9 1.2 %shard_map.90._ = f32[2,256,256]{2,1,0:T(8,128)S(1)} custom-call(s32[1]{0:T(128)} %bitcast.place_ref, s32[2,16]{1,0:T(2,128)S(1)} %copy-done.1, f32[8,2,256,128]{3,2,1,0:T(8,128)S(1)} %get-tuple-element.61.edge_ref, bf16[4,256,256]{2,1,0:T(8,128)(2,1)S(1)} %get-tuple-element.73.power_high.refs_4_, bf16[4,256,256]{2,1,0:T(8,128)(2,1)S(1)} %get-tuple-element.74.power_low, ...), custom_call_target="tpu_custom_call" | custom-call | flops 402653184 | bytes 1048576 | tf_op jit(solution)/shard_map/pallas_call | solution.py:906
  58.1 1.2 %shard_map.91 = (f32[2,256,256]{2,1,0:T(8,128)S(1)}, f32[1,256]{1,0:T(1,128)S(1)}) custom-call(s32[1]{0:T(128)} %bitcast.place_ref, s32[2,16]{1,0:T(2,128)S(1)} %copy-done.1, f32[8,2,256,128]{3,2,1,0:T(8,128)S(1)} %get-tuple-element.61.edge_ref, bf16[4,256,256]{2,1,0:T(8,128)(2,1)S(1)} %get-tuple-element.73.power_high.refs_4_, ...), custom_call_target="tpu_custom_call" | custom-call | flops 402653184 | bytes 1048576 | tf_op jit(solution)/shard_map/pallas_call | solution.py:906
  59.3 3.5 %collective-permute-done.12.far_ref = f32[520,128]{1,0:T(8,128)S(1)} collective-permute-done((f32[520,128]{1,0:T(8,128)S(1)}, f32[520,128]{1,0:T(8,128)S(1)}, u32[]{:S(2)}, u32[]{:S(2)}) %collective-permute-start.12) | collective-permute-done | bytes 266272 | tf_op jit(solution)/shard_map/ppermute | solution.py:895
  66.3 1.8 %collective-permute-start.16 = (f32[520,128]{1,0:T(8,128)S(1)}, f32[520,128]{1,0:T(8,128)S(1)}, u32[]{:S(2)}, u32[]{:S(2)}) collective-permute-start(f32[520,128]{1,0:T(8,128)S(1)} %get-tuple-element.104), channel_id=1, source_target_pairs={{0,6},{1,7},{2,4},{3,5},{4,2},{5,3},{6,0},{7,1},{8,14},{9,15},{10,... | collective-permute-start | bytes 798728 | tf_op jit(solution)/shard_map/ppermute | solution.py:895
  68.1 1.4 %shard_map.93 = (f32[2,256,256]{2,1,0:T(8,128)S(1)}, f32[1,256]{1,0:T(1,128)S(1)}) custom-call(s32[1]{0:T(128)} %bitcast.place_ref, s32[2,16]{1,0:T(2,128)S(1)} %copy-done.1, f32[8,2,256,128]{3,2,1,0:T(8,128)S(1)} %get-tuple-element.61.edge_ref, bf16[4,256,256]{2,1,0:T(8,128)(2,1)S(1)} %get-tuple-element.73.power_high.refs_4_, ...), custom_call_target="tpu_custom_call" | custom-call | flops 402653184 | bytes 1048576 | tf_op jit(solution)/shard_map/pallas_call | solution.py:906
  69.5 3.8 %shard_map.94 = (f32[1,2,256,2048]{3,2,1,0:T(8,128)}, f32[256,256]{1,0:T(8,128)S(1)}, f32[2,256,128]{2,1,0:T(8,128)S(1)}, f32[1,256]{1,0:T(1,128)S(1)}) custom-call(s32[1]{0:T(128)} %bitcast.place_ref, s32[2,16]{1,0:T(2,128)S(1)} %copy-done.2, bf16[9,256,256]{2,1,0:T(8,128)(2,1)S(1)} %get-tuple-element.58.high_ref, ...), custom_call_target="tpu_custom_call" | custom-call | flops 1610612736 | bytes 4194304 | tf_op jit(solution)/shard_map/pallas_call | solution.py:748
  75.0 1.4 %shard_map.96 = (f32[2,256,256]{2,1,0:T(8,128)S(1)}, f32[1,256]{1,0:T(1,128)S(1)}) custom-call(s32[1]{0:T(128)} %bitcast.place_ref, s32[2,16]{1,0:T(2,128)S(1)} %copy-done.1, f32[8,2,256,128]{3,2,1,0:T(8,128)S(1)} %get-tuple-element.61.edge_ref, bf16[4,256,256]{2,1,0:T(8,128)(2,1)S(1)} %get-tuple-element.73.power_high.refs_4_, ...), custom_call_target="tpu_custom_call" | custom-call | flops 402653184 | bytes 1048576 | tf_op jit(solution)/shard_map/pallas_call | solution.py:906
  76.5 2.6 %collective-permute-done.15.near_ref = f32[520,128]{1,0:T(8,128)S(1)} collective-permute-done((f32[520,128]{1,0:T(8,128)S(1)}, f32[520,128]{1,0:T(8,128)S(1)}, u32[]{:S(2)}, u32[]{:S(2)}) %collective-permute-start.15) | collective-permute-done | bytes 266272 | tf_op jit(solution)/shard_map/ppermute | solution.py:895
  83.0 3.5 %shard_map.99 = (f32[9,2,256,128]{3,2,1,0:T(8,128)S(1)}, f32[2,256]{1,0:T(2,128)S(1)}) custom-call(s32[1]{0:T(128)} %bitcast.place_ref, s32[2,16]{1,0:T(2,128)S(1)} %copy-done.2, bf16[9,256,256]{2,1,0:T(8,128)(2,1)S(1)} %get-tuple-element.58.high_ref, bf16[9,256,256]{2,1,0:T(8,128)(2,1)S(1)} %get-tuple-element.59.low_ref, ...), custom_call_target="tpu_custom_call" | custom-call | flops 1610612736 | bytes 4194304 | tf_op jit(solution)/shard_map/pallas_call | solution.py:748
  86.6 1.6 %collective-permute-start.19 = (f32[2,256]{1,0:T(2,128)S(1)}, f32[2,256]{1,0:T(2,128)S(1)}, u32[]{:S(2)}, u32[]{:S(2)}) collective-permute-start(f32[2,256]{1,0:T(2,128)S(1)} %get-tuple-element.113), channel_id=1, source_target_pairs={{0,8},{8,0},{16,24},{24,16},{1,9},{9,1},{17,25},{25,17},{2,10},{10... | collective-permute-start | bytes 6152 | tf_op jit(solution)/shard_map/ppermute | solution.py:787
  88.2 2.0 %collective-permute-done.19 = f32[2,256]{1,0:T(2,128)S(1)} collective-permute-done((f32[2,256]{1,0:T(2,128)S(1)}, f32[2,256]{1,0:T(2,128)S(1)}, u32[]{:S(2)}, u32[]{:S(2)}) %collective-permute-start.19) | collective-permute-done | bytes 2080 | tf_op jit(solution)/shard_map/ppermute | solution.py:787
  90.2 2.6 %collective-permute-start.20 = (f32[2,256]{1,0:T(2,128)S(1)}, f32[2,256]{1,0:T(2,128)S(1)}, u32[]{:S(2)}, u32[]{:S(2)}) collective-permute-start(f32[2,256]{1,0:T(2,128)S(1)} %add.6), channel_id=1, source_target_pairs={{0,16},{8,24},{16,0},{24,8},{1,17},{9,25},{17,1},{25,9},{2,18},{10... | collective-permute-start | bytes 6152 | tf_op jit(solution)/shard_map/ppermute | solution.py:787
  92.8 1.5 %shard_map.100 = f32[1,2,256,2048]{3,2,1,0:T(8,128)} custom-call(f32[9,2,256,128]{3,2,1,0:T(8,128)S(1)} %get-tuple-element.111.groups_ref, f32[1,2,256,2048]{3,2,1,0:T(8,128)} %get-tuple-element.112._), custom_call_target="tpu_custom_call", output_to_operand_aliasing={{}: (1, {})} | custom-call | bytes 8388608 | tf_op jit(solution)/shard_map/pallas_call | solution.py:772
  (49 shorter events, 17.2 us)
Async XLA Ops:
  0.6 2.3 %copy-start.5 = (f32[1,8,2]{1,2,0:T(2,128)S(1)}, f32[1,8,2]{1,2,0:T(2,128)}, u32[]{:S(2)}) copy-start(f32[1,8,2]{1,2,0:T(2,128)} %param.9) | copy-start | bytes 196
  0.6 2.4 %copy-start.3 = (f32[1,8,2,128,128]{4,3,2,1,0:T(8,128)S(1)}, f32[1,8,2,128,128]{4,3,2,1,0:T(8,128)}, u32[]{:S(2)}) copy-start(f32[1,8,2,128,128]{4,3,2,1,0:T(8,128)} %param.7) | copy-start | bytes 3145732
  0.7 2.4 %copy-start.4 = (f32[1,2,128,128]{3,2,1,0:T(8,128)S(1)}, f32[1,2,128,128]{3,2,1,0:T(8,128)}, u32[]{:S(2)}) copy-start(f32[1,2,128,128]{3,2,1,0:T(8,128)} %param.8) | copy-start | bytes 393220
  2.3 2.7 %collective-permute-start = (f32[1,2,1,2048]{3,2,1,0:T(1,128)}, f32[1,2,1,2048]{3,2,1,0:T(1,128)S(1)}, u32[]{:S(2)}, u32[]{:S(2)}) collective-permute-start(f32[1,2,1,2048]{3,2,1,0:T(1,128)} %shard_map.79), channel_id=1, source_target_pairs={{1,2},{3,4},{5,6},{2,1},{4,3},{6,5},{9,10},{11,12},{13,14},{10,9},... | collective-permute-start | bytes 49160 | tf_op jit(solution)/shard_map/ppermute | solution.py:805
  3.1 2.2 %copy-start = (f32[1,2,256,2048]{3,2,1,0:T(8,128)S(1)}, f32[1,2,256,2048]{3,2,1,0:T(8,128)}, u32[]{:S(2)}) copy-start(f32[1,2,256,2048]{3,2,1,0:T(8,128)} %beside_ref.3) | copy-start | bytes 12582916
  3.1 2.2 %copy-start.2 = (s32[2,16]{1,0:T(2,128)S(1)}, s32[2,16]{1,0:T(2,128)}, u32[]{:S(2)}) copy-start(s32[2,16]{1,0:T(2,128)} %index_ref.35) | copy-start | bytes 388
  8.9 6.7 %copy-start.1 = (s32[2,16]{1,0:T(2,128)S(1)}, s32[2,16]{1,0:T(2,128)}, u32[]{:S(2)}) copy-start(s32[2,16]{1,0:T(2,128)} %index_ref.34) | copy-start | bytes 388
  8.9 6.7 %collective-permute-start.1 = (f32[2,2,264,256]{3,2,1,0:T(8,128)S(1)}, f32[2,2,264,256]{3,2,1,0:T(8,128)S(1)}, u32[]{:S(2)}, u32[]{:S(2)}) collective-permute-start(f32[2,2,264,256]{3,2,1,0:T(8,128)S(1)} %get-tuple-element.66), channel_id=1, source_target_pairs={{0,1},{1,0},{2,3},{3,2},{4,5},{5,4},{6,7},{7,6},{8,9},{9,8},{10,11... | collective-permute-start | bytes 3244040 | tf_op jit(solution)/shard_map/ppermute | solution.py:837
  22.4 7.3 %collective-permute-start.2 = (f32[2,2,264,256]{3,2,1,0:T(8,128)S(1)}, f32[2,2,264,256]{3,2,1,0:T(8,128)S(1)}, u32[]{:S(2)}, u32[]{:S(2)}) collective-permute-start(f32[2,2,264,256]{3,2,1,0:T(8,128)S(1)} %get-tuple-element.69), channel_id=1, source_target_pairs={{0,1},{1,0},{2,3},{3,2},{4,5},{5,4},{6,7},{7,6},{8,9},{9,8},{10,11... | collective-permute-start | bytes 3244040 | tf_op jit(solution)/shard_map/ppermute | solution.py:837
  22.9 19.2 %collective-permute-start.4 = (f32[520,128]{1,0:T(8,128)S(1)}, f32[520,128]{1,0:T(8,128)S(1)}, u32[]{:S(2)}, u32[]{:S(2)}) collective-permute-start(f32[520,128]{1,0:T(8,128)S(1)} %get-tuple-element.67.refs_1_), channel_id=1, source_target_pairs={{0,4},{1,5},{2,6},{3,7},{4,0},{5,1},{6,2},{7,3},{8,12},{9,13},{10,... | collective-permute-start | bytes 798728 | tf_op jit(solution)/shard_map/ppermute | solution.py:860
  24.9 16.4 %collective-permute-start.5 = (f32[520,128]{1,0:T(8,128)S(1)}, f32[520,128]{1,0:T(8,128)S(1)}, u32[]{:S(2)}, u32[]{:S(2)}) collective-permute-start(f32[520,128]{1,0:T(8,128)S(1)} %get-tuple-element.79), channel_id=1, source_target_pairs={{0,6},{1,7},{2,4},{3,5},{4,2},{5,3},{6,0},{7,1},{8,14},{9,15},{10,... | collective-permute-start | bytes 798728 | tf_op jit(solution)/shard_map/ppermute | solution.py:860
  29.4 12.7 %collective-permute-start.3 = (f32[520,128]{1,0:T(8,128)S(1)}, f32[520,128]{1,0:T(8,128)S(1)}, u32[]{:S(2)}, u32[]{:S(2)}) collective-permute-start(f32[520,128]{1,0:T(8,128)S(1)} %get-tuple-element.78), channel_id=1, source_target_pairs={{0,2},{1,3},{2,0},{3,1},{4,6},{5,7},{6,4},{7,5},{8,10},{9,11},{10,... | collective-permute-start | bytes 798728 | tf_op jit(solution)/shard_map/ppermute | solution.py:860
  35.8 10.2 %collective-permute-start.6 = (f32[520,128]{1,0:T(8,128)S(1)}, f32[520,128]{1,0:T(8,128)S(1)}, u32[]{:S(2)}, u32[]{:S(2)}) collective-permute-start(f32[520,128]{1,0:T(8,128)S(1)} %get-tuple-element.85), channel_id=1, source_target_pairs={{0,2},{1,3},{2,0},{3,1},{4,6},{5,7},{6,4},{7,5},{8,10},{9,11},{10,... | collective-permute-start | bytes 798728 | tf_op jit(solution)/shard_map/ppermute | solution.py:860
  37.6 14.7 %collective-permute-start.7 = (f32[520,128]{1,0:T(8,128)S(1)}, f32[520,128]{1,0:T(8,128)S(1)}, u32[]{:S(2)}, u32[]{:S(2)}) collective-permute-start(f32[520,128]{1,0:T(8,128)S(1)} %get-tuple-element.71._), channel_id=1, source_target_pairs={{0,4},{1,5},{2,6},{3,7},{4,0},{5,1},{6,2},{7,3},{8,12},{9,13},{10,... | collective-permute-start | bytes 798728 | tf_op jit(solution)/shard_map/ppermute | solution.py:860
  41.3 11.0 %collective-permute-start.8 = (f32[520,128]{1,0:T(8,128)S(1)}, f32[520,128]{1,0:T(8,128)S(1)}, u32[]{:S(2)}, u32[]{:S(2)}) collective-permute-start(f32[520,128]{1,0:T(8,128)S(1)} %get-tuple-element.86), channel_id=1, source_target_pairs={{0,6},{1,7},{2,4},{3,5},{4,2},{5,3},{6,0},{7,1},{8,14},{9,15},{10,... | collective-permute-start | bytes 798728 | tf_op jit(solution)/shard_map/ppermute | solution.py:860
  43.2 13.7 %collective-permute-start.10 = (f32[520,128]{1,0:T(8,128)S(1)}, f32[520,128]{1,0:T(8,128)S(1)}, u32[]{:S(2)}, u32[]{:S(2)}) collective-permute-start(f32[520,128]{1,0:T(8,128)S(1)} %get-tuple-element.91), channel_id=1, source_target_pairs={{0,2},{1,3},{2,0},{3,1},{4,6},{5,7},{6,4},{7,5},{8,10},{9,11},{10,... | collective-permute-start | bytes 798728 | tf_op jit(solution)/shard_map/ppermute | solution.py:895
  45.1 14.2 %collective-permute-start.11 = (f32[520,128]{1,0:T(8,128)S(1)}, f32[520,128]{1,0:T(8,128)S(1)}, u32[]{:S(2)}, u32[]{:S(2)}) collective-permute-start(f32[520,128]{1,0:T(8,128)S(1)} %get-tuple-element.95), channel_id=1, source_target_pairs={{0,4},{1,5},{2,6},{3,7},{4,0},{5,1},{6,2},{7,3},{8,12},{9,13},{10,... | collective-permute-start | bytes 798728 | tf_op jit(solution)/shard_map/ppermute | solution.py:895
  46.0 16.8 %collective-permute-start.12 = (f32[520,128]{1,0:T(8,128)S(1)}, f32[520,128]{1,0:T(8,128)S(1)}, u32[]{:S(2)}, u32[]{:S(2)}) collective-permute-start(f32[520,128]{1,0:T(8,128)S(1)} %get-tuple-element.96), channel_id=1, source_target_pairs={{0,6},{1,7},{2,4},{3,5},{4,2},{5,3},{6,0},{7,1},{8,14},{9,15},{10,... | collective-permute-start | bytes 798728 | tf_op jit(solution)/shard_map/ppermute | solution.py:895
  64.0 5.5 %collective-permute-start.14 = (f32[2,256,256]{2,1,0:T(8,128)S(1)}, f32[2,256,256]{2,1,0:T(8,128)S(1)}, u32[]{:S(2)}, u32[]{:S(2)}) collective-permute-start(f32[2,256,256]{2,1,0:T(8,128)S(1)} %shard_map.92._), channel_id=1, source_target_pairs={{0,1},{1,0},{2,3},{3,2},{4,5},{5,4},{6,7},{7,6},{8,9},{9,8},{10,11... | collective-permute-start | bytes 1572872 | tf_op jit(solution)/shard_map/ppermute | solution.py:922
  64.1 5.4 %collective-permute-start.13 = (f32[2,256,256]{2,1,0:T(8,128)S(1)}, f32[2,256,256]{2,1,0:T(8,128)S(1)}, u32[]{:S(2)}, u32[]{:S(2)}) collective-permute-start(f32[2,256,256]{2,1,0:T(8,128)S(1)} %shard_map.90._), channel_id=1, source_target_pairs={{0,1},{1,0},{2,3},{3,2},{4,5},{5,4},{6,7},{7,6},{8,9},{9,8},{10,11... | collective-permute-start | bytes 1572872 | tf_op jit(solution)/shard_map/ppermute | solution.py:922
  64.6 9.3 %collective-permute-start.9 = (f32[520,128]{1,0:T(8,128)S(1)}, f32[520,128]{1,0:T(8,128)S(1)}, u32[]{:S(2)}, u32[]{:S(2)}) collective-permute-start(f32[520,128]{1,0:T(8,128)S(1)} %get-tuple-element.88), channel_id=1, source_target_pairs={{0,2},{1,3},{2,0},{3,1},{4,6},{5,7},{6,4},{7,5},{8,10},{9,11},{10,... | collective-permute-start | bytes 798728 | tf_op jit(solution)/shard_map/ppermute | solution.py:895
  65.3 13.8 %collective-permute-start.15 = (f32[520,128]{1,0:T(8,128)S(1)}, f32[520,128]{1,0:T(8,128)S(1)}, u32[]{:S(2)}, u32[]{:S(2)}) collective-permute-start(f32[520,128]{1,0:T(8,128)S(1)} %get-tuple-element.103), channel_id=1, source_target_pairs={{0,4},{1,5},{2,6},{3,7},{4,0},{5,1},{6,2},{7,3},{8,12},{9,13},{10,... | collective-permute-start | bytes 798728 | tf_op jit(solution)/shard_map/ppermute | solution.py:895
  66.3 12.8 %collective-permute-start.16 = (f32[520,128]{1,0:T(8,128)S(1)}, f32[520,128]{1,0:T(8,128)S(1)}, u32[]{:S(2)}, u32[]{:S(2)}) collective-permute-start(f32[520,128]{1,0:T(8,128)S(1)} %get-tuple-element.104), channel_id=1, source_target_pairs={{0,6},{1,7},{2,4},{3,5},{4,2},{5,3},{6,0},{7,1},{8,14},{9,15},{10,... | collective-permute-start | bytes 798728 | tf_op jit(solution)/shard_map/ppermute | solution.py:895
  80.3 2.0 %collective-permute-start.18 = (f32[2,256,256]{2,1,0:T(8,128)S(1)}, f32[2,256,256]{2,1,0:T(8,128)S(1)}, u32[]{:S(2)}, u32[]{:S(2)}) collective-permute-start(f32[2,256,256]{2,1,0:T(8,128)S(1)} %shard_map.97._), channel_id=1, source_target_pairs={{0,1},{1,0},{2,3},{3,2},{4,5},{5,4},{6,7},{7,6},{8,9},{9,8},{10,11... | collective-permute-start | bytes 1572872 | tf_op jit(solution)/shard_map/ppermute | solution.py:922
  80.4 2.6 %collective-permute-start.17 = (f32[2,256,256]{2,1,0:T(8,128)S(1)}, f32[2,256,256]{2,1,0:T(8,128)S(1)}, u32[]{:S(2)}, u32[]{:S(2)}) collective-permute-start(f32[2,256,256]{2,1,0:T(8,128)S(1)} %shard_map.95._), channel_id=1, source_target_pairs={{0,1},{1,0},{2,3},{3,2},{4,5},{5,4},{6,7},{7,6},{8,9},{9,8},{10,11... | collective-permute-start | bytes 1572872 | tf_op jit(solution)/shard_map/ppermute | solution.py:922
  86.6 3.6 %collective-permute-start.19 = (f32[2,256]{1,0:T(2,128)S(1)}, f32[2,256]{1,0:T(2,128)S(1)}, u32[]{:S(2)}, u32[]{:S(2)}) collective-permute-start(f32[2,256]{1,0:T(2,128)S(1)} %get-tuple-element.113), channel_id=1, source_target_pairs={{0,8},{8,0},{16,24},{24,16},{1,9},{9,1},{17,25},{25,17},{2,10},{10... | collective-permute-start | bytes 6152 | tf_op jit(solution)/shard_map/ppermute | solution.py:787
  90.2 4.5 %collective-permute-start.20 = (f32[2,256]{1,0:T(2,128)S(1)}, f32[2,256]{1,0:T(2,128)S(1)}, u32[]{:S(2)}, u32[]{:S(2)}) collective-permute-start(f32[2,256]{1,0:T(2,128)S(1)} %add.6), channel_id=1, source_target_pairs={{0,16},{8,24},{16,0},{24,8},{1,17},{9,25},{17,1},{25,9},{2,18},{10... | collective-permute-start | bytes 6152 | tf_op jit(solution)/shard_map/ppermute | solution.py:787

commit v3 on v2

--- a/solution.py
+++ b/solution.py
@@ -323,10 +323,10 @@
 def first_pass_kernel(place_ref, index_ref, field_ref, beside_ref, halo_ref, high_ref, low_ref, edge_ref, *refs,
                       half, group, block):
     if half:
-        carry_ref, keep_ref, send_ref, own = None, refs[1], refs[2], refs[3]
+        carry_ref, keep_ref, send_ref, odd = None, refs[1], refs[2], refs[3]
         state_ref = refs[0]
     else:
-        carry_ref, _, keep_ref, send_ref, own = refs
+        carry_ref, _, keep_ref, send_ref, odd = refs
         state_ref = None
     width = field_ref.shape[-1]
     count = width // group
@@ -349,16 +349,21 @@
     def write(k, solved):
         start = (k - low) * group
         b, inner = start // block, start % block
-        own[b % 2, b // 2, 0, :, inner : inner + group] = solved[:, :group]
-        own[b % 2, b // 2, 1, :, inner : inner + group] = solved[:, group:]
+        columns = slice(inner, inner + group)
+        for part in range(2):
+            value = solved[:, part * group : (part + 1) * group]
+            if b % 2:
+                odd[b // 2, part, :, columns] = value
+            else:
+                other = odd[b // 2, part, :, columns]
+                keep_ref[b // 2, part, :, columns] = jnp.where(core == 0, value, other)
+                send_ref[b // 2, part, :, columns] = jnp.where(core == 0, other, value)
         if half and k == low:
             state_ref[...] = solved
 
     line_groups(
         read, lambda k: index_ref[0, k], (high_ref, low_ref, edge_ref), low, low + count, following, below, above, write
     )
-    keep_ref[...] = own[core]
-    send_ref[...] = own[1 - core]
 
 
 def first_pass(place, recv_index, field, halo, tables, half, carry, after, block, group):
@@ -386,7 +391,7 @@
         out_shape=outs,
         in_specs=specs,
         out_specs=[vmem()] * len(outs),
-        scratch_shapes=[pltpu.VMEM((2,) + shape, f32)],
+        scratch_shapes=[pltpu.VMEM(shape, f32)],
         compiler_params=params(36),
         cost_estimate=cost(lines * width * group * 24, 8 * lines * width * 2),
     )(*args)
@@ -439,7 +444,7 @@
 
 
 def open_sweep_kernel(place_ref, index_ref, high_ref, low_ref, edge_ref, keep_ref, come_ref, _, near_ref, far_ref, local_ref,
-                      base_ref, pair, *, groups, group):
+                      base_ref, *, groups, group):
     device = place_ref[0]
     chip, core = device // 2, device % 2
     tables = (high_ref, low_ref, edge_ref)
@@ -457,8 +462,9 @@
         ]
 
     def store_pair(where, value):
-        for sub in range(2):
-            pair[sub, where, :] = value[:, sub * (width // 2) : (sub + 1) * (width // 2)]
+        low_side, high_side = value[:, : width // 2], value[:, width // 2 :]
+        near_ref[where, :] = jnp.where(chip % 2 == 0, low_side, high_side)
+        far_ref[where, :] = jnp.where(chip % 2 == 0, high_side, low_side)
 
     def given(k):
         return rows(k // half, (k % half) * group, group)
@@ -498,8 +504,6 @@
     local_ref[0] = done
     store_pair(slice(0, 2 * group), solved)
     store_pair(slice(2 * group, 4 * group), done)
-    near_ref[...] = pair[chip % 2]
-    far_ref[...] = pair[1 - chip % 2]
 
 
 def unit_rows(group):
@@ -717,11 +721,9 @@
     for i in range(block // group):
         mine = device * (block // group) + i
         here = mine > count if half else mine <= count
-
-        @pl.when(here)
-        def _():
-            square = result[jnp.where(here, mine - first, 0), 0, i * group : (i + 1) * group, :]
-            image_ref[row : row + 1, i * group : (i + 1) * group] = diagonal_of(square)
+        square = result[jnp.where(here, mine - first, 0), 0, i * group : (i + 1) * group, :]
+        columns = slice(i * group, (i + 1) * group)
+        image_ref[row : row + 1, columns] = jnp.where(here, diagonal_of(square), image_ref[row : row + 1, columns])
 
     for copy in copies:
         copy.wait()
@@ -845,7 +847,6 @@
             + [pl.BlockSpec((1,) + keep[half].shape[1:], lambda i, at, _: ((at[0] // 4) ^ second_pair, 0, 0, 0))] * 2
             + [anywhere()],
             out_specs=[vmem()] * 4,
-            scratch_shapes=[pltpu.VMEM((2,) + piece.shape, f32)],
         )
         name = "%d_%d" % (half, second_pair)
         near, far, locals_[name], bases[name] = pl.pallas_call(

time: 95.4 us -> 94.5 us (level)
  Pallas kernels: 50.4 us -> 49 us
where the time goes in v3:
time: 94.5 us; the launch traced here: 94.3 us
  Pallas kernels  49 us (52%)
  starting transfers between devices  26 us (28%)
  waiting for transfers between devices  17.5 us (19%)
    pallas_call x4, Pallas kernels, open_sweep(): pl.pallas_call(functools.partial(open_sweep_kernel, groups=groups, group=...  11.8 us
    ppermute x6, waiting for transfers between devices, fast_shards(): lax.ppermute(carries[offset], 'plane', moves)  10.2 us
    pallas_call x8, Pallas kernels, fast_shards(): pl.pallas_call(functools.partial(close_sweep_kernel, groups=groups, group...  9.94 us
    ppermute x6, starting transfers between devices, fast_shards(): lax.ppermute(carries[offset], 'plane', moves)  7.91 us
    pallas_call x2, Pallas kernels, last_pass(): pl.pallas_call(functools.partial(last_pass_kernel, half=half, step=step,...  7.29 us
    ppermute x6, starting transfers between devices, open_sweep(): lax.ppermute(item, 'plane', moves)  7.18 us
    pallas_call x2, Pallas kernels, first_pass(): pl.pallas_call(functools.partial(first_pass_kernel, half=half, group=grou...  6.58 us
    ppermute x2, starting transfers between devices, first(): come[half] = lax.ppermute(send, 'plane', partner)  4.83 us
  transfers between devices with their start and end apart: 21, of which 10 were waited for; matrix products, arithmetic and copies ran while one was open for 0% of the time, Pallas kernels for 34%

profile of v3, /device:TPU:0, one launch (start us, length us, event | category | flops | bytes accessed | tf_op | source)
XLA Modules:
  0.0 94.3 jit_solution(15026762995110252930)
XLA Ops:
  0.7 1.6 %shard_map.79 = f32[1,2,1,2048]{3,2,1,0:T(1,128)} custom-call(s32[1]{0:T(128)} %bitcast.place_ref, f32[1,2,256,2048]{3,2,1,0:T(8,128)} %beside_ref.3), custom_call_target="tpu_custom_call" | custom-call | flops 20000000000 | bytes 1048576 | tf_op jit(solution)/shard_map/pallas_call | solution.py:285
  3.1 1.9 %shard_map.77 = (bf16[9,256,256]{2,1,0:T(8,128)(2,1)S(1)}, bf16[9,256,256]{2,1,0:T(8,128)(2,1)S(1)}, f32[8,4,256]{2,1,0:T(4,128)S(1)}) custom-call(f32[1,8,2]{2,1,0:T(8,128)S(1)} %copy.9.rhs_ref, f32[8,2,128,128]{3,2,1,0:T(8,128)S(1)} %bitcast.3, f32[2,128,128]{2,1,0:T(8,128)S(1)} %bitcast.5), custom_call_target="tpu_custom_call" | custom-call | flops 20000000000 | bytes 4194304 | tf_op jit(solution)/shard_map/pallas_call | solution.py:262
  5.3 3.2 %shard_map.80 = (f32[264,256]{1,0:T(8,128)S(1)}, f32[2,2,264,256]{3,2,1,0:T(8,128)S(1)}, f32[2,2,264,256]{3,2,1,0:T(8,128)S(1)}) custom-call(s32[1]{0:T(128)} %bitcast.place_ref, s32[2,16]{1,0:T(2,128)S(1)} %copy-done.2, f32[1,2,256,2048]{3,2,1,0:T(8,128)S(1)} %copy-done, f32[1,2,256,2048]{3,2,1,0:T(8,128)S(1)} %copy-done, ...), custom_call_target="tpu_custom_call" | custom-call | flops 1660944384 | bytes 4325376 | tf_op jit(solution)/shard_map/pallas_call | solution.py:388
  8.5 4.4 %collective-permute-start.1 = (f32[2,2,264,256]{3,2,1,0:T(8,128)S(1)}, f32[2,2,264,256]{3,2,1,0:T(8,128)S(1)}, u32[]{:S(2)}, u32[]{:S(2)}) collective-permute-start(f32[2,2,264,256]{3,2,1,0:T(8,128)S(1)} %get-tuple-element.66), channel_id=1, source_target_pairs={{0,1},{1,0},{2,3},{3,2},{4,5},{5,4},{6,7},{7,6},{8,9},{9,8},{10,11... | collective-permute-start | bytes 3244040 | tf_op jit(solution)/shard_map/ppermute | solution.py:839
  12.9 1.9 %shard_map.78 = (bf16[9,256,256]{2,1,0:T(8,128)(2,1)S(1)}, bf16[9,256,256]{2,1,0:T(8,128)(2,1)S(1)}, f32[8,2,256,128]{3,2,1,0:T(8,128)S(1)}) custom-call(f32[1,8,2]{2,1,0:T(8,128)S(1)} %copy.9.rhs_ref, f32[8,2,128,128]{3,2,1,0:T(8,128)S(1)} %bitcast.4, f32[2,128,128]{2,1,0:T(8,128)S(1)} %bitcast.6), custom_call_target="tpu_custom_call" | custom-call | flops 20000000000 | bytes 4194304 | tf_op jit(solution)/shard_map/pallas_call | solution.py:262
  15.2 2.9 %shard_map.81 = (f32[520,128]{1,0:T(8,128)S(1)}, f32[520,128]{1,0:T(8,128)S(1)}, f32[4,256,256]{2,1,0:T(8,128)S(1)}, f32[2,2,128,128]{3,2,1,0:T(8,128)S(1)}) custom-call(s32[1]{0:T(128)} %bitcast.place_ref, s32[2,16]{1,0:T(2,128)S(1)} %copy-done.1, bf16[9,256,256]{2,1,0:T(8,128)(2,1)S(1)} %get-tuple-element.62.high_ref, ...), custom_call_target="tpu_custom_call" | custom-call | flops 1610612736 | bytes 3145728 | tf_op jit(solution)/shard_map/pallas_call | solution.py:852
  18.1 3.4 %shard_map.82 = (f32[2,2,264,256]{3,2,1,0:T(8,128)S(1)}, f32[2,2,264,256]{3,2,1,0:T(8,128)S(1)}) custom-call(s32[1]{0:T(128)} %bitcast.place_ref, s32[2,16]{1,0:T(2,128)S(1)} %copy-done.2, f32[1,2,256,2048]{3,2,1,0:T(8,128)S(1)} %copy-done, f32[1,2,256,2048]{3,2,1,0:T(8,128)S(1)} %copy-done, f32[1,2,1,2048]{3,2,1,0:T(1,128)S(1)} %collective-permute-done.halo_ref, ...), custom_call_target="tpu_custom_call" | custom-call | flops 1660944384 | bytes 4325376 | tf_op jit(solution)/shard_map/pallas_call | solution.py:388
  22.0 2.0 %collective-permute-start.4 = (f32[520,128]{1,0:T(8,128)S(1)}, f32[520,128]{1,0:T(8,128)S(1)}, u32[]{:S(2)}, u32[]{:S(2)}) collective-permute-start(f32[520,128]{1,0:T(8,128)S(1)} %get-tuple-element.67.refs_1_), channel_id=1, source_target_pairs={{0,4},{1,5},{2,6},{3,7},{4,0},{5,1},{6,2},{7,3},{8,12},{9,13},{10,... | collective-permute-start | bytes 798728 | tf_op jit(solution)/shard_map/ppermute | solution.py:861
  24.0 1.3 %collective-permute-start.5 = (f32[520,128]{1,0:T(8,128)S(1)}, f32[520,128]{1,0:T(8,128)S(1)}, u32[]{:S(2)}, u32[]{:S(2)}) collective-permute-start(f32[520,128]{1,0:T(8,128)S(1)} %get-tuple-element.79), channel_id=1, source_target_pairs={{0,6},{1,7},{2,4},{3,5},{4,2},{5,3},{6,0},{7,1},{8,14},{9,15},{10,... | collective-permute-start | bytes 798728 | tf_op jit(solution)/shard_map/ppermute | solution.py:861
  25.2 2.9 %shard_map.83 = (f32[520,128]{1,0:T(8,128)S(1)}, f32[520,128]{1,0:T(8,128)S(1)}, f32[4,256,256]{2,1,0:T(8,128)S(1)}, f32[2,2,128,128]{3,2,1,0:T(8,128)S(1)}) custom-call(s32[1]{0:T(128)} %bitcast.place_ref, s32[2,16]{1,0:T(2,128)S(1)} %copy-done.1, bf16[9,256,256]{2,1,0:T(8,128)(2,1)S(1)} %get-tuple-element.62.high_ref, ...), custom_call_target="tpu_custom_call" | custom-call | flops 1610612736 | bytes 3145728 | tf_op jit(solution)/shard_map/pallas_call | solution.py:852
  28.4 3.1 %shard_map.84 = (f32[520,128]{1,0:T(8,128)S(1)}, f32[520,128]{1,0:T(8,128)S(1)}, f32[4,256,256]{2,1,0:T(8,128)S(1)}, f32[2,2,128,128]{3,2,1,0:T(8,128)S(1)}) custom-call(s32[1]{0:T(128)} %bitcast.place_ref, s32[2,16]{1,0:T(2,128)S(1)} %copy-done.1, bf16[9,256,256]{2,1,0:T(8,128)(2,1)S(1)} %get-tuple-element.62.high_ref, ...), custom_call_target="tpu_custom_call" | custom-call | flops 1610612736 | bytes 3145728 | tf_op jit(solution)/shard_map/pallas_call | solution.py:852
  31.5 2.9 %shard_map.85 = (f32[520,128]{1,0:T(8,128)S(1)}, f32[520,128]{1,0:T(8,128)S(1)}, f32[4,256,256]{2,1,0:T(8,128)S(1)}, f32[2,2,128,128]{3,2,1,0:T(8,128)S(1)}) custom-call(s32[1]{0:T(128)} %bitcast.place_ref, s32[2,16]{1,0:T(2,128)S(1)} %copy-done.1, bf16[9,256,256]{2,1,0:T(8,128)(2,1)S(1)} %get-tuple-element.62.high_ref, ...), custom_call_target="tpu_custom_call" | custom-call | flops 1610612736 | bytes 3145728 | tf_op jit(solution)/shard_map/pallas_call | solution.py:852
  34.4 1.9 %collective-permute-start.6 = (f32[520,128]{1,0:T(8,128)S(1)}, f32[520,128]{1,0:T(8,128)S(1)}, u32[]{:S(2)}, u32[]{:S(2)}) collective-permute-start(f32[520,128]{1,0:T(8,128)S(1)} %get-tuple-element.85), channel_id=1, source_target_pairs={{0,2},{1,3},{2,0},{3,1},{4,6},{5,7},{6,4},{7,5},{8,10},{9,11},{10,... | collective-permute-start | bytes 798728 | tf_op jit(solution)/shard_map/ppermute | solution.py:861
  37.2 2.7 %shard_map.86 = (bf16[4,256,256]{2,1,0:T(8,128)(2,1)S(1)}, bf16[4,256,256]{2,1,0:T(8,128)(2,1)S(1)}, f32[4,128,256]{2,1,0:T(8,128)S(1)}, bf16[2,256,256]{2,1,0:T(8,128)(2,1)S(1)}, bf16[2,256,256]{2,1,0:T(8,128)(2,1)S(1)}) custom-call(s32[2,16]{1,0:T(2,128)S(1)} %copy-done.1, bf16[9,256,256]{2,1,0:T(8,128)(2,1)S(1)} %get-tuple-element.58.high_ref, ...), custom_call_target="tpu_custom_call" | custom-call | flops 1073741824 | bytes 4194304 | tf_op jit(solution)/shard_map/pallas_call | solution.py:822
  41.9 1.9 %collective-permute-start.10 = (f32[520,128]{1,0:T(8,128)S(1)}, f32[520,128]{1,0:T(8,128)S(1)}, u32[]{:S(2)}, u32[]{:S(2)}) collective-permute-start(f32[520,128]{1,0:T(8,128)S(1)} %get-tuple-element.91), channel_id=1, source_target_pairs={{0,2},{1,3},{2,0},{3,1},{4,6},{5,7},{6,4},{7,5},{8,10},{9,11},{10,... | collective-permute-start | bytes 798728 | tf_op jit(solution)/shard_map/ppermute | solution.py:896
  44.7 1.6 %collective-permute-start.12 = (f32[520,128]{1,0:T(8,128)S(1)}, f32[520,128]{1,0:T(8,128)S(1)}, u32[]{:S(2)}, u32[]{:S(2)}) collective-permute-start(f32[520,128]{1,0:T(8,128)S(1)} %get-tuple-element.96), channel_id=1, source_target_pairs={{0,6},{1,7},{2,4},{3,5},{4,2},{5,3},{6,0},{7,1},{8,14},{9,15},{10,... | collective-permute-start | bytes 798728 | tf_op jit(solution)/shard_map/ppermute | solution.py:896
  46.3 1.6 %shard_map.88 = (bf16[4,256,256]{2,1,0:T(8,128)(2,1)S(1)}, bf16[4,256,256]{2,1,0:T(8,128)(2,1)S(1)}) custom-call(s32[1]{0:T(128)} %bitcast.place_ref, s32[2,16]{1,0:T(2,128)S(1)} %copy-done.1, bf16[9,256,256]{2,1,0:T(8,128)(2,1)S(1)} %get-tuple-element.58.high_ref, bf16[9,256,256]{2,1,0:T(8,128)(2,1)S(1)} %get-tuple-element.59.low_ref, ...), custom_call_target="tpu_custom_call" | custom-call | flops 536870912 | bytes 4194304 | tf_op jit(solution)/shard_map/pallas_call | solution.py:885
  47.9 3.4 %collective-permute-done.8.refs_3_ = f32[520,128]{1,0:T(8,128)S(1)} collective-permute-done((f32[520,128]{1,0:T(8,128)S(1)}, f32[520,128]{1,0:T(8,128)S(1)}, u32[]{:S(2)}, u32[]{:S(2)}) %collective-permute-start.8) | collective-permute-done | bytes 266272 | tf_op jit(solution)/shard_map/ppermute | solution.py:861
  52.4 3.2 %collective-permute-done.10.far_ref = f32[520,128]{1,0:T(8,128)S(1)} collective-permute-done((f32[520,128]{1,0:T(8,128)S(1)}, f32[520,128]{1,0:T(8,128)S(1)}, u32[]{:S(2)}, u32[]{:S(2)}) %collective-permute-start.10) | collective-permute-done | bytes 266272 | tf_op jit(solution)/shard_map/ppermute | solution.py:896
  55.6 1.2 %shard_map.90._ = f32[2,256,256]{2,1,0:T(8,128)S(1)} custom-call(s32[1]{0:T(128)} %bitcast.place_ref, s32[2,16]{1,0:T(2,128)S(1)} %copy-done.1, f32[8,2,256,128]{3,2,1,0:T(8,128)S(1)} %get-tuple-element.61.edge_ref, bf16[4,256,256]{2,1,0:T(8,128)(2,1)S(1)} %get-tuple-element.73.power_high.refs_4_, bf16[4,256,256]{2,1,0:T(8,128)(2,1)S(1)} %get-tuple-element.74.power_low, ...), custom_call_target="tpu_custom_call" | custom-call | flops 402653184 | bytes 1048576 | tf_op jit(solution)/shard_map/pallas_call | solution.py:907
  56.8 1.2 %shard_map.91 = (f32[2,256,256]{2,1,0:T(8,128)S(1)}, f32[1,256]{1,0:T(1,128)S(1)}) custom-call(s32[1]{0:T(128)} %bitcast.place_ref, s32[2,16]{1,0:T(2,128)S(1)} %copy-done.1, f32[8,2,256,128]{3,2,1,0:T(8,128)S(1)} %get-tuple-element.61.edge_ref, bf16[4,256,256]{2,1,0:T(8,128)(2,1)S(1)} %get-tuple-element.73.power_high.refs_4_, ...), custom_call_target="tpu_custom_call" | custom-call | flops 402653184 | bytes 1048576 | tf_op jit(solution)/shard_map/pallas_call | solution.py:907
  58.0 3.9 %collective-permute-done.12.far_ref = f32[520,128]{1,0:T(8,128)S(1)} collective-permute-done((f32[520,128]{1,0:T(8,128)S(1)}, f32[520,128]{1,0:T(8,128)S(1)}, u32[]{:S(2)}, u32[]{:S(2)}) %collective-permute-start.12) | collective-permute-done | bytes 266272 | tf_op jit(solution)/shard_map/ppermute | solution.py:896
  65.2 1.9 %collective-permute-start.16 = (f32[520,128]{1,0:T(8,128)S(1)}, f32[520,128]{1,0:T(8,128)S(1)}, u32[]{:S(2)}, u32[]{:S(2)}) collective-permute-start(f32[520,128]{1,0:T(8,128)S(1)} %get-tuple-element.104), channel_id=1, source_target_pairs={{0,6},{1,7},{2,4},{3,5},{4,2},{5,3},{6,0},{7,1},{8,14},{9,15},{10,... | collective-permute-start | bytes 798728 | tf_op jit(solution)/shard_map/ppermute | solution.py:896
  67.1 1.4 %shard_map.93 = (f32[2,256,256]{2,1,0:T(8,128)S(1)}, f32[1,256]{1,0:T(1,128)S(1)}) custom-call(s32[1]{0:T(128)} %bitcast.place_ref, s32[2,16]{1,0:T(2,128)S(1)} %copy-done.1, f32[8,2,256,128]{3,2,1,0:T(8,128)S(1)} %get-tuple-element.61.edge_ref, bf16[4,256,256]{2,1,0:T(8,128)(2,1)S(1)} %get-tuple-element.73.power_high.refs_4_, ...), custom_call_target="tpu_custom_call" | custom-call | flops 402653184 | bytes 1048576 | tf_op jit(solution)/shard_map/pallas_call | solution.py:907
  68.6 3.8 %shard_map.94 = (f32[1,2,256,2048]{3,2,1,0:T(8,128)}, f32[256,256]{1,0:T(8,128)S(1)}, f32[2,256,128]{2,1,0:T(8,128)S(1)}, f32[1,256]{1,0:T(1,128)S(1)}) custom-call(s32[1]{0:T(128)} %bitcast.place_ref, s32[2,16]{1,0:T(2,128)S(1)} %copy-done.2, bf16[9,256,256]{2,1,0:T(8,128)(2,1)S(1)} %get-tuple-element.58.high_ref, ...), custom_call_target="tpu_custom_call" | custom-call | flops 1610612736 | bytes 4194304 | tf_op jit(solution)/shard_map/pallas_call | solution.py:750
  74.1 1.4 %shard_map.96 = (f32[2,256,256]{2,1,0:T(8,128)S(1)}, f32[1,256]{1,0:T(1,128)S(1)}) custom-call(s32[1]{0:T(128)} %bitcast.place_ref, s32[2,16]{1,0:T(2,128)S(1)} %copy-done.1, f32[8,2,256,128]{3,2,1,0:T(8,128)S(1)} %get-tuple-element.61.edge_ref, bf16[4,256,256]{2,1,0:T(8,128)(2,1)S(1)} %get-tuple-element.73.power_high.refs_4_, ...), custom_call_target="tpu_custom_call" | custom-call | flops 402653184 | bytes 1048576 | tf_op jit(solution)/shard_map/pallas_call | solution.py:907
  75.5 2.6 %collective-permute-done.15.near_ref = f32[520,128]{1,0:T(8,128)S(1)} collective-permute-done((f32[520,128]{1,0:T(8,128)S(1)}, f32[520,128]{1,0:T(8,128)S(1)}, u32[]{:S(2)}, u32[]{:S(2)}) %collective-permute-start.15) | collective-permute-done | bytes 266272 | tf_op jit(solution)/shard_map/ppermute | solution.py:896
  82.1 3.5 %shard_map.99 = (f32[9,2,256,128]{3,2,1,0:T(8,128)S(1)}, f32[2,256]{1,0:T(2,128)S(1)}) custom-call(s32[1]{0:T(128)} %bitcast.place_ref, s32[2,16]{1,0:T(2,128)S(1)} %copy-done.2, bf16[9,256,256]{2,1,0:T(8,128)(2,1)S(1)} %get-tuple-element.58.high_ref, bf16[9,256,256]{2,1,0:T(8,128)(2,1)S(1)} %get-tuple-element.59.low_ref, ...), custom_call_target="tpu_custom_call" | custom-call | flops 1610612736 | bytes 4194304 | tf_op jit(solution)/shard_map/pallas_call | solution.py:750
  85.6 1.6 %collective-permute-start.19 = (f32[2,256]{1,0:T(2,128)S(1)}, f32[2,256]{1,0:T(2,128)S(1)}, u32[]{:S(2)}, u32[]{:S(2)}) collective-permute-start(f32[2,256]{1,0:T(2,128)S(1)} %get-tuple-element.113), channel_id=1, source_target_pairs={{0,8},{8,0},{16,24},{24,16},{1,9},{9,1},{17,25},{25,17},{2,10},{10... | collective-permute-start | bytes 6152 | tf_op jit(solution)/shard_map/ppermute | solution.py:789
  87.2 2.0 %collective-permute-done.19 = f32[2,256]{1,0:T(2,128)S(1)} collective-permute-done((f32[2,256]{1,0:T(2,128)S(1)}, f32[2,256]{1,0:T(2,128)S(1)}, u32[]{:S(2)}, u32[]{:S(2)}) %collective-permute-start.19) | collective-permute-done | bytes 2080 | tf_op jit(solution)/shard_map/ppermute | solution.py:789
  89.3 2.6 %collective-permute-start.20 = (f32[2,256]{1,0:T(2,128)S(1)}, f32[2,256]{1,0:T(2,128)S(1)}, u32[]{:S(2)}, u32[]{:S(2)}) collective-permute-start(f32[2,256]{1,0:T(2,128)S(1)} %add.6), channel_id=1, source_target_pairs={{0,16},{8,24},{16,0},{24,8},{1,17},{9,25},{17,1},{25,9},{2,18},{10... | collective-permute-start | bytes 6152 | tf_op jit(solution)/shard_map/ppermute | solution.py:789
  91.9 1.5 %shard_map.100 = f32[1,2,256,2048]{3,2,1,0:T(8,128)} custom-call(f32[9,2,256,128]{3,2,1,0:T(8,128)S(1)} %get-tuple-element.111.groups_ref, f32[1,2,256,2048]{3,2,1,0:T(8,128)} %get-tuple-element.112._), custom_call_target="tpu_custom_call", output_to_operand_aliasing={{}: (1, {})} | custom-call | bytes 8388608 | tf_op jit(solution)/shard_map/pallas_call | solution.py:774
  (49 shorter events, 17.0 us)
Async XLA Ops:
  0.6 2.3 %copy-start.5 = (f32[1,8,2]{1,2,0:T(2,128)S(1)}, f32[1,8,2]{1,2,0:T(2,128)}, u32[]{:S(2)}) copy-start(f32[1,8,2]{1,2,0:T(2,128)} %param.9) | copy-start | bytes 196
  0.6 2.4 %copy-start.3 = (f32[1,8,2,128,128]{4,3,2,1,0:T(8,128)S(1)}, f32[1,8,2,128,128]{4,3,2,1,0:T(8,128)}, u32[]{:S(2)}) copy-start(f32[1,8,2,128,128]{4,3,2,1,0:T(8,128)} %param.7) | copy-start | bytes 3145732
  0.7 2.4 %copy-start.4 = (f32[1,2,128,128]{3,2,1,0:T(8,128)S(1)}, f32[1,2,128,128]{3,2,1,0:T(8,128)}, u32[]{:S(2)}) copy-start(f32[1,2,128,128]{3,2,1,0:T(8,128)} %param.8) | copy-start | bytes 393220
  2.3 2.7 %collective-permute-start = (f32[1,2,1,2048]{3,2,1,0:T(1,128)}, f32[1,2,1,2048]{3,2,1,0:T(1,128)S(1)}, u32[]{:S(2)}, u32[]{:S(2)}) collective-permute-start(f32[1,2,1,2048]{3,2,1,0:T(1,128)} %shard_map.79), channel_id=1, source_target_pairs={{1,2},{3,4},{5,6},{2,1},{4,3},{6,5},{9,10},{11,12},{13,14},{10,9},... | collective-permute-start | bytes 49160 | tf_op jit(solution)/shard_map/ppermute | solution.py:807
  3.1 2.2 %copy-start = (f32[1,2,256,2048]{3,2,1,0:T(8,128)S(1)}, f32[1,2,256,2048]{3,2,1,0:T(8,128)}, u32[]{:S(2)}) copy-start(f32[1,2,256,2048]{3,2,1,0:T(8,128)} %beside_ref.3) | copy-start | bytes 12582916
  3.1 2.2 %copy-start.2 = (s32[2,16]{1,0:T(2,128)S(1)}, s32[2,16]{1,0:T(2,128)}, u32[]{:S(2)}) copy-start(s32[2,16]{1,0:T(2,128)} %index_ref.35) | copy-start | bytes 388
  8.5 6.7 %copy-start.1 = (s32[2,16]{1,0:T(2,128)S(1)}, s32[2,16]{1,0:T(2,128)}, u32[]{:S(2)}) copy-start(s32[2,16]{1,0:T(2,128)} %index_ref.34) | copy-start | bytes 388
  8.5 6.7 %collective-permute-start.1 = (f32[2,2,264,256]{3,2,1,0:T(8,128)S(1)}, f32[2,2,264,256]{3,2,1,0:T(8,128)S(1)}, u32[]{:S(2)}, u32[]{:S(2)}) collective-permute-start(f32[2,2,264,256]{3,2,1,0:T(8,128)S(1)} %get-tuple-element.66), channel_id=1, source_target_pairs={{0,1},{1,0},{2,3},{3,2},{4,5},{5,4},{6,7},{7,6},{8,9},{9,8},{10,11... | collective-permute-start | bytes 3244040 | tf_op jit(solution)/shard_map/ppermute | solution.py:839
  21.5 6.9 %collective-permute-start.2 = (f32[2,2,264,256]{3,2,1,0:T(8,128)S(1)}, f32[2,2,264,256]{3,2,1,0:T(8,128)S(1)}, u32[]{:S(2)}, u32[]{:S(2)}) collective-permute-start(f32[2,2,264,256]{3,2,1,0:T(8,128)S(1)} %get-tuple-element.69), channel_id=1, source_target_pairs={{0,1},{1,0},{2,3},{3,2},{4,5},{5,4},{6,7},{7,6},{8,9},{9,8},{10,11... | collective-permute-start | bytes 3244040 | tf_op jit(solution)/shard_map/ppermute | solution.py:839
  22.0 18.8 %collective-permute-start.4 = (f32[520,128]{1,0:T(8,128)S(1)}, f32[520,128]{1,0:T(8,128)S(1)}, u32[]{:S(2)}, u32[]{:S(2)}) collective-permute-start(f32[520,128]{1,0:T(8,128)S(1)} %get-tuple-element.67.refs_1_), channel_id=1, source_target_pairs={{0,4},{1,5},{2,6},{3,7},{4,0},{5,1},{6,2},{7,3},{8,12},{9,13},{10,... | collective-permute-start | bytes 798728 | tf_op jit(solution)/shard_map/ppermute | solution.py:861
  24.0 16.0 %collective-permute-start.5 = (f32[520,128]{1,0:T(8,128)S(1)}, f32[520,128]{1,0:T(8,128)S(1)}, u32[]{:S(2)}, u32[]{:S(2)}) collective-permute-start(f32[520,128]{1,0:T(8,128)S(1)} %get-tuple-element.79), channel_id=1, source_target_pairs={{0,6},{1,7},{2,4},{3,5},{4,2},{5,3},{6,0},{7,1},{8,14},{9,15},{10,... | collective-permute-start | bytes 798728 | tf_op jit(solution)/shard_map/ppermute | solution.py:861
  28.2 12.6 %collective-permute-start.3 = (f32[520,128]{1,0:T(8,128)S(1)}, f32[520,128]{1,0:T(8,128)S(1)}, u32[]{:S(2)}, u32[]{:S(2)}) collective-permute-start(f32[520,128]{1,0:T(8,128)S(1)} %get-tuple-element.78), channel_id=1, source_target_pairs={{0,2},{1,3},{2,0},{3,1},{4,6},{5,7},{6,4},{7,5},{8,10},{9,11},{10,... | collective-permute-start | bytes 798728 | tf_op jit(solution)/shard_map/ppermute | solution.py:861
  34.4 10.2 %collective-permute-start.6 = (f32[520,128]{1,0:T(8,128)S(1)}, f32[520,128]{1,0:T(8,128)S(1)}, u32[]{:S(2)}, u32[]{:S(2)}) collective-permute-start(f32[520,128]{1,0:T(8,128)S(1)} %get-tuple-element.85), channel_id=1, source_target_pairs={{0,2},{1,3},{2,0},{3,1},{4,6},{5,7},{6,4},{7,5},{8,10},{9,11},{10,... | collective-permute-start | bytes 798728 | tf_op jit(solution)/shard_map/ppermute | solution.py:861
  36.3 15.0 %collective-permute-start.7 = (f32[520,128]{1,0:T(8,128)S(1)}, f32[520,128]{1,0:T(8,128)S(1)}, u32[]{:S(2)}, u32[]{:S(2)}) collective-permute-start(f32[520,128]{1,0:T(8,128)S(1)} %get-tuple-element.71._), channel_id=1, source_target_pairs={{0,4},{1,5},{2,6},{3,7},{4,0},{5,1},{6,2},{7,3},{8,12},{9,13},{10,... | collective-permute-start | bytes 798728 | tf_op jit(solution)/shard_map/ppermute | solution.py:861
  40.0 11.4 %collective-permute-start.8 = (f32[520,128]{1,0:T(8,128)S(1)}, f32[520,128]{1,0:T(8,128)S(1)}, u32[]{:S(2)}, u32[]{:S(2)}) collective-permute-start(f32[520,128]{1,0:T(8,128)S(1)} %get-tuple-element.86), channel_id=1, source_target_pairs={{0,6},{1,7},{2,4},{3,5},{4,2},{5,3},{6,0},{7,1},{8,14},{9,15},{10,... | collective-permute-start | bytes 798728 | tf_op jit(solution)/shard_map/ppermute | solution.py:861
  41.9 13.7 %collective-permute-start.10 = (f32[520,128]{1,0:T(8,128)S(1)}, f32[520,128]{1,0:T(8,128)S(1)}, u32[]{:S(2)}, u32[]{:S(2)}) collective-permute-start(f32[520,128]{1,0:T(8,128)S(1)} %get-tuple-element.91), channel_id=1, source_target_pairs={{0,2},{1,3},{2,0},{3,1},{4,6},{5,7},{6,4},{7,5},{8,10},{9,11},{10,... | collective-permute-start | bytes 798728 | tf_op jit(solution)/shard_map/ppermute | solution.py:896
  43.8 14.2 %collective-permute-start.11 = (f32[520,128]{1,0:T(8,128)S(1)}, f32[520,128]{1,0:T(8,128)S(1)}, u32[]{:S(2)}, u32[]{:S(2)}) collective-permute-start(f32[520,128]{1,0:T(8,128)S(1)} %get-tuple-element.95), channel_id=1, source_target_pairs={{0,4},{1,5},{2,6},{3,7},{4,0},{5,1},{6,2},{7,3},{8,12},{9,13},{10,... | collective-permute-start | bytes 798728 | tf_op jit(solution)/shard_map/ppermute | solution.py:896
  44.7 17.2 %collective-permute-start.12 = (f32[520,128]{1,0:T(8,128)S(1)}, f32[520,128]{1,0:T(8,128)S(1)}, u32[]{:S(2)}, u32[]{:S(2)}) collective-permute-start(f32[520,128]{1,0:T(8,128)S(1)} %get-tuple-element.96), channel_id=1, source_target_pairs={{0,6},{1,7},{2,4},{3,5},{4,2},{5,3},{6,0},{7,1},{8,14},{9,15},{10,... | collective-permute-start | bytes 798728 | tf_op jit(solution)/shard_map/ppermute | solution.py:896
  63.1 5.5 %collective-permute-start.14 = (f32[2,256,256]{2,1,0:T(8,128)S(1)}, f32[2,256,256]{2,1,0:T(8,128)S(1)}, u32[]{:S(2)}, u32[]{:S(2)}) collective-permute-start(f32[2,256,256]{2,1,0:T(8,128)S(1)} %shard_map.92._), channel_id=1, source_target_pairs={{0,1},{1,0},{2,3},{3,2},{4,5},{5,4},{6,7},{7,6},{8,9},{9,8},{10,11... | collective-permute-start | bytes 1572872 | tf_op jit(solution)/shard_map/ppermute | solution.py:923
  63.1 5.4 %collective-permute-start.13 = (f32[2,256,256]{2,1,0:T(8,128)S(1)}, f32[2,256,256]{2,1,0:T(8,128)S(1)}, u32[]{:S(2)}, u32[]{:S(2)}) collective-permute-start(f32[2,256,256]{2,1,0:T(8,128)S(1)} %shard_map.90._), channel_id=1, source_target_pairs={{0,1},{1,0},{2,3},{3,2},{4,5},{5,4},{6,7},{7,6},{8,9},{9,8},{10,11... | collective-permute-start | bytes 1572872 | tf_op jit(solution)/shard_map/ppermute | solution.py:923
  63.6 9.3 %collective-permute-start.9 = (f32[520,128]{1,0:T(8,128)S(1)}, f32[520,128]{1,0:T(8,128)S(1)}, u32[]{:S(2)}, u32[]{:S(2)}) collective-permute-start(f32[520,128]{1,0:T(8,128)S(1)} %get-tuple-element.88), channel_id=1, source_target_pairs={{0,2},{1,3},{2,0},{3,1},{4,6},{5,7},{6,4},{7,5},{8,10},{9,11},{10,... | collective-permute-start | bytes 798728 | tf_op jit(solution)/shard_map/ppermute | solution.py:896
  64.4 13.8 %collective-permute-start.15 = (f32[520,128]{1,0:T(8,128)S(1)}, f32[520,128]{1,0:T(8,128)S(1)}, u32[]{:S(2)}, u32[]{:S(2)}) collective-permute-start(f32[520,128]{1,0:T(8,128)S(1)} %get-tuple-element.103), channel_id=1, source_target_pairs={{0,4},{1,5},{2,6},{3,7},{4,0},{5,1},{6,2},{7,3},{8,12},{9,13},{10,... | collective-permute-start | bytes 798728 | tf_op jit(solution)/shard_map/ppermute | solution.py:896
  65.2 12.9 %collective-permute-start.16 = (f32[520,128]{1,0:T(8,128)S(1)}, f32[520,128]{1,0:T(8,128)S(1)}, u32[]{:S(2)}, u32[]{:S(2)}) collective-permute-start(f32[520,128]{1,0:T(8,128)S(1)} %get-tuple-element.104), channel_id=1, source_target_pairs={{0,6},{1,7},{2,4},{3,5},{4,2},{5,3},{6,0},{7,1},{8,14},{9,15},{10,... | collective-permute-start | bytes 798728 | tf_op jit(solution)/shard_map/ppermute | solution.py:896
  79.4 2.0 %collective-permute-start.18 = (f32[2,256,256]{2,1,0:T(8,128)S(1)}, f32[2,256,256]{2,1,0:T(8,128)S(1)}, u32[]{:S(2)}, u32[]{:S(2)}) collective-permute-start(f32[2,256,256]{2,1,0:T(8,128)S(1)} %shard_map.97._), channel_id=1, source_target_pairs={{0,1},{1,0},{2,3},{3,2},{4,5},{5,4},{6,7},{7,6},{8,9},{9,8},{10,11... | collective-permute-start | bytes 1572872 | tf_op jit(solution)/shard_map/ppermute | solution.py:923
  79.4 2.6 %collective-permute-start.17 = (f32[2,256,256]{2,1,0:T(8,128)S(1)}, f32[2,256,256]{2,1,0:T(8,128)S(1)}, u32[]{:S(2)}, u32[]{:S(2)}) collective-permute-start(f32[2,256,256]{2,1,0:T(8,128)S(1)} %shard_map.95._), channel_id=1, source_target_pairs={{0,1},{1,0},{2,3},{3,2},{4,5},{5,4},{6,7},{7,6},{8,9},{9,8},{10,11... | collective-permute-start | bytes 1572872 | tf_op jit(solution)/shard_map/ppermute | solution.py:923
  85.6 3.7 %collective-permute-start.19 = (f32[2,256]{1,0:T(2,128)S(1)}, f32[2,256]{1,0:T(2,128)S(1)}, u32[]{:S(2)}, u32[]{:S(2)}) collective-permute-start(f32[2,256]{1,0:T(2,128)S(1)} %get-tuple-element.113), channel_id=1, source_target_pairs={{0,8},{8,0},{16,24},{24,16},{1,9},{9,1},{17,25},{25,17},{2,10},{10... | collective-permute-start | bytes 6152 | tf_op jit(solution)/shard_map/ppermute | solution.py:789
  89.3 4.5 %collective-permute-start.20 = (f32[2,256]{1,0:T(2,128)S(1)}, f32[2,256]{1,0:T(2,128)S(1)}, u32[]{:S(2)}, u32[]{:S(2)}) collective-permute-start(f32[2,256]{1,0:T(2,128)S(1)} %add.6), channel_id=1, source_target_pairs={{0,16},{8,24},{16,0},{24,8},{1,17},{9,25},{17,1},{25,9},{2,18},{10... | collective-permute-start | bytes 6152 | tf_op jit(solution)/shard_map/ppermute | solution.py:789

commit v4 on v3

--- a/solution.py
+++ b/solution.py
@@ -607,15 +607,15 @@
 
 def close_sweep_kernel(place_ref, index_ref, edge_ref, power_high, power_low, map_high, map_low, local_ref, base_ref,
                        near_ref, far_ref, _, out_ref, *refs, groups, group, part_of, second_pair):
-    image_ref, pair = refs if len(refs) == 2 else (None, refs[0])
+    image_ref = refs[0] if refs else None
     device = place_ref[0]
     chip, core = device // 2, device % 2
     side = core if image_ref is not None else 1 - core
-    pair[chip % 2] = near_ref[...]
-    pair[1 - chip % 2] = far_ref[...]
+    even = chip % 2 == 0
 
     def carried(start, count):
-        return jnp.concatenate([pair[0, start : start + count, :], pair[1, start : start + count, :]], axis=1)
+        near, far = near_ref[start : start + count, :], far_ref[start : start + count, :]
+        return jnp.concatenate([jnp.where(even, near, far), jnp.where(even, far, near)], axis=1)
 
     first = halves(carried(0, 2 * group))
     second = halves(carried(2 * group, 2 * group))
@@ -911,7 +911,6 @@
                     out_shape=outs,
                     in_specs=[smem()] * 2 + [vmem()] * 9 + [anywhere()],
                     out_specs=[vmem()] * len(outs),
-                    scratch_shapes=[pltpu.VMEM((2,) + piece.shape, f32)],
                     compiler_params=params(20),
                     cost_estimate=cost(groups * group * block * group * 12, 4 * groups * group * block * 2),
                 )(

time: 94.5 us -> 94.4 us (level)
  no operation moved by 1% of the time
where the time goes in v4:
time: 94.4 us; the launch traced here: 94.2 us
  Pallas kernels  48.7 us (52%)
  starting transfers between devices  26 us (28%)
  waiting for transfers between devices  17.8 us (19%)
    pallas_call x4, Pallas kernels, open_sweep(): pl.pallas_call(functools.partial(open_sweep_kernel, groups=groups, group=...  11.8 us
    ppermute x6, waiting for transfers between devices, fast_shards(): lax.ppermute(carries[offset], 'plane', moves)  10.4 us
    pallas_call x8, Pallas kernels, fast_shards(): pl.pallas_call(functools.partial(close_sweep_kernel, groups=groups, group...  9.63 us
    ppermute x6, starting transfers between devices, fast_shards(): lax.ppermute(carries[offset], 'plane', moves)  7.91 us
    pallas_call x2, Pallas kernels, last_pass(): pl.pallas_call(functools.partial(last_pass_kernel, half=half, step=step,...  7.27 us
    ppermute x6, starting transfers between devices, open_sweep(): lax.ppermute(item, 'plane', moves)  7.18 us
    pallas_call x2, Pallas kernels, first_pass(): pl.pallas_call(functools.partial(first_pass_kernel, half=half, group=grou...  6.58 us
    ppermute x2, starting transfers between devices, first(): come[half] = lax.ppermute(send, 'plane', partner)  4.83 us
  transfers between devices with their start and end apart: 21, of which 10 were waited for; matrix products, arithmetic and copies ran while one was open for 0% of the time, Pallas kernels for 34%

profile of v4, /device:TPU:0, one launch (start us, length us, event | category | flops | bytes accessed | tf_op | source)
XLA Modules:
  0.0 94.2 jit_solution(7222656903389552647)
XLA Ops:
  0.7 1.6 %shard_map.79 = f32[1,2,1,2048]{3,2,1,0:T(1,128)} custom-call(s32[1]{0:T(128)} %bitcast.place_ref, f32[1,2,256,2048]{3,2,1,0:T(8,128)} %beside_ref.3), custom_call_target="tpu_custom_call" | custom-call | flops 20000000000 | bytes 1048576 | tf_op jit(solution)/shard_map/pallas_call | solution.py:285
  3.1 1.9 %shard_map.77 = (bf16[9,256,256]{2,1,0:T(8,128)(2,1)S(1)}, bf16[9,256,256]{2,1,0:T(8,128)(2,1)S(1)}, f32[8,4,256]{2,1,0:T(4,128)S(1)}) custom-call(f32[1,8,2]{2,1,0:T(8,128)S(1)} %copy.9.rhs_ref, f32[8,2,128,128]{3,2,1,0:T(8,128)S(1)} %bitcast.3, f32[2,128,128]{2,1,0:T(8,128)S(1)} %bitcast.5), custom_call_target="tpu_custom_call" | custom-call | flops 20000000000 | bytes 4194304 | tf_op jit(solution)/shard_map/pallas_call | solution.py:262
  5.3 3.2 %shard_map.80 = (f32[264,256]{1,0:T(8,128)S(1)}, f32[2,2,264,256]{3,2,1,0:T(8,128)S(1)}, f32[2,2,264,256]{3,2,1,0:T(8,128)S(1)}) custom-call(s32[1]{0:T(128)} %bitcast.place_ref, s32[2,16]{1,0:T(2,128)S(1)} %copy-done.2, f32[1,2,256,2048]{3,2,1,0:T(8,128)S(1)} %copy-done, f32[1,2,256,2048]{3,2,1,0:T(8,128)S(1)} %copy-done, ...), custom_call_target="tpu_custom_call" | custom-call | flops 1660944384 | bytes 4325376 | tf_op jit(solution)/shard_map/pallas_call | solution.py:388
  8.5 4.4 %collective-permute-start.1 = (f32[2,2,264,256]{3,2,1,0:T(8,128)S(1)}, f32[2,2,264,256]{3,2,1,0:T(8,128)S(1)}, u32[]{:S(2)}, u32[]{:S(2)}) collective-permute-start(f32[2,2,264,256]{3,2,1,0:T(8,128)S(1)} %get-tuple-element.66), channel_id=1, source_target_pairs={{0,1},{1,0},{2,3},{3,2},{4,5},{5,4},{6,7},{7,6},{8,9},{9,8},{10,11... | collective-permute-start | bytes 3244040 | tf_op jit(solution)/shard_map/ppermute | solution.py:839
  12.9 1.9 %shard_map.78 = (bf16[9,256,256]{2,1,0:T(8,128)(2,1)S(1)}, bf16[9,256,256]{2,1,0:T(8,128)(2,1)S(1)}, f32[8,2,256,128]{3,2,1,0:T(8,128)S(1)}) custom-call(f32[1,8,2]{2,1,0:T(8,128)S(1)} %copy.9.rhs_ref, f32[8,2,128,128]{3,2,1,0:T(8,128)S(1)} %bitcast.4, f32[2,128,128]{2,1,0:T(8,128)S(1)} %bitcast.6), custom_call_target="tpu_custom_call" | custom-call | flops 20000000000 | bytes 4194304 | tf_op jit(solution)/shard_map/pallas_call | solution.py:262
  15.2 2.9 %shard_map.81 = (f32[520,128]{1,0:T(8,128)S(1)}, f32[520,128]{1,0:T(8,128)S(1)}, f32[4,256,256]{2,1,0:T(8,128)S(1)}, f32[2,2,128,128]{3,2,1,0:T(8,128)S(1)}) custom-call(s32[1]{0:T(128)} %bitcast.place_ref, s32[2,16]{1,0:T(2,128)S(1)} %copy-done.1, bf16[9,256,256]{2,1,0:T(8,128)(2,1)S(1)} %get-tuple-element.62.high_ref, ...), custom_call_target="tpu_custom_call" | custom-call | flops 1610612736 | bytes 3145728 | tf_op jit(solution)/shard_map/pallas_call | solution.py:852
  18.1 3.4 %shard_map.82 = (f32[2,2,264,256]{3,2,1,0:T(8,128)S(1)}, f32[2,2,264,256]{3,2,1,0:T(8,128)S(1)}) custom-call(s32[1]{0:T(128)} %bitcast.place_ref, s32[2,16]{1,0:T(2,128)S(1)} %copy-done.2, f32[1,2,256,2048]{3,2,1,0:T(8,128)S(1)} %copy-done, f32[1,2,256,2048]{3,2,1,0:T(8,128)S(1)} %copy-done, f32[1,2,1,2048]{3,2,1,0:T(1,128)S(1)} %collective-permute-done.halo_ref, ...), custom_call_target="tpu_custom_call" | custom-call | flops 1660944384 | bytes 4325376 | tf_op jit(solution)/shard_map/pallas_call | solution.py:388
  22.0 2.0 %collective-permute-start.4 = (f32[520,128]{1,0:T(8,128)S(1)}, f32[520,128]{1,0:T(8,128)S(1)}, u32[]{:S(2)}, u32[]{:S(2)}) collective-permute-start(f32[520,128]{1,0:T(8,128)S(1)} %get-tuple-element.67.refs_1_), channel_id=1, source_target_pairs={{0,4},{1,5},{2,6},{3,7},{4,0},{5,1},{6,2},{7,3},{8,12},{9,13},{10,... | collective-permute-start | bytes 798728 | tf_op jit(solution)/shard_map/ppermute | solution.py:861
  24.0 1.3 %collective-permute-start.5 = (f32[520,128]{1,0:T(8,128)S(1)}, f32[520,128]{1,0:T(8,128)S(1)}, u32[]{:S(2)}, u32[]{:S(2)}) collective-permute-start(f32[520,128]{1,0:T(8,128)S(1)} %get-tuple-element.79), channel_id=1, source_target_pairs={{0,6},{1,7},{2,4},{3,5},{4,2},{5,3},{6,0},{7,1},{8,14},{9,15},{10,... | collective-permute-start | bytes 798728 | tf_op jit(solution)/shard_map/ppermute | solution.py:861
  25.2 2.9 %shard_map.83 = (f32[520,128]{1,0:T(8,128)S(1)}, f32[520,128]{1,0:T(8,128)S(1)}, f32[4,256,256]{2,1,0:T(8,128)S(1)}, f32[2,2,128,128]{3,2,1,0:T(8,128)S(1)}) custom-call(s32[1]{0:T(128)} %bitcast.place_ref, s32[2,16]{1,0:T(2,128)S(1)} %copy-done.1, bf16[9,256,256]{2,1,0:T(8,128)(2,1)S(1)} %get-tuple-element.62.high_ref, ...), custom_call_target="tpu_custom_call" | custom-call | flops 1610612736 | bytes 3145728 | tf_op jit(solution)/shard_map/pallas_call | solution.py:852
  28.4 3.1 %shard_map.84 = (f32[520,128]{1,0:T(8,128)S(1)}, f32[520,128]{1,0:T(8,128)S(1)}, f32[4,256,256]{2,1,0:T(8,128)S(1)}, f32[2,2,128,128]{3,2,1,0:T(8,128)S(1)}) custom-call(s32[1]{0:T(128)} %bitcast.place_ref, s32[2,16]{1,0:T(2,128)S(1)} %copy-done.1, bf16[9,256,256]{2,1,0:T(8,128)(2,1)S(1)} %get-tuple-element.62.high_ref, ...), custom_call_target="tpu_custom_call" | custom-call | flops 1610612736 | bytes 3145728 | tf_op jit(solution)/shard_map/pallas_call | solution.py:852
  31.5 2.9 %shard_map.85 = (f32[520,128]{1,0:T(8,128)S(1)}, f32[520,128]{1,0:T(8,128)S(1)}, f32[4,256,256]{2,1,0:T(8,128)S(1)}, f32[2,2,128,128]{3,2,1,0:T(8,128)S(1)}) custom-call(s32[1]{0:T(128)} %bitcast.place_ref, s32[2,16]{1,0:T(2,128)S(1)} %copy-done.1, bf16[9,256,256]{2,1,0:T(8,128)(2,1)S(1)} %get-tuple-element.62.high_ref, ...), custom_call_target="tpu_custom_call" | custom-call | flops 1610612736 | bytes 3145728 | tf_op jit(solution)/shard_map/pallas_call | solution.py:852
  34.4 1.9 %collective-permute-start.6 = (f32[520,128]{1,0:T(8,128)S(1)}, f32[520,128]{1,0:T(8,128)S(1)}, u32[]{:S(2)}, u32[]{:S(2)}) collective-permute-start(f32[520,128]{1,0:T(8,128)S(1)} %get-tuple-element.85), channel_id=1, source_target_pairs={{0,2},{1,3},{2,0},{3,1},{4,6},{5,7},{6,4},{7,5},{8,10},{9,11},{10,... | collective-permute-start | bytes 798728 | tf_op jit(solution)/shard_map/ppermute | solution.py:861
  37.2 2.7 %shard_map.86 = (bf16[4,256,256]{2,1,0:T(8,128)(2,1)S(1)}, bf16[4,256,256]{2,1,0:T(8,128)(2,1)S(1)}, f32[4,128,256]{2,1,0:T(8,128)S(1)}, bf16[2,256,256]{2,1,0:T(8,128)(2,1)S(1)}, bf16[2,256,256]{2,1,0:T(8,128)(2,1)S(1)}) custom-call(s32[2,16]{1,0:T(2,128)S(1)} %copy-done.1, bf16[9,256,256]{2,1,0:T(8,128)(2,1)S(1)} %get-tuple-element.58.high_ref, ...), custom_call_target="tpu_custom_call" | custom-call | flops 1073741824 | bytes 4194304 | tf_op jit(solution)/shard_map/pallas_call | solution.py:822
  41.9 1.9 %collective-permute-start.10 = (f32[520,128]{1,0:T(8,128)S(1)}, f32[520,128]{1,0:T(8,128)S(1)}, u32[]{:S(2)}, u32[]{:S(2)}) collective-permute-start(f32[520,128]{1,0:T(8,128)S(1)} %get-tuple-element.91), channel_id=1, source_target_pairs={{0,2},{1,3},{2,0},{3,1},{4,6},{5,7},{6,4},{7,5},{8,10},{9,11},{10,... | collective-permute-start | bytes 798728 | tf_op jit(solution)/shard_map/ppermute | solution.py:896
  44.7 1.6 %collective-permute-start.12 = (f32[520,128]{1,0:T(8,128)S(1)}, f32[520,128]{1,0:T(8,128)S(1)}, u32[]{:S(2)}, u32[]{:S(2)}) collective-permute-start(f32[520,128]{1,0:T(8,128)S(1)} %get-tuple-element.96), channel_id=1, source_target_pairs={{0,6},{1,7},{2,4},{3,5},{4,2},{5,3},{6,0},{7,1},{8,14},{9,15},{10,... | collective-permute-start | bytes 798728 | tf_op jit(solution)/shard_map/ppermute | solution.py:896
  46.3 1.6 %shard_map.88 = (bf16[4,256,256]{2,1,0:T(8,128)(2,1)S(1)}, bf16[4,256,256]{2,1,0:T(8,128)(2,1)S(1)}) custom-call(s32[1]{0:T(128)} %bitcast.place_ref, s32[2,16]{1,0:T(2,128)S(1)} %copy-done.1, bf16[9,256,256]{2,1,0:T(8,128)(2,1)S(1)} %get-tuple-element.58.high_ref, bf16[9,256,256]{2,1,0:T(8,128)(2,1)S(1)} %get-tuple-element.59.low_ref, ...), custom_call_target="tpu_custom_call" | custom-call | flops 536870912 | bytes 4194304 | tf_op jit(solution)/shard_map/pallas_call | solution.py:885
  47.9 3.4 %collective-permute-done.8.refs_3_ = f32[520,128]{1,0:T(8,128)S(1)} collective-permute-done((f32[520,128]{1,0:T(8,128)S(1)}, f32[520,128]{1,0:T(8,128)S(1)}, u32[]{:S(2)}, u32[]{:S(2)}) %collective-permute-start.8) | collective-permute-done | bytes 266272 | tf_op jit(solution)/shard_map/ppermute | solution.py:861
  52.4 3.2 %collective-permute-done.10.far_ref = f32[520,128]{1,0:T(8,128)S(1)} collective-permute-done((f32[520,128]{1,0:T(8,128)S(1)}, f32[520,128]{1,0:T(8,128)S(1)}, u32[]{:S(2)}, u32[]{:S(2)}) %collective-permute-start.10) | collective-permute-done | bytes 266272 | tf_op jit(solution)/shard_map/ppermute | solution.py:896
  56.8 1.2 %shard_map.91 = (f32[2,256,256]{2,1,0:T(8,128)S(1)}, f32[1,256]{1,0:T(1,128)S(1)}) custom-call(s32[1]{0:T(128)} %bitcast.place_ref, s32[2,16]{1,0:T(2,128)S(1)} %copy-done.1, f32[8,2,256,128]{3,2,1,0:T(8,128)S(1)} %get-tuple-element.61.edge_ref, bf16[4,256,256]{2,1,0:T(8,128)(2,1)S(1)} %get-tuple-element.73.power_high.refs_4_, ...), custom_call_target="tpu_custom_call" | custom-call | flops 402653184 | bytes 1048576 | tf_op jit(solution)/shard_map/pallas_call | solution.py:907
  57.9 4.0 %collective-permute-done.12.far_ref = f32[520,128]{1,0:T(8,128)S(1)} collective-permute-done((f32[520,128]{1,0:T(8,128)S(1)}, f32[520,128]{1,0:T(8,128)S(1)}, u32[]{:S(2)}, u32[]{:S(2)}) %collective-permute-start.12) | collective-permute-done | bytes 266272 | tf_op jit(solution)/shard_map/ppermute | solution.py:896
  65.2 1.9 %collective-permute-start.16 = (f32[520,128]{1,0:T(8,128)S(1)}, f32[520,128]{1,0:T(8,128)S(1)}, u32[]{:S(2)}, u32[]{:S(2)}) collective-permute-start(f32[520,128]{1,0:T(8,128)S(1)} %get-tuple-element.104), channel_id=1, source_target_pairs={{0,6},{1,7},{2,4},{3,5},{4,2},{5,3},{6,0},{7,1},{8,14},{9,15},{10,... | collective-permute-start | bytes 798728 | tf_op jit(solution)/shard_map/ppermute | solution.py:896
  67.1 1.4 %shard_map.93 = (f32[2,256,256]{2,1,0:T(8,128)S(1)}, f32[1,256]{1,0:T(1,128)S(1)}) custom-call(s32[1]{0:T(128)} %bitcast.place_ref, s32[2,16]{1,0:T(2,128)S(1)} %copy-done.1, f32[8,2,256,128]{3,2,1,0:T(8,128)S(1)} %get-tuple-element.61.edge_ref, bf16[4,256,256]{2,1,0:T(8,128)(2,1)S(1)} %get-tuple-element.73.power_high.refs_4_, ...), custom_call_target="tpu_custom_call" | custom-call | flops 402653184 | bytes 1048576 | tf_op jit(solution)/shard_map/pallas_call | solution.py:907
  68.5 3.8 %shard_map.94 = (f32[1,2,256,2048]{3,2,1,0:T(8,128)}, f32[256,256]{1,0:T(8,128)S(1)}, f32[2,256,128]{2,1,0:T(8,128)S(1)}, f32[1,256]{1,0:T(1,128)S(1)}) custom-call(s32[1]{0:T(128)} %bitcast.place_ref, s32[2,16]{1,0:T(2,128)S(1)} %copy-done.2, bf16[9,256,256]{2,1,0:T(8,128)(2,1)S(1)} %get-tuple-element.58.high_ref, ...), custom_call_target="tpu_custom_call" | custom-call | flops 1610612736 | bytes 4194304 | tf_op jit(solution)/shard_map/pallas_call | solution.py:750
  74.0 1.4 %shard_map.96 = (f32[2,256,256]{2,1,0:T(8,128)S(1)}, f32[1,256]{1,0:T(1,128)S(1)}) custom-call(s32[1]{0:T(128)} %bitcast.place_ref, s32[2,16]{1,0:T(2,128)S(1)} %copy-done.1, f32[8,2,256,128]{3,2,1,0:T(8,128)S(1)} %get-tuple-element.61.edge_ref, bf16[4,256,256]{2,1,0:T(8,128)(2,1)S(1)} %get-tuple-element.73.power_high.refs_4_, ...), custom_call_target="tpu_custom_call" | custom-call | flops 402653184 | bytes 1048576 | tf_op jit(solution)/shard_map/pallas_call | solution.py:907
  75.4 2.7 %collective-permute-done.15.near_ref = f32[520,128]{1,0:T(8,128)S(1)} collective-permute-done((f32[520,128]{1,0:T(8,128)S(1)}, f32[520,128]{1,0:T(8,128)S(1)}, u32[]{:S(2)}, u32[]{:S(2)}) %collective-permute-start.15) | collective-permute-done | bytes 266272 | tf_op jit(solution)/shard_map/ppermute | solution.py:896
  79.9 1.1 %shard_map.98 = (f32[2,256,256]{2,1,0:T(8,128)S(1)}, f32[1,256]{1,0:T(1,128)S(1)}) custom-call(s32[1]{0:T(128)} %bitcast.place_ref, s32[2,16]{1,0:T(2,128)S(1)} %copy-done.1, f32[8,2,256,128]{3,2,1,0:T(8,128)S(1)} %get-tuple-element.61.edge_ref, bf16[4,256,256]{2,1,0:T(8,128)(2,1)S(1)} %get-tuple-element.73.power_high.refs_4_, ...), custom_call_target="tpu_custom_call" | custom-call | flops 402653184 | bytes 1048576 | tf_op jit(solution)/shard_map/pallas_call | solution.py:907
  82.0 3.5 %shard_map.99 = (f32[9,2,256,128]{3,2,1,0:T(8,128)S(1)}, f32[2,256]{1,0:T(2,128)S(1)}) custom-call(s32[1]{0:T(128)} %bitcast.place_ref, s32[2,16]{1,0:T(2,128)S(1)} %copy-done.2, bf16[9,256,256]{2,1,0:T(8,128)(2,1)S(1)} %get-tuple-element.58.high_ref, bf16[9,256,256]{2,1,0:T(8,128)(2,1)S(1)} %get-tuple-element.59.low_ref, ...), custom_call_target="tpu_custom_call" | custom-call | flops 1610612736 | bytes 4194304 | tf_op jit(solution)/shard_map/pallas_call | solution.py:750
  85.5 1.6 %collective-permute-start.19 = (f32[2,256]{1,0:T(2,128)S(1)}, f32[2,256]{1,0:T(2,128)S(1)}, u32[]{:S(2)}, u32[]{:S(2)}) collective-permute-start(f32[2,256]{1,0:T(2,128)S(1)} %get-tuple-element.113), channel_id=1, source_target_pairs={{0,8},{8,0},{16,24},{24,16},{1,9},{9,1},{17,25},{25,17},{2,10},{10... | collective-permute-start | bytes 6152 | tf_op jit(solution)/shard_map/ppermute | solution.py:789
  87.2 2.0 %collective-permute-done.19 = f32[2,256]{1,0:T(2,128)S(1)} collective-permute-done((f32[2,256]{1,0:T(2,128)S(1)}, f32[2,256]{1,0:T(2,128)S(1)}, u32[]{:S(2)}, u32[]{:S(2)}) %collective-permute-start.19) | collective-permute-done | bytes 2080 | tf_op jit(solution)/shard_map/ppermute | solution.py:789
  89.2 2.6 %collective-permute-start.20 = (f32[2,256]{1,0:T(2,128)S(1)}, f32[2,256]{1,0:T(2,128)S(1)}, u32[]{:S(2)}, u32[]{:S(2)}) collective-permute-start(f32[2,256]{1,0:T(2,128)S(1)} %add.6), channel_id=1, source_target_pairs={{0,16},{8,24},{16,0},{24,8},{1,17},{9,25},{17,1},{25,9},{2,18},{10... | collective-permute-start | bytes 6152 | tf_op jit(solution)/shard_map/ppermute | solution.py:789
  91.8 1.5 %shard_map.100 = f32[1,2,256,2048]{3,2,1,0:T(8,128)} custom-call(f32[9,2,256,128]{3,2,1,0:T(8,128)S(1)} %get-tuple-element.111.groups_ref, f32[1,2,256,2048]{3,2,1,0:T(8,128)} %get-tuple-element.112._), custom_call_target="tpu_custom_call", output_to_operand_aliasing={{}: (1, {})} | custom-call | bytes 8388608 | tf_op jit(solution)/shard_map/pallas_call | solution.py:774
  (49 shorter events, 17.0 us)
Async XLA Ops:
  0.6 2.3 %copy-start.5 = (f32[1,8,2]{1,2,0:T(2,128)S(1)}, f32[1,8,2]{1,2,0:T(2,128)}, u32[]{:S(2)}) copy-start(f32[1,8,2]{1,2,0:T(2,128)} %param.9) | copy-start | bytes 196
  0.6 2.4 %copy-start.3 = (f32[1,8,2,128,128]{4,3,2,1,0:T(8,128)S(1)}, f32[1,8,2,128,128]{4,3,2,1,0:T(8,128)}, u32[]{:S(2)}) copy-start(f32[1,8,2,128,128]{4,3,2,1,0:T(8,128)} %param.7) | copy-start | bytes 3145732
  0.7 2.4 %copy-start.4 = (f32[1,2,128,128]{3,2,1,0:T(8,128)S(1)}, f32[1,2,128,128]{3,2,1,0:T(8,128)}, u32[]{:S(2)}) copy-start(f32[1,2,128,128]{3,2,1,0:T(8,128)} %param.8) | copy-start | bytes 393220
  2.3 2.7 %collective-permute-start = (f32[1,2,1,2048]{3,2,1,0:T(1,128)}, f32[1,2,1,2048]{3,2,1,0:T(1,128)S(1)}, u32[]{:S(2)}, u32[]{:S(2)}) collective-permute-start(f32[1,2,1,2048]{3,2,1,0:T(1,128)} %shard_map.79), channel_id=1, source_target_pairs={{1,2},{3,4},{5,6},{2,1},{4,3},{6,5},{9,10},{11,12},{13,14},{10,9},... | collective-permute-start | bytes 49160 | tf_op jit(solution)/shard_map/ppermute | solution.py:807
  3.1 2.2 %copy-start = (f32[1,2,256,2048]{3,2,1,0:T(8,128)S(1)}, f32[1,2,256,2048]{3,2,1,0:T(8,128)}, u32[]{:S(2)}) copy-start(f32[1,2,256,2048]{3,2,1,0:T(8,128)} %beside_ref.3) | copy-start | bytes 12582916
  3.1 2.2 %copy-start.2 = (s32[2,16]{1,0:T(2,128)S(1)}, s32[2,16]{1,0:T(2,128)}, u32[]{:S(2)}) copy-start(s32[2,16]{1,0:T(2,128)} %index_ref.35) | copy-start | bytes 388
  8.5 6.7 %copy-start.1 = (s32[2,16]{1,0:T(2,128)S(1)}, s32[2,16]{1,0:T(2,128)}, u32[]{:S(2)}) copy-start(s32[2,16]{1,0:T(2,128)} %index_ref.34) | copy-start | bytes 388
  8.5 6.7 %collective-permute-start.1 = (f32[2,2,264,256]{3,2,1,0:T(8,128)S(1)}, f32[2,2,264,256]{3,2,1,0:T(8,128)S(1)}, u32[]{:S(2)}, u32[]{:S(2)}) collective-permute-start(f32[2,2,264,256]{3,2,1,0:T(8,128)S(1)} %get-tuple-element.66), channel_id=1, source_target_pairs={{0,1},{1,0},{2,3},{3,2},{4,5},{5,4},{6,7},{7,6},{8,9},{9,8},{10,11... | collective-permute-start | bytes 3244040 | tf_op jit(solution)/shard_map/ppermute | solution.py:839
  21.5 6.9 %collective-permute-start.2 = (f32[2,2,264,256]{3,2,1,0:T(8,128)S(1)}, f32[2,2,264,256]{3,2,1,0:T(8,128)S(1)}, u32[]{:S(2)}, u32[]{:S(2)}) collective-permute-start(f32[2,2,264,256]{3,2,1,0:T(8,128)S(1)} %get-tuple-element.69), channel_id=1, source_target_pairs={{0,1},{1,0},{2,3},{3,2},{4,5},{5,4},{6,7},{7,6},{8,9},{9,8},{10,11... | collective-permute-start | bytes 3244040 | tf_op jit(solution)/shard_map/ppermute | solution.py:839
  22.0 18.8 %collective-permute-start.4 = (f32[520,128]{1,0:T(8,128)S(1)}, f32[520,128]{1,0:T(8,128)S(1)}, u32[]{:S(2)}, u32[]{:S(2)}) collective-permute-start(f32[520,128]{1,0:T(8,128)S(1)} %get-tuple-element.67.refs_1_), channel_id=1, source_target_pairs={{0,4},{1,5},{2,6},{3,7},{4,0},{5,1},{6,2},{7,3},{8,12},{9,13},{10,... | collective-permute-start | bytes 798728 | tf_op jit(solution)/shard_map/ppermute | solution.py:861
  24.0 16.0 %collective-permute-start.5 = (f32[520,128]{1,0:T(8,128)S(1)}, f32[520,128]{1,0:T(8,128)S(1)}, u32[]{:S(2)}, u32[]{:S(2)}) collective-permute-start(f32[520,128]{1,0:T(8,128)S(1)} %get-tuple-element.79), channel_id=1, source_target_pairs={{0,6},{1,7},{2,4},{3,5},{4,2},{5,3},{6,0},{7,1},{8,14},{9,15},{10,... | collective-permute-start | bytes 798728 | tf_op jit(solution)/shard_map/ppermute | solution.py:861
  28.2 12.6 %collective-permute-start.3 = (f32[520,128]{1,0:T(8,128)S(1)}, f32[520,128]{1,0:T(8,128)S(1)}, u32[]{:S(2)}, u32[]{:S(2)}) collective-permute-start(f32[520,128]{1,0:T(8,128)S(1)} %get-tuple-element.78), channel_id=1, source_target_pairs={{0,2},{1,3},{2,0},{3,1},{4,6},{5,7},{6,4},{7,5},{8,10},{9,11},{10,... | collective-permute-start | bytes 798728 | tf_op jit(solution)/shard_map/ppermute | solution.py:861
  34.4 10.2 %collective-permute-start.6 = (f32[520,128]{1,0:T(8,128)S(1)}, f32[520,128]{1,0:T(8,128)S(1)}, u32[]{:S(2)}, u32[]{:S(2)}) collective-permute-start(f32[520,128]{1,0:T(8,128)S(1)} %get-tuple-element.85), channel_id=1, source_target_pairs={{0,2},{1,3},{2,0},{3,1},{4,6},{5,7},{6,4},{7,5},{8,10},{9,11},{10,... | collective-permute-start | bytes 798728 | tf_op jit(solution)/shard_map/ppermute | solution.py:861
  36.3 15.0 %collective-permute-start.7 = (f32[520,128]{1,0:T(8,128)S(1)}, f32[520,128]{1,0:T(8,128)S(1)}, u32[]{:S(2)}, u32[]{:S(2)}) collective-permute-start(f32[520,128]{1,0:T(8,128)S(1)} %get-tuple-element.71._), channel_id=1, source_target_pairs={{0,4},{1,5},{2,6},{3,7},{4,0},{5,1},{6,2},{7,3},{8,12},{9,13},{10,... | collective-permute-start | bytes 798728 | tf_op jit(solution)/shard_map/ppermute | solution.py:861
  40.0 11.4 %collective-permute-start.8 = (f32[520,128]{1,0:T(8,128)S(1)}, f32[520,128]{1,0:T(8,128)S(1)}, u32[]{:S(2)}, u32[]{:S(2)}) collective-permute-start(f32[520,128]{1,0:T(8,128)S(1)} %get-tuple-element.86), channel_id=1, source_target_pairs={{0,6},{1,7},{2,4},{3,5},{4,2},{5,3},{6,0},{7,1},{8,14},{9,15},{10,... | collective-permute-start | bytes 798728 | tf_op jit(solution)/shard_map/ppermute | solution.py:861
  41.9 13.7 %collective-permute-start.10 = (f32[520,128]{1,0:T(8,128)S(1)}, f32[520,128]{1,0:T(8,128)S(1)}, u32[]{:S(2)}, u32[]{:S(2)}) collective-permute-start(f32[520,128]{1,0:T(8,128)S(1)} %get-tuple-element.91), channel_id=1, source_target_pairs={{0,2},{1,3},{2,0},{3,1},{4,6},{5,7},{6,4},{7,5},{8,10},{9,11},{10,... | collective-permute-start | bytes 798728 | tf_op jit(solution)/shard_map/ppermute | solution.py:896
  43.8 14.2 %collective-permute-start.11 = (f32[520,128]{1,0:T(8,128)S(1)}, f32[520,128]{1,0:T(8,128)S(1)}, u32[]{:S(2)}, u32[]{:S(2)}) collective-permute-start(f32[520,128]{1,0:T(8,128)S(1)} %get-tuple-element.95), channel_id=1, source_target_pairs={{0,4},{1,5},{2,6},{3,7},{4,0},{5,1},{6,2},{7,3},{8,12},{9,13},{10,... | collective-permute-start | bytes 798728 | tf_op jit(solution)/shard_map/ppermute | solution.py:896
  44.7 17.2 %collective-permute-start.12 = (f32[520,128]{1,0:T(8,128)S(1)}, f32[520,128]{1,0:T(8,128)S(1)}, u32[]{:S(2)}, u32[]{:S(2)}) collective-permute-start(f32[520,128]{1,0:T(8,128)S(1)} %get-tuple-element.96), channel_id=1, source_target_pairs={{0,6},{1,7},{2,4},{3,5},{4,2},{5,3},{6,0},{7,1},{8,14},{9,15},{10,... | collective-permute-start | bytes 798728 | tf_op jit(solution)/shard_map/ppermute | solution.py:896
  63.0 5.4 %collective-permute-start.14 = (f32[2,256,256]{2,1,0:T(8,128)S(1)}, f32[2,256,256]{2,1,0:T(8,128)S(1)}, u32[]{:S(2)}, u32[]{:S(2)}) collective-permute-start(f32[2,256,256]{2,1,0:T(8,128)S(1)} %shard_map.92._), channel_id=1, source_target_pairs={{0,1},{1,0},{2,3},{3,2},{4,5},{5,4},{6,7},{7,6},{8,9},{9,8},{10,11... | collective-permute-start | bytes 1572872 | tf_op jit(solution)/shard_map/ppermute | solution.py:922
  63.1 5.4 %collective-permute-start.13 = (f32[2,256,256]{2,1,0:T(8,128)S(1)}, f32[2,256,256]{2,1,0:T(8,128)S(1)}, u32[]{:S(2)}, u32[]{:S(2)}) collective-permute-start(f32[2,256,256]{2,1,0:T(8,128)S(1)} %shard_map.90._), channel_id=1, source_target_pairs={{0,1},{1,0},{2,3},{3,2},{4,5},{5,4},{6,7},{7,6},{8,9},{9,8},{10,11... | collective-permute-start | bytes 1572872 | tf_op jit(solution)/shard_map/ppermute | solution.py:922
  63.6 9.3 %collective-permute-start.9 = (f32[520,128]{1,0:T(8,128)S(1)}, f32[520,128]{1,0:T(8,128)S(1)}, u32[]{:S(2)}, u32[]{:S(2)}) collective-permute-start(f32[520,128]{1,0:T(8,128)S(1)} %get-tuple-element.88), channel_id=1, source_target_pairs={{0,2},{1,3},{2,0},{3,1},{4,6},{5,7},{6,4},{7,5},{8,10},{9,11},{10,... | collective-permute-start | bytes 798728 | tf_op jit(solution)/shard_map/ppermute | solution.py:896
  64.3 13.8 %collective-permute-start.15 = (f32[520,128]{1,0:T(8,128)S(1)}, f32[520,128]{1,0:T(8,128)S(1)}, u32[]{:S(2)}, u32[]{:S(2)}) collective-permute-start(f32[520,128]{1,0:T(8,128)S(1)} %get-tuple-element.103), channel_id=1, source_target_pairs={{0,4},{1,5},{2,6},{3,7},{4,0},{5,1},{6,2},{7,3},{8,12},{9,13},{10,... | collective-permute-start | bytes 798728 | tf_op jit(solution)/shard_map/ppermute | solution.py:896
  65.2 12.9 %collective-permute-start.16 = (f32[520,128]{1,0:T(8,128)S(1)}, f32[520,128]{1,0:T(8,128)S(1)}, u32[]{:S(2)}, u32[]{:S(2)}) collective-permute-start(f32[520,128]{1,0:T(8,128)S(1)} %get-tuple-element.104), channel_id=1, source_target_pairs={{0,6},{1,7},{2,4},{3,5},{4,2},{5,3},{6,0},{7,1},{8,14},{9,15},{10,... | collective-permute-start | bytes 798728 | tf_op jit(solution)/shard_map/ppermute | solution.py:896
  79.3 2.0 %collective-permute-start.18 = (f32[2,256,256]{2,1,0:T(8,128)S(1)}, f32[2,256,256]{2,1,0:T(8,128)S(1)}, u32[]{:S(2)}, u32[]{:S(2)}) collective-permute-start(f32[2,256,256]{2,1,0:T(8,128)S(1)} %shard_map.97._), channel_id=1, source_target_pairs={{0,1},{1,0},{2,3},{3,2},{4,5},{5,4},{6,7},{7,6},{8,9},{9,8},{10,11... | collective-permute-start | bytes 1572872 | tf_op jit(solution)/shard_map/ppermute | solution.py:922
  79.4 2.6 %collective-permute-start.17 = (f32[2,256,256]{2,1,0:T(8,128)S(1)}, f32[2,256,256]{2,1,0:T(8,128)S(1)}, u32[]{:S(2)}, u32[]{:S(2)}) collective-permute-start(f32[2,256,256]{2,1,0:T(8,128)S(1)} %shard_map.95._), channel_id=1, source_target_pairs={{0,1},{1,0},{2,3},{3,2},{4,5},{5,4},{6,7},{7,6},{8,9},{9,8},{10,11... | collective-permute-start | bytes 1572872 | tf_op jit(solution)/shard_map/ppermute | solution.py:922
  85.5 3.7 %collective-permute-start.19 = (f32[2,256]{1,0:T(2,128)S(1)}, f32[2,256]{1,0:T(2,128)S(1)}, u32[]{:S(2)}, u32[]{:S(2)}) collective-permute-start(f32[2,256]{1,0:T(2,128)S(1)} %get-tuple-element.113), channel_id=1, source_target_pairs={{0,8},{8,0},{16,24},{24,16},{1,9},{9,1},{17,25},{25,17},{2,10},{10... | collective-permute-start | bytes 6152 | tf_op jit(solution)/shard_map/ppermute | solution.py:789
  89.2 4.5 %collective-permute-start.20 = (f32[2,256]{1,0:T(2,128)S(1)}, f32[2,256]{1,0:T(2,128)S(1)}, u32[]{:S(2)}, u32[]{:S(2)}) collective-permute-start(f32[2,256]{1,0:T(2,128)S(1)} %add.6), channel_id=1, source_target_pairs={{0,16},{8,24},{16,0},{24,8},{1,17},{9,25},{17,1},{25,9},{2,18},{10... | collective-permute-start | bytes 6152 | tf_op jit(solution)/shard_map/ppermute | solution.py:789
